TPU v7x, 32 devices: a whole 2x2x4 slice. The times are simulated.
32 devices in a mesh: dp: 8 (over y, x, core), tensor: 4 (over z).
Axes of the slice: x: 2, y: 2, z: 4, core: 2. Of those that a mesh axis runs over, the one named last changes fastest.
Arguments:
- tokens: bfloat16 [20736, 1280], P(('dp', 'tensor')), may hold values from -14 to 14
- counts: int32 [8, 4], P('dp'), may hold values from 1 to 648, 2056 in all within a row
- gains: float32 [2, 1280], P(None, ('dp', 'tensor')), may hold values from 0.1 to 1.9
- biases: float32 [6, 1280], P(None, ('dp', 'tensor')), may hold values from -3 to 3
- fc1_bias: float32 [5120], P(('dp', 'tensor')), may hold values from -3 to 3
- w_qkv: bfloat16 [1280, 3, 1280], P('dp', None, 'tensor'), may hold values from -0.1677051 to 0.1677051
- w_o: bfloat16 [1280, 1280], P('tensor', 'dp'), may hold values from -1.25 to 1.25
- w_1: bfloat16 [1280, 5120], P('dp', 'tensor'), may hold values from -0.15625 to 0.15625
- w_2: bfloat16 [5120, 1280], P('tensor', 'dp'), may hold values from -0.078125 to 0.078125
- cotangent: bfloat16 [20736, 1280], P(('dp', 'tensor')), may hold values from -6 to 6
Outputs:
- mixed: bfloat16 [20736, 1280], P(('dp', 'tensor'))
- d_tokens: bfloat16 [20736, 1280], P(('dp', 'tensor'))
- d_w_qkv: float32 [1280, 3, 1280], P('dp', None, 'tensor')
- d_w_o: float32 [1280, 1280], P('tensor', 'dp')
- d_w_1: float32 [1280, 5120], P('dp', 'tensor')
- d_w_2: float32 [5120, 1280], P('tensor', 'dp')
- d_gains: float32 [2, 1280], P(None, ('dp', 'tensor'))
- d_biases: float32 [6, 1280], P(None, ('dp', 'tensor'))
- d_fc1_bias: float32 [5120], P(('dp', 'tensor'))
Inputs may be any that keep to these rules, and one draw needn't show every extreme that they name: Each row of counts sums to 2056, and each row has a block with exactly 648 valid rows.
All inputs are finite; a program needn't handle non-finite values.
Results may differ from a plain program's by a relative error of at most 0.015.
The roundings to bfloat16 on the way count: a program that leaves them out, or rounds other values in their place, can miss the bound.
Values may be sent and summed in bfloat16 or wider, within the bound.
A program may use at most 192 MiB of HBM per device.

v0:
```python
import math

import jax
import jax.numpy as jnp
from jax import lax
from jax.sharding import PartitionSpec as P

D = 1280
HD = 80
FF = 5120
TOK_IMG = 257
IMG_DEV = 8


EPS = 1e-06


def norm_rows(values, gain, shift):
    mean = jnp.mean(values, axis=-1, keepdims=True)
    centred = values - mean
    spread = jnp.mean(centred * centred, axis=-1, keepdims=True)
    inverse = lax.rsqrt(spread + EPS)
    normed = centred * inverse
    return (normed * gain + shift, normed, inverse)


def norm_back(upstream, normed, inverse, gain):
    scaled = upstream * gain
    return inverse * (
        scaled
        - jnp.mean(scaled, axis=-1, keepdims=True)
        - normed * jnp.mean(scaled * normed, axis=-1, keepdims=True)
    )


def gelu_slope(pre):
    return 0.5 * (1.0 + lax.erf(pre * (1.0 / math.sqrt(2.0)))) + pre * jnp.exp(-0.5 * pre * pre) * (
        1.0 / math.sqrt(2.0 * math.pi)
    )


def block_layout(counts_row, block_rows, total):
    parts = counts_row.shape[0]
    ends = jnp.cumsum(counts_row)
    starts = ends - counts_row
    places = jnp.arange(total, dtype=jnp.int32)
    owners = jnp.sum((places[:, None] >= ends[None, :]).astype(jnp.int32), axis=1)
    picked = owners[:, None] == jnp.arange(parts, dtype=jnp.int32)[None, :]
    first = jnp.sum(jnp.where(picked, starts[None, :], 0), axis=1)
    return owners * block_rows + places - first


def padded_rows(counts_row, block_rows, total, row_count):
    parts = counts_row.shape[0]
    ends = jnp.cumsum(counts_row)
    starts = ends - counts_row
    rows = jnp.arange(row_count, dtype=jnp.int32)
    owners = rows // block_rows
    within = rows - owners * block_rows
    picked = owners[:, None] == jnp.arange(parts, dtype=jnp.int32)[None, :]
    limit = jnp.sum(jnp.where(picked, counts_row[None, :], 0), axis=1)
    first = jnp.sum(jnp.where(picked, starts[None, :], 0), axis=1)
    valid = within < limit
    places = jnp.clip(first + within, 0, total - 1)
    return (places, valid)


def attention_forward(query, keys, values):
    total, heads, size = query.shape
    shaped = (total // (2 * TOK_IMG), 2, TOK_IMG, heads, size)
    scale = size ** (-0.5)

    def one_pair(inputs):
        query_pair, keys_pair, values_pair = inputs
        scores = (
            jnp.einsum("itgd,isgd->igts", query_pair, keys_pair, preferred_element_type=jnp.float32)
            * scale
        )
        top = jnp.max(scores, axis=-1, keepdims=True)
        expo = jnp.exp(scores - top)
        summed = jnp.sum(expo, axis=-1, keepdims=True)
        probs = (expo / summed).astype(jnp.bfloat16)
        output = jnp.einsum(
            "igts,isgd->itgd", probs, values_pair, preferred_element_type=jnp.float32
        ).astype(jnp.bfloat16)
        return (output, (top + jnp.log(summed))[..., 0])

    output, lse = lax.map(
        one_pair, (query.reshape(shaped), keys.reshape(shaped), values.reshape(shaped))
    )
    return (output.reshape(total, heads * size), lse)


def attention_backward(query, keys, values, attended, grad_att, lse):
    total, heads, size = query.shape
    shaped = (total // (2 * TOK_IMG), 2, TOK_IMG, heads, size)
    scale = size ** (-0.5)

    def one_pair(inputs):
        query_pair, keys_pair, values_pair, output_pair, grad_pair, lse_pair = inputs
        scores = (
            jnp.einsum("itgd,isgd->igts", query_pair, keys_pair, preferred_element_type=jnp.float32)
            * scale
        )
        probs = jnp.exp(scores - lse_pair[..., None])
        probs_b = probs.astype(jnp.bfloat16)
        grad_v = jnp.einsum(
            "igts,itgd->isgd", probs_b, grad_pair, preferred_element_type=jnp.float32
        )
        grad_p = jnp.einsum(
            "itgd,isgd->igts", grad_pair, values_pair, preferred_element_type=jnp.float32
        )
        delta = jnp.einsum(
            "itgd,itgd->igt", grad_pair, output_pair, preferred_element_type=jnp.float32
        )
        grad_s = (probs * (grad_p - delta[..., None]) * scale).astype(jnp.bfloat16)
        grad_q = jnp.einsum(
            "igts,isgd->itgd", grad_s, keys_pair, preferred_element_type=jnp.float32
        )
        grad_k = jnp.einsum(
            "igts,itgd->isgd", grad_s, query_pair, preferred_element_type=jnp.float32
        )
        return (grad_q, grad_k, grad_v)

    grad_q, grad_k, grad_v = lax.map(
        one_pair,
        (
            query.reshape(shaped),
            keys.reshape(shaped),
            values.reshape(shaped),
            attended.reshape(shaped),
            grad_att.reshape(shaped),
            lse,
        ),
    )
    flat = (total, heads * size)
    return (grad_q.reshape(flat), grad_k.reshape(flat), grad_v.reshape(flat))


def body(tokens, counts, gains, biases, fc1_bias, w_qkv, w_o, w_1, w_2, cotangent):
    n_tensor = lax.axis_size("tensor")
    tensor_index = lax.axis_index("tensor")
    block_rows = tokens.shape[0]
    total = IMG_DEV * TOK_IMG
    width_dev = w_qkv.shape[2]
    heads_dev = width_dev // HD
    counts_row = counts[0]
    part_ids = jnp.arange(n_tensor, dtype=jnp.int32)
    own_count = jnp.sum(jnp.where(part_ids == tensor_index, counts_row, 0))
    own_valid = (jnp.arange(block_rows, dtype=jnp.int32) < own_count)[:, None]
    source = block_layout(counts_row, block_rows, total)

    def expand(compact, count):
        places, valid = padded_rows(counts_row, block_rows, total, count)
        picked = jnp.take(compact, places, axis=0)
        shaped_mask = valid.reshape((count,) + (1,) * (compact.ndim - 1))
        return jnp.where(shaped_mask, picked, jnp.zeros((), compact.dtype))

    gain_all, shift_all, fc1_all = (
        lax.all_gather(gains, ("dp", "tensor"), axis=1, tiled=True),
        lax.all_gather(biases, ("dp", "tensor"), axis=1, tiled=True),
        lax.all_gather(fc1_bias, ("dp", "tensor"), axis=0, tiled=True),
    )
    qkv_all, out_all = (
        lax.all_gather(w_qkv, "dp", axis=0, tiled=True),
        lax.all_gather(w_o, "dp", axis=1, tiled=True),
    )
    column = tensor_index * width_dev
    query_bias = lax.dynamic_slice_in_dim(shift_all[2], column, width_dev)
    value_bias = lax.dynamic_slice_in_dim(shift_all[3], column, width_dev)
    x = tokens.astype(jnp.float32)
    attn_norm, normed1, inverse1 = norm_rows(x, gain_all[0], shift_all[0])
    attn_rows = lax.all_gather(attn_norm.astype(jnp.bfloat16), "tensor", axis=0, tiled=True)
    attn_in = jnp.take(attn_rows, source, axis=0)
    qkv = jnp.einsum("td,dcf->tcf", attn_in, qkv_all, preferred_element_type=jnp.float32)
    query = (qkv[:, 0] + query_bias).astype(jnp.bfloat16).reshape(total, heads_dev, HD)
    keys = qkv[:, 1].astype(jnp.bfloat16).reshape(total, heads_dev, HD)
    values = (qkv[:, 2] + value_bias).astype(jnp.bfloat16).reshape(total, heads_dev, HD)
    attended, lse = attention_forward(query, keys, values)
    attn_block = lax.psum_scatter(
        jnp.dot(
            expand(attended, block_rows * lax.axis_size("tensor")),
            out_all,
            preferred_element_type=jnp.float32,
        ),
        "tensor",
        scatter_dimension=0,
        tiled=True,
    )
    hidden = x + attn_block + shift_all[4]
    mlp_norm, normed2, inverse2 = norm_rows(hidden, gain_all[1], shift_all[1])
    mlp_block = mlp_norm.astype(jnp.bfloat16)
    grad_y = jnp.where(own_valid, cotangent, jnp.zeros((), jnp.bfloat16))
    first_all, second_all = (
        lax.all_gather(w_1, "dp", axis=0, tiled=True),
        lax.all_gather(w_2, "dp", axis=1, tiled=True),
    )
    ff_dev = w_1.shape[1]
    mlp_rows = lax.all_gather(mlp_block, "tensor", axis=0, tiled=True)
    mlp_in = jnp.take(mlp_rows, source, axis=0)
    fc1_cols = lax.dynamic_slice_in_dim(fc1_all, tensor_index * ff_dev, ff_dev)
    pre = jnp.dot(mlp_in, first_all, preferred_element_type=jnp.float32) + fc1_cols
    act = jax.nn.gelu(pre, approximate=False).astype(jnp.bfloat16)
    mlp_out = lax.psum_scatter(
        jnp.dot(
            expand(act, block_rows * lax.axis_size("tensor")),
            second_all,
            preferred_element_type=jnp.float32,
        ).astype(jnp.bfloat16),
        "tensor",
        scatter_dimension=0,
        tiled=True,
    ).astype(jnp.float32)
    cot_rows = lax.all_gather(grad_y, "tensor", axis=0, tiled=True)
    cot_compact = jnp.take(cot_rows, source, axis=0)
    grad_pre = jnp.einsum(
        "td,fd->tf", cot_compact, second_all, preferred_element_type=jnp.float32
    ) * gelu_slope(pre)
    grad_pre_b = grad_pre.astype(jnp.bfloat16)
    grad_second = jnp.einsum("tf,td->fd", act, cot_compact, preferred_element_type=jnp.float32)
    grad_first = jnp.einsum("td,tf->df", mlp_in, grad_pre_b, preferred_element_type=jnp.float32)
    fc1_terms = lax.dynamic_update_slice(
        jnp.zeros((FF,), jnp.float32), jnp.sum(grad_pre, axis=0), (tensor_index * ff_dev,)
    )
    grad_mlp_in = lax.psum_scatter(
        jnp.einsum(
            "tf,df->td",
            expand(grad_pre_b, block_rows * lax.axis_size("tensor")),
            first_all,
            preferred_element_type=jnp.float32,
        ),
        "tensor",
        scatter_dimension=0,
        tiled=True,
    )
    mixed = jnp.where(own_valid, hidden + mlp_out + shift_all[5], 0.0).astype(jnp.bfloat16)
    grad_yf = grad_y.astype(jnp.float32)
    grad_hidden = grad_yf + norm_back(grad_mlp_in, normed2, inverse2, gain_all[1])
    hidden_rows = lax.all_gather(grad_hidden.astype(jnp.bfloat16), "tensor", axis=0, tiled=True)
    grad_hid_compact = jnp.take(hidden_rows, source, axis=0)
    grad_wo = jnp.einsum(
        "tf,td->fd", attended, grad_hid_compact, preferred_element_type=jnp.float32
    )
    grad_att = jnp.einsum(
        "td,fd->tf", grad_hid_compact, out_all, preferred_element_type=jnp.float32
    ).astype(jnp.bfloat16)
    grad_att = grad_att.reshape(total, heads_dev, HD)
    grad_q, grad_k, grad_v = attention_backward(
        query, keys, values, attended.reshape(total, heads_dev, HD), grad_att, lse
    )
    grad_qkv = jnp.stack([grad_q, grad_k, grad_v], axis=1).astype(jnp.bfloat16)
    grad_wqkv = jnp.einsum("td,tcf->dcf", attn_in, grad_qkv, preferred_element_type=jnp.float32)
    grad_attn_in = lax.psum_scatter(
        jnp.einsum(
            "tcf,dcf->td",
            expand(grad_qkv, block_rows * lax.axis_size("tensor")),
            qkv_all,
            preferred_element_type=jnp.float32,
        ).astype(jnp.bfloat16),
        "tensor",
        scatter_dimension=0,
        tiled=True,
    ).astype(jnp.float32)
    grad_x = grad_hidden + norm_back(grad_attn_in, normed1, inverse1, gain_all[0])
    d_tokens = jnp.where(own_valid, grad_x, 0.0).astype(jnp.bfloat16)
    grad_wqkv_own, grad_wo_own, grad_w1_own, grad_w2_own = (
        lax.psum_scatter(
            grad_wqkv.astype(jnp.bfloat16), "dp", scatter_dimension=0, tiled=True
        ).astype(jnp.float32),
        lax.psum_scatter(
            grad_wo.astype(jnp.bfloat16), "dp", scatter_dimension=1, tiled=True
        ).astype(jnp.float32),
        lax.psum_scatter(
            grad_first.astype(jnp.bfloat16), "dp", scatter_dimension=0, tiled=True
        ).astype(jnp.float32),
        lax.psum_scatter(
            grad_second.astype(jnp.bfloat16), "dp", scatter_dimension=1, tiled=True
        ).astype(jnp.float32),
    )
    query_terms = lax.dynamic_update_slice(
        jnp.zeros((D,), jnp.float32), jnp.sum(grad_q, axis=0), (column,)
    )
    value_terms = lax.dynamic_update_slice(
        jnp.zeros((D,), jnp.float32), jnp.sum(grad_v, axis=0), (column,)
    )
    gain_terms = jnp.stack(
        [jnp.sum(grad_attn_in * normed1, axis=0), jnp.sum(grad_mlp_in * normed2, axis=0)]
    )
    bias_terms = jnp.stack(
        [
            jnp.sum(grad_attn_in, axis=0),
            jnp.sum(grad_mlp_in, axis=0),
            query_terms,
            value_terms,
            jnp.sum(grad_hidden, axis=0),
            jnp.sum(grad_yf, axis=0),
        ]
    )
    d_gains, d_biases, d_fc1 = (
        lax.psum_scatter(gain_terms, ("dp", "tensor"), scatter_dimension=1, tiled=True),
        lax.psum_scatter(bias_terms, ("dp", "tensor"), scatter_dimension=1, tiled=True),
        lax.psum_scatter(fc1_terms, ("dp", "tensor"), scatter_dimension=0, tiled=True),
    )
    return (
        mixed,
        d_tokens,
        grad_wqkv_own,
        grad_wo_own,
        grad_w1_own,
        grad_w2_own,
        d_gains,
        d_biases,
        d_fc1,
    )


def solution(mesh):
    return jax.shard_map(
        body,
        mesh=mesh,
        in_specs=(
            P(("dp", "tensor"), None),
            P("dp", None),
            P(None, ("dp", "tensor")),
            P(None, ("dp", "tensor")),
            P(("dp", "tensor")),
            P("dp", None, "tensor"),
            P("tensor", "dp"),
            P("dp", "tensor"),
            P("tensor", "dp"),
            P(("dp", "tensor"), None),
        ),
        out_specs=(
            P(("dp", "tensor"), None),
            P(("dp", "tensor"), None),
            P("dp", None, "tensor"),
            P("tensor", "dp"),
            P("dp", "tensor"),
            P("tensor", "dp"),
            P(None, ("dp", "tensor")),
            P(None, ("dp", "tensor")),
            P(("dp", "tensor")),
        ),
        check_vma=False,
    )
```

profile of v0, /device:TPU:0, one launch (start us, length us, event | category | flops | bytes accessed | tf_op | source)
XLA Modules:
  0.0 1845.3 jit_solution(7397014202205605007)
XLA Ops:
  7.2 71.0 %all-gather.1 = f32[32,40,6]{1,2,0:T(8,128)S(1)} all-gather(f32[1,40,6]{1,2,0:T(8,128)} %bitcast.173), channel_id=1, replica_groups=mesh['dp'=8,'tensor'=4] {'dp','tensor'}, dimensions={0}, use_global_device_ids=true | all-gather | bytes 31680 | tf_op jit(solution)/shard_map/all_gather | solution.py:161
  81.4 63.6 %all-gather = f32[32,40,2]{1,2,0:T(2,128)S(1)} all-gather(f32[1,40,2]{1,2,0:T(2,128)S(1)} %bitcast.174), channel_id=1, replica_groups=mesh['dp'=8,'tensor'=4] {'dp','tensor'}, dimensions={0}, use_global_device_ids=true | all-gather | bytes 10560 | tf_op jit(solution)/shard_map/all_gather | solution.py:160
  149.6 10.9 all_gather.37
  160.6 106.3 %all-gather.10.cloned.1.call-done = bf16[2592,1280]{1,0:T(8,128)(2,1)} async-done(((bf16[648,1280]{1,0:T(8,128)(2,1)}), bf16[2592,1280]{1,0:T(8,128)(2,1)}) %all-gather.10.cloned.1.call-update) | async-done | bytes 6635536 | tf_op jit(solution)/shard_map/all_gather | solution.py:173
  266.8 16.8 gather_fusion.2
  283.6 14.9 all-gather.12.cloned.1.call-done
  298.5 10.2 fusion.70
  308.7 2.8 fusion.134
  311.6 7.3 squeeze.42
  318.9 7.3 squeeze.41
  326.3 3.4 convert_element_type.103
  329.6 3.3 copy.67
  337.8 23.7 %while.26 = (s32[]{:T(128)}, bf16[4,2,257,4,80]{2,4,3,1,0:T(8,128)(2,1)}, f32[4,2,4,257]{3,2,1,0:T(4,128)}, bf16[4,2,257,4,80]{2,4,3,1,0:T(8,128)(2,1)}, bf16[4,...) while((s32[]{:T(128)}, bf16[4,2,257,4,80]{2,4,3,1,0:T(8,128)(2,1)}, ...), condition=%wide.region_11.13_spmd, body=%wide.region_8.12_spmd.sunk | while | flops 174003392 | bytes 8379277 | solution.py:88
  340.9 2.7 fusion.171
  352.8 2.7 fusion.171
  358.7 2.7 fusion.171
  361.4 4.8 copy.68
  366.3 5.5 reshape.241
  371.8 3.0 copy.69
  374.8 8.6 gather_fusion
  383.4 9.0 fusion.99
  393.8 3.7 convert_reduce_fusion.2
  397.5 218.4 %reduce-scatter.11.cloned.1.call-done = f32[648,1280]{1,0:T(8,128)} async-done(((f32[2592,1280]{1,0:T(8,128)}), f32[648,1280]{1,0:T(8,128)}) %reduce-scatter.11.cloned.1.call-update) | async-done | bytes 3317776 | tf_op jit(solution)/shard_map/reduce_scatter | solution.py:180
  623.6 46.7 %all-reduce = f32[5120]{0:T(1024)S(1)} all-reduce(f32[5120]{0:T(1024)S(1)} %dynamic-update-slice), channel_id=1, replica_groups=mesh['dp'=8,'tensor'=4] {'dp','tensor'}, use_global_device_ids=true, to_apply=%add | all-reduce | flops 5120 | bytes 40960
  670.3 70.6 %all-gather.20.cloned.1.call-done = bf16[2592,1280]{1,0:T(8,128)(2,1)} async-done(((bf16[648,1280]{1,0:T(8,128)(2,1)}), bf16[2592,1280]{1,0:T(8,128)(2,1)}) %all-gather.20.cloned.1.call-update) | async-done | bytes 6635536 | tf_op jit(solution)/shard_map/all_gather | solution.py:214
  740.9 16.3 gather_fusion.5
  757.2 104.9 %all-gather.14.cloned.1.call-done = bf16[2592,1280]{1,0:T(8,128)(2,1)} async-done(((bf16[648,1280]{1,0:T(8,128)(2,1)}), bf16[2592,1280]{1,0:T(8,128)(2,1)}) %all-gather.14.cloned.1.call-update) | async-done | bytes 6635536 | tf_op jit(solution)/shard_map/all_gather | solution.py:199
  862.2 16.3 gather_fusion.3
  878.5 16.6 all-gather.16.cloned.1.call-done
  895.0 32.8 %fusion.50 = (bf16[2056,1280]{1,0:T(8,128)(2,1)}, f32[2056,1280]{1,0:T(8,128)}) fusion(f32[1280]{0:T(1024)S(1)} %dynamic_slice.40, bf16[1280,1280]{1,0:T(8,128)(2,1)} %all-gather.16.cloned.1.call-done, bf16[2056,1280]{1,0:T(8,128)(2,1)} %gather_fusion.3, pred[2056]{0:T(1024)(128)(4,1)S(1)} %get-tuple-element.224), kind=kOutput, calls=%fused_computation.72 | convolution fusion | flops 6913423360 | bytes 24337416 | tf_op jit(solution)/shard_map/dot_general | solution.py:202
  929.8 15.5 fusion.133
  945.3 18.5 %gather_fusion.6 = bf16[2592,1280]{1,0:T(8,128)(2,1)} fusion(bf16[2056,1280]{1,0:T(8,128)(2,1)} %get-tuple-element.229, s32[3072]{0:T(1024)S(1)} %pad_clamp_fusion), kind=kCustom, calls=%fused_computation.5.clone | custom fusion | bytes 13281408 | tf_op jit(solution)/shard_map/jit(_take)/gather | solution.py:155
  963.8 14.7 fusion.62
  978.5 18.6 %gather_fusion.4 = bf16[2592,1280]{1,0:T(8,128)(2,1)} fusion(bf16[2056,1280]{1,0:T(8,128)(2,1)} %get-tuple-element.244, s32[3072]{0:T(1024)S(1)} %pad_clamp_fusion), kind=kCustom, calls=%fused_computation.1.clone | custom fusion | bytes 13281408 | tf_op jit(solution)/shard_map/jit(_take)/gather | solution.py:155
  997.2 13.7 convolution_convert_fusion
  1010.9 191.0 %reduce-scatter.15.cloned.1.call-done = f32[648,1280]{1,0:T(8,128)} async-done(((f32[2592,1280]{1,0:T(8,128)}), f32[648,1280]{1,0:T(8,128)}) %reduce-scatter.15.cloned.1.call-update) | async-done | bytes 3317776 | tf_op jit(solution)/shard_map/reduce_scatter | solution.py:225
  1201.9 3.9 multiply_reduce_fusion.2
  1205.8 116.0 %reduce-scatter.13.cloned.1.call-done = bf16[648,1280]{1,0:T(8,128)(2,1)} async-done(((bf16[2592,1280]{1,0:T(8,128)(2,1)}), bf16[648,1280]{1,0:T(8,128)(2,1)}) %reduce-scatter.13.cloned.1.call-update) | async-done | bytes 1658896 | tf_op jit(solution)/shard_map/reduce_scatter | solution.py:204
  1321.8 5.3 fusion.130
  1330.3 13.4 convolution_convert_fusion.2
  1343.8 12.9 convolution_convert_fusion.1
  1356.8 95.1 %all-gather.22.cloned.1.call-done = bf16[2592,1280]{1,0:T(8,128)(2,1)} async-done(((bf16[648,1280]{1,0:T(8,128)(2,1)}), bf16[2592,1280]{1,0:T(8,128)(2,1)}) %all-gather.22.cloned.1.call-update) | async-done | bytes 6635536 | tf_op jit(solution)/shard_map/all_gather | solution.py:239
  1451.9 16.7 gather_fusion.7
  1468.6 5.9 convolution_convert_fusion.3
  1474.5 6.6 reshape_reshape.2
  1481.1 70.2 %while.27 = (s32[]{:T(128)}, f32[4,2,257,4,80]{2,4,3,1,0:T(8,128)}, bf16[4,2,257,4,80]{2,4,3,1,0:T(8,128)(2,1)}, f32[4,2,257,4,80]{2,4,3,1,0:T(8,128)}, bf16[4,2...) while((s32[]{:T(128)}, f32[4,2,257,4,80]{2,4,3,1,0:T(8,128)}, ...), condition=%wide.region_20.23_spmd, body=%wide.region_19.22_spmd.sunk | while | flops 428124992 | bytes 42527848 | solution.py:125
  1490.8 2.8 fusion.183
  1508.3 3.0 fusion.183
  1526.0 2.8 fusion.183
  1543.4 2.8 fusion.183
  1551.3 8.0 fusion.135
  1562.7 3.6 copy.74
  1568.5 3.6 copy.75
  1578.6 6.8 convolution_convert_fusion.4
  1585.5 13.0 fusion.75
  1598.6 12.1 copy.76
  1610.8 16.9 gather_fusion.1
  1627.6 15.0 select_select_fusion
  1642.6 10.8 bitcast_convert_fusion.1
  1660.5 7.8 reduce-scatter.19.cloned.1.call-done
  1670.3 116.9 %reduce-scatter.17.cloned.1.call-done = bf16[648,1280]{1,0:T(8,128)(2,1)} async-done(((bf16[2592,1280]{1,0:T(8,128)(2,1)}), bf16[648,1280]{1,0:T(8,128)(2,1)}) %reduce-scatter.17.cloned.1.call-update) | async-done | bytes 1658896 | tf_op jit(solution)/shard_map/reduce_scatter | solution.py:253
  1787.2 3.1 fusion.94
  1790.5 42.2 %all-reduce.4 = (f32[2,1280]{1,0:T(2,128)S(1)}, f32[6,1280]{1,0:T(8,128)S(1)}, f32[5120]{0:T(1024)S(1)}) all-reduce(f32[2,1280]{1,0:T(2,128)S(1)} %pad_maximum_fusion, f32[6,1280]{1,0:T(8,128)S(1)} %stack.47, f32[5120]{0:T(1024)S(1)} %dynamic_update_slice.31), channel_id=10, replica_groups=mesh['dp'=8,'tensor'=4] {'dp','tensor'}, use_global_device_ids=true, to_apply=%region_30.33.clone | all-reduce | flops 15360 | bytes 122880
  1834.6 3.9 fusion.90
  (305 shorter events, 124.3 us)
Async XLA Ops:
  7.2 73.6 %copy-start.2 = (bf16[648,1280]{1,0:T(8,128)(2,1)S(1)}, bf16[648,1280]{1,0:T(8,128)(2,1)}, u32[]{:S(2)}) copy-start(bf16[648,1280]{1,0:T(8,128)(2,1)} %param.18) | copy-start | bytes 4976644
  7.2 74.2 %copy-start.46 = (f32[2,40]{1,0:T(2,128)S(1)}, f32[2,40]{1,0:T(2,128)}, u32[]{:S(2)}) copy-start(f32[2,40]{1,0:T(2,128)} %param.20) | copy-start | bytes 964
  7.2 259.6 %all-gather.10.cloned.1.call-start = ((), (), s32[]{:S(2)}) async-start(), calls=%async_computation.8 | async-start | bytes 8294400 | tf_op jit(solution)/shard_map/all_gather | solution.py:173
  80.8 66.9 %copy-start.25 = (f32[648]{0:T(1024)}, f32[648]{0:T(1024)S(1)}, u32[]{:S(2)}) copy-start(f32[648]{0:T(1024)S(1)} %broadcast_multiply_fusion.5) | copy-start | bytes 7780
  80.8 67.7 %copy-start.48 = (s32[1,4]{1,0:T(1,128)S(1)}, s32[1,4]{1,0:T(1,128)}, u32[]{:S(2)}) copy-start(s32[1,4]{1,0:T(1,128)} %param.19) | copy-start | bytes 52
  81.4 68.2 %copy-start.22 = (bf16[320,160]{0,1:T(8,128)(2,1)S(1)}, bf16[320,160]{0,1:T(8,128)(2,1)}, u32[]{:S(2)}) copy-start(bf16[320,160]{0,1:T(8,128)(2,1)} %param.24) | copy-start | bytes 307204
  81.4 67.9 %copy-start.29 = (f32[648]{0:T(1024)}, f32[648]{0:T(1024)S(1)}, u32[]{:S(2)}) copy-start(f32[648]{0:T(1024)S(1)} %add_rsqrt_fusion.1) | copy-start | bytes 7780
  145.2 473.7 %copy-start.20 = (f32[1280]{0:T(1024)}, f32[1280]{0:T(1024)S(1)}, u32[]{:S(2)}) copy-start(f32[1280]{0:T(1024)S(1)} %get-tuple-element.181) | copy-start | bytes 15364
  147.7 150.8 %all-gather.12.cloned.1.call-start = ((), (), s32[]{:S(2)}) async-start(), calls=%async_computation.9 | async-start | bytes 3317760 | tf_op jit(solution)/shard_map/all_gather | solution.py:165
  148.4 467.4 %reduce-scatter.11.cloned.1.call-start = ((), (), s32[]{:S(2)}) async-start(), calls=%async_computation.10 | async-start | bytes 16588800 | tf_op jit(solution)/shard_map/reduce_scatter | solution.py:180
  149.5 712.6 %copy-start.16 = (s32[3072]{0:T(1024)}, s32[3072]{0:T(1024)S(1)}, u32[]{:S(2)}) copy-start(s32[3072]{0:T(1024)S(1)} %pad_clamp_fusion.2) | copy-start | bytes 36868
  149.6 225.2 %copy-start.23 = (s32[3072]{0:T(1024)}, s32[3072]{0:T(1024)S(1)}, u32[]{:S(2)}) copy-start(s32[3072]{0:T(1024)S(1)} %pad_clamp_fusion.1) | copy-start | bytes 36868
  160.5 222.9 %copy-start.33 = (pred[2592]{0:T(1024)(128)(4,1)}, pred[2592]{0:T(1024)(128)(4,1)S(1)}, u32[]{:S(2)}) copy-start(pred[2592]{0:T(1024)(128)(4,1)S(1)} %compare_and_fusion.1) | copy-start | bytes 7780
  160.5 222.9 %copy-start.35 = (pred[2592]{0:T(1024)(128)(4,1)}, pred[2592]{0:T(1024)(128)(4,1)S(1)}, u32[]{:S(2)}) copy-start(pred[2592]{0:T(1024)(128)(4,1)S(1)} %fusion.109) | copy-start | bytes 7780
  329.6 3.3 copy-start.5
  332.9 2.6 copy-start.6
  392.4 348.5 %all-gather.20.cloned.1.call-start = ((), (), s32[]{:S(2)}) async-start(), calls=%async_computation.15 | async-start | bytes 8294400 | tf_op jit(solution)/shard_map/all_gather | solution.py:214
  393.7 222.1 %copy-start.42 = (pred[648]{0:T(1024)(128)(4,1)}, pred[648]{0:T(1024)(128)(4,1)S(1)}, u32[]{:S(2)}) copy-start(pred[648]{0:T(1024)(128)(4,1)S(1)} %iota_compare_fusion.3) | copy-start | bytes 1948
  397.4 464.7 %all-gather.14.cloned.1.call-start = ((), (), s32[]{:S(2)}) async-start(), calls=%async_computation.11 | async-start | bytes 8294400 | tf_op jit(solution)/shard_map/all_gather | solution.py:199
  620.1 3.2 copy-start.47
  621.9 273.2 %all-gather.16.cloned.1.call-start = ((), (), s32[]{:S(2)}) async-start(), calls=%async_computation.12 | async-start | bytes 3686400 | tf_op jit(solution)/shard_map/all_gather | solution.py:195
  622.4 307.4 %all-gather.18.cloned.1.call-start = ((), (), s32[]{:S(2)}) async-start(), calls=%async_computation.13 | async-start | bytes 3686400 | tf_op jit(solution)/shard_map/all_gather | solution.py:196
  623.2 578.7 %reduce-scatter.15.cloned.1.call-start = ((), (), s32[]{:S(2)}) async-start(), calls=%async_computation.16 | async-start | bytes 16588800 | tf_op jit(solution)/shard_map/reduce_scatter | solution.py:225
  945.3 18.5 %copy-start.34 = (pred[2592]{0:T(1024)(128)(4,1)S(1)}, pred[2592]{0:T(1024)(128)(4,1)}, u32[]{:S(2)}) copy-start(pred[2592]{0:T(1024)(128)(4,1)} %copy-done.33) | copy-start | bytes 7780
  945.3 18.5 %copy-start.36 = (pred[2592]{0:T(1024)(128)(4,1)S(1)}, pred[2592]{0:T(1024)(128)(4,1)}, u32[]{:S(2)}) copy-start(pred[2592]{0:T(1024)(128)(4,1)} %copy-done.35) | copy-start | bytes 7780
  945.3 18.5 %copy-start.50 = (bf16[1280,1280]{1,0:T(8,128)(2,1)S(1)}, bf16[1280,1280]{1,0:T(8,128)(2,1)}, u32[]{:S(2)}) copy-start(bf16[1280,1280]{1,0:T(8,128)(2,1)} %all-gather.16.cloned.1.call-done) | copy-start | bytes 9830404
  978.5 343.3 %reduce-scatter.13.cloned.1.call-start = ((), (), s32[]{:S(2)}) async-start(), calls=%async_computation.14 | async-start | bytes 8294400 | tf_op jit(solution)/shard_map/reduce_scatter | solution.py:204
  978.5 18.7 %copy-start.49 = (bf16[1280,1280]{0,1:T(8,128)(2,1)S(1)}, bf16[1280,1280]{0,1:T(8,128)(2,1)}, u32[]{:S(2)}) copy-start(bf16[1280,1280]{0,1:T(8,128)(2,1)} %all-gather.18.cloned.1.call-done) | copy-start | bytes 9830404
  1010.8 191.1 %copy-start.1 = (f32[648,1280]{1,0:T(8,128)S(1)}, f32[648,1280]{1,0:T(8,128)}, u32[]{:S(2)}) copy-start(f32[648,1280]{1,0:T(8,128)} %copy-done) | copy-start | bytes 9953284
  1010.8 191.1 %copy-start.21 = (f32[1280]{0:T(1024)S(1)}, f32[1280]{0:T(1024)}, u32[]{:S(2)}) copy-start(f32[1280]{0:T(1024)} %copy-done.20) | copy-start | bytes 15364
  1010.8 191.1 %copy-start.28 = (f32[648]{0:T(1024)S(1)}, f32[648]{0:T(1024)}, u32[]{:S(2)}) copy-start(f32[648]{0:T(1024)} %copy-done.27) | copy-start | bytes 7780
  1010.8 191.1 %copy-start.32 = (f32[648]{0:T(1024)S(1)}, f32[648]{0:T(1024)}, u32[]{:S(2)}) copy-start(f32[648]{0:T(1024)} %copy-done.31) | copy-start | bytes 7780
  1010.9 310.9 %copy-start.37 = (f32[1280]{0:T(1024)S(1)}, f32[1280]{0:T(1024)}, u32[]{:S(2)}) copy-start(f32[1280]{0:T(1024)} %get-tuple-element.242) | copy-start | bytes 15364
  1010.9 310.9 %copy-start.43 = (pred[648]{0:T(1024)(128)(4,1)S(1)}, pred[648]{0:T(1024)(128)(4,1)}, u32[]{:S(2)}) copy-start(pred[648]{0:T(1024)(128)(4,1)} %copy-done.42) | copy-start | bytes 1948
  1010.9 441.0 %all-gather.22.cloned.1.call-start = ((), (), s32[]{:S(2)}) async-start(), calls=%async_computation.17 | async-start | bytes 8294400 | tf_op jit(solution)/shard_map/all_gather | solution.py:239
  1330.2 324.2 %reduce-scatter.23.cloned.1.call-start = ((), (), s32[]{:S(2)}) async-start(), calls=%async_computation.21 | async-start | bytes 3686400 | tf_op jit(solution)/shard_map/reduce_scatter | solution.py:273
  1343.7 312.7 %reduce-scatter.25.cloned.1.call-start = ((), (), s32[]{:S(2)}) async-start(), calls=%async_computation.22 | async-start | bytes 3686400 | tf_op jit(solution)/shard_map/reduce_scatter | solution.py:276
  1343.8 108.1 %copy-start.17 = (s32[3072]{0:T(1024)S(1)}, s32[3072]{0:T(1024)}, u32[]{:S(2)}) copy-start(s32[3072]{0:T(1024)} %copy-done.16) | copy-start | bytes 36868
  1356.7 111.9 %copy-start.13 = (bf16[320,1280]{0,1:T(8,128)(2,1)S(1)}, bf16[320,1280]{0,1:T(8,128)(2,1)}, u32[]{:S(2)}) copy-start(bf16[320,1280]{0,1:T(8,128)(2,1)} %all_gather.37) | copy-start | bytes 2457604
  1356.7 302.2 %reduce-scatter.21.cloned.1.call-start = ((), (), s32[]{:S(2)}) async-start(), calls=%async_computation.20 | async-start | bytes 1105920 | tf_op jit(solution)/shard_map/reduce_scatter | solution.py:270
  1488.3 5.3 copy-start.14
  1493.6 5.0 copy-start.8
  1505.7 5.5 copy-start.14
  1511.2 5.0 copy-start.8
  1523.4 5.3 copy-start.14
  1528.7 5.0 copy-start.8
  1540.9 5.3 copy-start.14
  1546.2 5.0 copy-start.8
  1574.4 1.9 copy-start.11
  1574.4 3.0 copy-start.12
  1576.3 2.4 copy-start.10
  1585.5 82.9 %reduce-scatter.19.cloned.1.call-start = ((), (), s32[]{:S(2)}) async-start(), calls=%async_computation.19 | async-start | bytes 3317760 | tf_op jit(solution)/shard_map/reduce_scatter | solution.py:267
  1598.6 12.2 copy-start.24
  1598.6 188.6 %reduce-scatter.17.cloned.1.call-start = ((), (), s32[]{:S(2)}) async-start(), calls=%async_computation.18 | async-start | bytes 8294400 | tf_op jit(solution)/shard_map/reduce_scatter | solution.py:253
  1627.6 15.0 copy-start.51
  1653.4 4.9 copy-start.41
  1653.4 5.0 copy-start.40
  1653.4 5.0 copy-start.39
  1653.4 133.8 %copy-start.3 = (bf16[648,1280]{1,0:T(8,128)(2,1)S(1)}, bf16[648,1280]{1,0:T(8,128)(2,1)}, u32[]{:S(2)}) copy-start(bf16[648,1280]{1,0:T(8,128)(2,1)} %param.18) | copy-start | bytes 4976644
  1653.4 133.8 %copy-start.19 = (f32[1280]{0:T(1024)S(1)}, f32[1280]{0:T(1024)}, u32[]{:S(2)}) copy-start(f32[1280]{0:T(1024)} %copy-done.18) | copy-start | bytes 15364
  1653.4 133.8 %copy-start.26 = (f32[648]{0:T(1024)S(1)}, f32[648]{0:T(1024)}, u32[]{:S(2)}) copy-start(f32[648]{0:T(1024)} %copy-done.25) | copy-start | bytes 7780
  1653.4 133.8 %copy-start.30 = (f32[648]{0:T(1024)S(1)}, f32[648]{0:T(1024)}, u32[]{:S(2)}) copy-start(f32[648]{0:T(1024)} %copy-done.29) | copy-start | bytes 7780
  1656.4 178.2 %copy-start.44 = (pred[648]{0:T(1024)(128)(4,1)S(1)}, pred[648]{0:T(1024)(128)(4,1)}, u32[]{:S(2)}) copy-start(pred[648]{0:T(1024)(128)(4,1)} %copy-done.42) | copy-start | bytes 1948
  1787.2 47.4 %copy-start.9 = (bf16[648,1280]{1,0:T(8,128)(2,1)S(1)}, bf16[648,1280]{1,0:T(8,128)(2,1)}, u32[]{:S(2)}) copy-start(bf16[648,1280]{1,0:T(8,128)(2,1)} %reduce-scatter.17.cloned.1.call-done) | copy-start | bytes 4976644
  (15 other events, 18.8 us)
Sparse Core Ops, SparseCore 0:
  147.8 119.0 all-gather.9
  268.7 29.7 all-gather.11
  392.5 223.3 reduce-scatter.10
  617.9 122.9 all-gather.19
  742.9 119.1 all-gather.13
  863.9 31.0 all-gather.15
  896.9 32.8 all-gather.17
  978.6 223.2 reduce-scatter.14
  1204.2 117.5 reduce-scatter.12
  1330.4 121.4 all-gather.21
  1455.3 45.0 reduce-scatter.22
  1503.7 46.8 reduce-scatter.24
  1585.6 33.8 reduce-scatter.20
  1623.2 45.1 reduce-scatter.18
  1670.7 116.5 reduce-scatter.16
where the time goes:
time: 1850 us
  waiting for transfers between devices  1060 us (57%)
  local copies, waits for them, and re-layouts  237 us (13%)
  blocking collectives  234 us (13%)
  matrix products  221 us (12%)
  other arithmetic  74.7 us (4%)
    reduce_scatter x1, waiting for transfers between devices, body(): lax.psum_scatter(jnp.dot(expand(attended, block_rows * lax.axis_size('ten...  218 us
    reduce_scatter x1, waiting for transfers between devices, body(): lax.psum_scatter(jnp.einsum('tf,df->td', expand(grad_pre_b, block_rows *...  191 us
    reduce_scatter x1, waiting for transfers between devices, body(): lax.psum_scatter(jnp.einsum('tcf,dcf->td', expand(grad_qkv, block_rows *...  117 us
    reduce_scatter x1, waiting for transfers between devices, body(): lax.psum_scatter(jnp.dot(expand(act, block_rows * lax.axis_size('tensor')...  116 us
    all_gather x1, waiting for transfers between devices, body(): lax.all_gather(attn_norm.astype(jnp.bfloat16), 'tensor', axis=0, tiled=True)  106 us
    all_gather x1, waiting for transfers between devices, body(): mlp_rows = lax.all_gather(mlp_block, 'tensor', axis=0, tiled=True)  105 us
    all_gather x1, waiting for transfers between devices, body(): lax.all_gather(grad_hidden.astype(jnp.bfloat16), 'tensor', axis=0, tiled=...  95.1 us
    unnamed x2, blocking collectives  88.8 us
  transfers between devices with their start and end apart: 15, of which 12 were waited for; matrix products, arithmetic and copies ran while one was open for 19% of the time, Pallas kernels for 0%

commit v1 on v0

v1 whole, which is shorter than its diff:
```python
import functools
import math

import jax
import jax.numpy as jnp
from jax import lax
from jax.experimental import pallas as pl
from jax.experimental.pallas import tpu as pltpu
from jax.sharding import PartitionSpec as P

D = 1280
HD = 80
HEADS = 16
FF = 5120
TOK_IMG = 257
IMG_DEV = 8
TOTAL = IMG_DEV * TOK_IMG
EPS = 1e-06
PT = 272
F32 = jnp.float32
BF16 = jnp.bfloat16
NEG = -1e30
VMEM_LIMIT = 56 * 1024 * 1024


class Cfg:
    def __init__(self, n_dp, n_t, block_rows):
        self.n_dp, self.n_t, self.block = n_dp, n_t, block_rows
        self.n_p = n_dp // 2
        self.imgs = IMG_DEV // n_t
        self.ni = 2 * self.imgs
        self.rows = self.imgs * TOK_IMG
        self.m = self.ni * PT
        self.pd = D // n_dp
        self.hh = HEADS // n_t // 2
        self.hc = self.hh * HD
        self.f2 = FF // n_t // 2
        assert 4 * self.hc == self.f2
        self.caps = self._caps()

    def _caps(self):
        n, b, r = self.n_t, self.block, self.rows
        low = [max(t, TOTAL - (n - t) * b) for t in range(n + 1)]
        high = [min(t * b, TOTAL - (n - t)) for t in range(n + 1)]
        caps = {}
        for t in range(n):
            for dest in range(n):
                size = min(high[t + 1], r * (dest + 1)) - max(low[t], r * dest)
                size = min(size, b, r)
                if size > 0 and dest != t:
                    caps[dest - t] = max(caps.get(dest - t, 0), size)
        return {s: min(-(-c // 16) * 16, b, r) for s, c in sorted(caps.items())}


def dot(a, b):
    return lax.dot_general(a, b, (((1,), (0,)), ((), ())), preferred_element_type=F32)


def dot_nt(a, b):
    return lax.dot_general(a, b, (((1,), (1,)), ((), ())), preferred_element_type=F32)


def dot_tn(a, b):
    return lax.dot_general(a, b, (((0,), (0,)), ((), ())), preferred_element_type=F32)


def norm(values):
    mean = jnp.mean(values, axis=-1, keepdims=True)
    centred = values - mean
    spread = jnp.mean(centred * centred, axis=-1, keepdims=True)
    inverse = lax.rsqrt(spread + EPS)
    return centred * inverse, inverse


def norm_back(upstream, normed, inverse, gain):
    scaled = upstream * gain
    return inverse * (
        scaled
        - jnp.mean(scaled, axis=-1, keepdims=True)
        - normed * jnp.mean(scaled * normed, axis=-1, keepdims=True)
    )


def swap_dp(value, bit, cfg):
    return lax.ppermute(value, "dp", [(i, i ^ bit) for i in range(cfg.n_dp)])


def turn_tensor(value, shift, cfg):
    return lax.ppermute(value, "tensor", [(i, (i + shift) % cfg.n_t) for i in range(cfg.n_t)])


def step_tensor(value, shift, cfg):
    pairs = [(i, i + shift) for i in range(cfg.n_t) if 0 <= i + shift < cfg.n_t]
    return lax.ppermute(value, "tensor", pairs)


def gather_pair(a, b, cfg):
    both = jnp.stack([a, b])
    if cfg.n_p == 4:
        from_x = swap_dp(both, 2, cfg)
        from_y = swap_dp(both, 4, cfg)
        diag_a = swap_dp(from_x[0], 4, cfg)
        diag_b = swap_dp(from_y[1], 2, cfg)
        arrays = [both, from_x, from_y, diag_a[None], diag_b[None]]
        where_a = [(0, 0), (1, 0), (2, 0), (3, 0)]
        where_b = [(0, 1), (1, 1), (2, 1), (4, 0)]
        return arrays, where_a, where_b
    arrays = [both] + [swap_dp(both, 2 * m, cfg) for m in range(1, cfg.n_p)]
    return arrays, [(m, 0) for m in range(cfg.n_p)], [(m, 1) for m in range(cfg.n_p)]


def slot_order(cfg):
    if cfg.n_p == 4:
        return [1, 3, 0, 2], [2, 3, 0, 1]
    order = list(range(1, cfg.n_p)) + [0]
    return order, order


def scatter_pair(send_a, keep_a, send_b, keep_b, cfg):
    if cfg.n_p == 4:
        got_a = swap_dp(send_a, 2, cfg)
        got_b = swap_dp(send_b, 4, cfg)
        next_a = (keep_a[1].astype(F32) + got_a[1].astype(F32)).astype(BF16)
        next_b = (keep_b[1].astype(F32) + got_b[1].astype(F32)).astype(BF16)
        last_a = swap_dp(next_a, 4, cfg)
        last_b = swap_dp(next_b, 2, cfg)
        sum_a = keep_a[0].astype(F32) + got_a[0].astype(F32) + last_a.astype(F32)
        sum_b = keep_b[0].astype(F32) + got_b[0].astype(F32) + last_b.astype(F32)
        return sum_a, sum_b
    sum_a, sum_b = keep_a[0].astype(F32), keep_b[0].astype(F32)
    for m in range(1, cfg.n_p):
        got = swap_dp(jnp.stack([send_a[m - 1], send_b[m - 1]]), 2 * m, cfg)
        sum_a = sum_a + got[0].astype(F32)
        sum_b = sum_b + got[1].astype(F32)
    return sum_a, sum_b


def gather_small(value, cfg, me, z):
    value = value[None]
    bit = 1
    while bit < cfg.n_t:
        other = lax.ppermute(value, "tensor", [(i, i ^ bit) for i in range(cfg.n_t)])
        first = (z & bit) == 0
        value = jnp.concatenate([jnp.where(first, value, other), jnp.where(first, other, value)])
        bit *= 2
    value = value[None]
    bit = 1
    while bit < cfg.n_dp:
        other = swap_dp(value, bit, cfg)
        first = (me & bit) == 0
        value = jnp.concatenate([jnp.where(first, value, other), jnp.where(first, other, value)])
        bit *= 2
    return value


def scatter_small(value, cfg, me, z):
    bit = cfg.n_dp // 2
    while bit >= 1:
        half = value.shape[0] // 2
        first = (me & bit) == 0
        keep = jnp.where(first, value[:half], value[half:])
        send = jnp.where(first, value[half:], value[:half])
        value = keep + swap_dp(send, bit, cfg)
        bit //= 2
    value = value[0]
    bit = cfg.n_t // 2
    while bit >= 1:
        half = value.shape[0] // 2
        first = (z & bit) == 0
        keep = jnp.where(first, value[:half], value[half:])
        send = jnp.where(first, value[half:], value[:half])
        value = keep + lax.ppermute(send, "tensor", [(i, i ^ bit) for i in range(cfg.n_t)])
        bit //= 2
    return value[0]


def pick(positions, limit):
    return (positions[:, None] == jnp.arange(limit, dtype=jnp.int32)[None, :]).astype(BF16)


def window_start(starts, t, dest, size, cfg):
    return jnp.clip(cfg.rows * dest - starts[t], 0, cfg.block - size)


def to_images(block, starts, ends, z, cfg):
    slot = jnp.arange(cfg.imgs * PT, dtype=jnp.int32)
    within = slot % PT
    place = cfg.rows * z + (slot // PT) * TOK_IMG + within
    valid = within < TOK_IMG
    owner = jnp.sum((place[:, None] >= ends[None, :]).astype(jnp.int32), axis=1)
    padded = jnp.where(valid & (owner == z), place - starts[z], -1)
    total = dot(pick(padded, cfg.block), block)
    for shift, size in cfg.caps.items():
        dest = jnp.clip(z + shift, 0, cfg.n_t - 1)
        sent = lax.dynamic_slice_in_dim(block, window_start(starts, z, dest, size, cfg), size)
        got = step_tensor(sent, shift, cfg)
        source = jnp.clip(z - shift, 0, cfg.n_t - 1)
        offset = place - starts[source] - window_start(starts, source, z, size, cfg)
        offset = jnp.where(valid & (owner == z - shift), offset, -1)
        total = total + dot(pick(offset, size), got)
    return total.astype(BF16)


def to_blocks(images, starts, ends, z, cfg):
    row = jnp.arange(cfg.block, dtype=jnp.int32)
    place = starts[z] + row
    valid = place < ends[z]
    owner = place // cfg.rows
    local = place - cfg.rows * z
    slots = (local // TOK_IMG) * PT + local % TOK_IMG
    total = dot(pick(jnp.where(valid & (owner == z), slots, -1), cfg.imgs * PT), images)
    for shift, size in cfg.caps.items():
        block_to = jnp.clip(z - shift, 0, cfg.n_t - 1)
        begin = jnp.clip(starts[block_to] - cfg.rows * z, 0, cfg.rows - size)
        want = begin + jnp.arange(size, dtype=jnp.int32)
        want = (want // TOK_IMG) * PT + want % TOK_IMG
        sent = dot(pick(want, cfg.imgs * PT), images).astype(BF16)
        got = step_tensor(sent, -shift, cfg)
        source = jnp.clip(z + shift, 0, cfg.n_t - 1)
        begin_there = jnp.clip(starts[z] - cfg.rows * source, 0, cfg.rows - size)
        offset = place - cfg.rows * source - begin_there
        offset = jnp.where(valid & (owner == z + shift), offset, -1)
        total = total + dot(pick(offset, size), got)
    return total.astype(BF16)


def weight_copies(scalars, refs, wheres, scratch, sem, cfg):
    plane, core = scalars[0], scalars[1]
    copies = []
    for m, (array, index) in enumerate(wheres):
        for r in range(2):
            owner = 2 * (plane ^ m) + (core ^ r)
            rows = pl.ds(pl.multiple_of(owner * cfg.pd, 16), cfg.pd)
            copies.append(
                pltpu.make_async_copy(refs[array].at[index, r], scratch.at[rows, :], sem)
            )
    return copies


def any_spec():
    return pl.BlockSpec(memory_space=pl.ANY)


def params(**more):
    return pltpu.CompilerParams(vmem_limit_bytes=VMEM_LIMIT, **more)


def image_spec(width):
    return pl.BlockSpec((1, PT, width), lambda i, s: (i, 0, 0))


def row_spec(count=1, width=D):
    return pl.BlockSpec((count, width), lambda i, s: (0, 0))


def attention_forward(scalars, x, gain, shift, query_bias, value_bias, weights, cfg):
    flat, plan = [], []
    for arrays, wheres in weights:
        ids = []
        for a in arrays:
            found = [i for i, f in enumerate(flat) if f is a]
            if not found:
                flat.append(a)
                found = [len(flat) - 1]
            ids.append(found[0])
        plan.append([(ids[a], i) for a, i in wheres])
    n_t, hc, hh = cfg.n_t, cfg.hc, cfg.hh

    def kernel(s, x_ref, gain_ref, shift_ref, qb_ref, vb_ref, *rest):
        w_refs = rest[: len(flat)]
        in_ref, qkv_ref, att_ref, lse_ref, out_ref, w, sem = rest[len(flat) :]

        @pl.when(pl.program_id(0) == 0)
        def _():
            copies = []
            for k in range(n_t):
                copies += weight_copies(s, w_refs, plan[k], w.at[k], sem, cfg)
            for copy in copies:
                copy.start()
            for copy in copies:
                copy.wait()

        normed, _ = norm(x_ref[0].astype(F32))
        attn_in = (normed * gain_ref[...] + shift_ref[...]).astype(BF16)
        in_ref[0] = attn_in
        keyed = lax.broadcasted_iota(jnp.int32, (PT, PT), 1) < TOK_IMG
        out = jnp.zeros((PT, D), F32)
        for k in range(n_t):
            block = 2 * lax.rem(s[2] - k + n_t, n_t) + s[1]
            qkv = dot(attn_in, w[k, :, : 3 * hc])
            query = (qkv[:, :hc] + qb_ref[pl.ds(block, 1), :]).astype(BF16)
            keys = qkv[:, hc : 2 * hc].astype(BF16)
            values = (qkv[:, 2 * hc :] + vb_ref[pl.ds(block, 1), :]).astype(BF16)
            qkv_ref[k, 0, :, :hc] = query
            qkv_ref[k, 0, :, hc : 2 * hc] = keys
            qkv_ref[k, 0, :, 2 * hc :] = values
            for h in range(hh):
                cols = slice(h * HD, (h + 1) * HD)
                scores = dot_nt(query[:, cols], keys[:, cols]) * (HD**-0.5)
                scores = jnp.where(keyed, scores, NEG)
                top = jnp.max(scores, axis=-1, keepdims=True)
                expo = jnp.exp(scores - top)
                summed = jnp.sum(expo, axis=-1, keepdims=True)
                probs = (expo / summed).astype(BF16)
                att_ref[k, 0, :, cols] = dot(probs, values[:, cols]).astype(BF16)
                j = k * hh + h
                lse_ref[0, :, j : j + 1] = top + jnp.log(summed)
            out = out + dot_nt(att_ref[k, 0], w[k, :, 3 * hc :])
        out_ref[0] = out

    return pl.pallas_call(
        kernel,
        grid_spec=pltpu.PrefetchScalarGridSpec(
            num_scalar_prefetch=1,
            grid=(cfg.ni,),
            in_specs=[
                image_spec(D),
                row_spec(),
                row_spec(),
                row_spec(2 * n_t, hc),
                row_spec(2 * n_t, hc),
            ]
            + [any_spec()] * len(flat),
            out_specs=[
                image_spec(D),
                pl.BlockSpec((n_t, 1, PT, 3 * hc), lambda i, s: (0, i, 0, 0)),
                pl.BlockSpec((n_t, 1, PT, hc), lambda i, s: (0, i, 0, 0)),
                image_spec(n_t * hh),
                image_spec(D),
            ],
            scratch_shapes=[
                pltpu.VMEM((n_t, D, cfg.f2), BF16),
                pltpu.SemaphoreType.DMA,
            ],
        ),
        out_shape=[
            jax.ShapeDtypeStruct((cfg.ni, PT, D), BF16),
            jax.ShapeDtypeStruct((n_t, cfg.ni, PT, 3 * hc), BF16),
            jax.ShapeDtypeStruct((n_t, cfg.ni, PT, hc), BF16),
            jax.ShapeDtypeStruct((cfg.ni, PT, n_t * hh), F32),
            jax.ShapeDtypeStruct((cfg.ni, PT, D), F32),
        ],
        compiler_params=params(),
        cost_estimate=pl.CostEstimate(
            flops=2 * cfg.m * D * cfg.f2 * n_t,
            bytes_accessed=2 * n_t * D * cfg.f2 + 12 * cfg.m * D,
            transcendentals=cfg.m * PT * n_t * hh,
        ),
        name="attention_forward",
    )(scalars, x, gain, shift, query_bias, value_bias, *flat)


def attention_backward(scalars, grad_hidden, qkv, attended, lse, weights, cfg):
    flat, plan = [], []
    for arrays, wheres in weights:
        ids = []
        for a in arrays:
            found = [i for i, f in enumerate(flat) if f is a]
            if not found:
                flat.append(a)
                found = [len(flat) - 1]
            ids.append(found[0])
        plan.append([(ids[a], i) for a, i in wheres])
    n_t, hc, hh = cfg.n_t, cfg.hc, cfg.hh
    scale = HD**-0.5

    def kernel(s, gh_ref, qkv_ref, att_ref, lse_ref, *rest):
        w_refs = rest[: len(flat)]
        gqkv_ref, out_ref, dq_ref, dv_ref, w, sem = rest[len(flat) :]

        @pl.when(pl.program_id(0) == 0)
        def _():
            copies = []
            for k in range(n_t):
                copies += weight_copies(s, w_refs, plan[k], w.at[k], sem, cfg)
            for copy in copies:
                copy.start()
            for copy in copies:
                copy.wait()
            dq_ref[...] = jnp.zeros_like(dq_ref)
            dv_ref[...] = jnp.zeros_like(dv_ref)

        keyed = lax.broadcasted_iota(jnp.int32, (PT, PT), 1) < TOK_IMG
        grad_hidden_b = gh_ref[0]
        out = jnp.zeros((PT, D), F32)
        for k in range(n_t):
            grad_att = dot(grad_hidden_b, w[k, :, 3 * hc :]).astype(BF16)
            for h in range(hh):
                cols = slice(h * HD, (h + 1) * HD)
                key_cols = slice(hc + h * HD, hc + (h + 1) * HD)
                value_cols = slice(2 * hc + h * HD, 2 * hc + (h + 1) * HD)
                query = qkv_ref[k, 0, :, cols]
                keys = qkv_ref[k, 0, :, key_cols]
                values = qkv_ref[k, 0, :, value_cols]
                grad = grad_att[:, cols]
                j = k * hh + h
                scores = dot_nt(query, keys) * scale - lse_ref[0, :, j : j + 1]
                probs = jnp.exp(jnp.where(keyed, scores, NEG))
                delta = jnp.sum(
                    grad.astype(F32) * att_ref[k, 0, :, cols].astype(F32), axis=-1, keepdims=True
                )
                grad_v = dot_tn(probs.astype(BF16), grad)
                grad_s = (probs * (dot_nt(grad, values) - delta) * scale).astype(BF16)
                grad_q = dot(grad_s, keys)
                grad_k = dot_tn(grad_s, query)
                dq_ref[k : k + 1, cols] += jnp.sum(grad_q, axis=0, keepdims=True)
                dv_ref[k : k + 1, cols] += jnp.sum(grad_v, axis=0, keepdims=True)
                gqkv_ref[k, 0, :, cols] = grad_q.astype(BF16)
                gqkv_ref[k, 0, :, key_cols] = grad_k.astype(BF16)
                gqkv_ref[k, 0, :, value_cols] = grad_v.astype(BF16)
            out = out + dot_nt(gqkv_ref[k, 0], w[k, :, : 3 * hc])
        out_ref[0] = out

    return pl.pallas_call(
        kernel,
        grid_spec=pltpu.PrefetchScalarGridSpec(
            num_scalar_prefetch=1,
            grid=(cfg.ni,),
            in_specs=[
                image_spec(D),
                pl.BlockSpec((n_t, 1, PT, 3 * hc), lambda i, s: (0, i, 0, 0)),
                pl.BlockSpec((n_t, 1, PT, hc), lambda i, s: (0, i, 0, 0)),
                image_spec(n_t * hh),
            ]
            + [any_spec()] * len(flat),
            out_specs=[
                pl.BlockSpec((n_t, 1, PT, 3 * hc), lambda i, s: (0, i, 0, 0)),
                image_spec(D),
                row_spec(n_t, hc),
                row_spec(n_t, hc),
            ],
            scratch_shapes=[
                pltpu.VMEM((n_t, D, cfg.f2), BF16),
                pltpu.SemaphoreType.DMA,
            ],
        ),
        out_shape=[
            jax.ShapeDtypeStruct((n_t, cfg.ni, PT, 3 * hc), BF16),
            jax.ShapeDtypeStruct((cfg.ni, PT, D), F32),
            jax.ShapeDtypeStruct((n_t, hc), F32),
            jax.ShapeDtypeStruct((n_t, hc), F32),
        ],
        compiler_params=params(),
        cost_estimate=pl.CostEstimate(
            flops=2 * cfg.m * D * cfg.f2 * n_t + 10 * cfg.m * PT * HD * n_t * hh,
            bytes_accessed=2 * n_t * D * cfg.f2 + 12 * cfg.m * D,
            transcendentals=cfg.m * PT * n_t * hh,
        ),
        name="attention_backward",
    )(scalars, grad_hidden, qkv, attended, lse, *flat)


def attention_weights(scalars, attn_in_t, grad_t, gqkv, attended, k, cfg):
    hc, pd = cfg.hc, cfg.pd
    order_a, order_b = slot_order(cfg)
    send = 2 if cfg.n_p == 4 else cfg.n_p - 1
    keep = cfg.n_p - send

    def kernel(s, in_ref, gt_ref, gqkv_ref, att_ref, sa_ref, ka_ref, sb_ref, kb_ref):
        step = pl.program_id(0)

        def one(order, chunk, send_ref, keep_ref):
            slot = functools.reduce(
                lambda acc, i: jnp.where(step == i, order[i], acc), range(cfg.n_p), 0
            )
            rows = pl.ds(pl.multiple_of((slot ^ s[0]) * 2 * pd, 16), 2 * pd)
            left = dot(in_ref[rows, :], gqkv_ref[chunk]).astype(BF16)
            right = dot(gt_ref[rows, :], att_ref[chunk]).astype(BF16)

            def put(ref):
                for r in range(2):
                    ref[0, s[1] ^ r, :, : 3 * hc] = left[r * pd : (r + 1) * pd]
                    ref[0, s[1] ^ r, :, 3 * hc :] = right[r * pd : (r + 1) * pd]

            @pl.when(step < send)
            def _():
                put(send_ref)

            @pl.when(step >= send)
            def _():
                put(keep_ref)

        one(order_a, 0, sa_ref, ka_ref)
        one(order_b, 1, sb_ref, kb_ref)

    send_spec = pl.BlockSpec(
        (1, 2, pd, cfg.f2), lambda i, s: (jnp.minimum(i, send - 1), 0, 0, 0)
    )
    keep_spec = pl.BlockSpec((1, 2, pd, cfg.f2), lambda i, s: (jnp.maximum(i - send, 0), 0, 0, 0))
    send_shape = jax.ShapeDtypeStruct((send, 2, pd, cfg.f2), BF16)
    keep_shape = jax.ShapeDtypeStruct((keep, 2, pd, cfg.f2), BF16)
    return pl.pallas_call(
        kernel,
        grid_spec=pltpu.PrefetchScalarGridSpec(
            num_scalar_prefetch=1,
            grid=(cfg.n_p,),
            in_specs=[
                row_spec(D, cfg.m),
                row_spec(D, cfg.m),
                pl.BlockSpec((2, cfg.m, 3 * hc), lambda i, s: (k // 2, 0, 0)),
                pl.BlockSpec((2, cfg.m, hc), lambda i, s: (k // 2, 0, 0)),
            ],
            out_specs=[send_spec, keep_spec, send_spec, keep_spec],
        ),
        out_shape=[send_shape, keep_shape, send_shape, keep_shape],
        compiler_params=params(),
        cost_estimate=pl.CostEstimate(
            flops=4 * cfg.m * D * cfg.f2,
            bytes_accessed=4 * cfg.m * D + 4 * D * cfg.f2,
            transcendentals=0,
        ),
        name="attention_weights",
    )(
        scalars,
        attn_in_t,
        grad_t,
        gqkv.reshape(cfg.n_t, cfg.m, 3 * hc),
        attended.reshape(cfg.n_t, cfg.m, hc),
    )


def mlp_chunk(scalars, mlp_in, cot, mlp_in_t, cot_t, fc1, weights, k, cfg):
    arrays, where_1, where_2 = weights
    n = len(arrays)
    pd, f2, ni = cfg.pd, cfg.f2, cfg.ni
    order_a, order_b = slot_order(cfg)
    send = 2 if cfg.n_p == 4 else cfg.n_p - 1
    keep = cfg.n_p - send

    def kernel(s, in_ref, cot_ref, in_t_ref, cot_t_ref, fc1_ref, *rest):
        w_refs = rest[:n]
        act_ref, gpre_ref, sum_ref, sa_ref, ka_ref, sb_ref, kb_ref, w1, w2, act_all, gpre_all, sem = (
            rest[n:]
        )
        step = pl.program_id(0)

        @pl.when(step == 0)
        def _():
            copies = weight_copies(s, w_refs, where_1, w1, sem, cfg)
            copies += weight_copies(s, w_refs, where_2, w2, sem, cfg)
            for copy in copies:
                copy.start()
            for copy in copies:
                copy.wait()
            sum_ref[...] = jnp.zeros_like(sum_ref)

        @pl.when(step < ni)
        def _():
            block = 2 * lax.rem(s[2] - k + cfg.n_t, cfg.n_t) + s[1]
            pre = dot(in_ref[0], w1[...]) + fc1_ref[pl.ds(block, 1), :]
            phi = 0.5 * (1.0 + lax.erf(pre * (1.0 / math.sqrt(2.0))))
            act = (pre * phi).astype(BF16)
            slope = phi + pre * jnp.exp(-0.5 * pre * pre) * (1.0 / math.sqrt(2.0 * math.pi))
            gpre = dot(cot_ref[0], w2[...]) * slope
            sum_ref[...] += jnp.sum(gpre, axis=0, keepdims=True)
            gpre = gpre.astype(BF16)
            act_ref[0] = act
            gpre_ref[0] = gpre
            rows = pl.ds(pl.multiple_of(step * PT, 16), PT)
            act_all[rows, :] = act
            gpre_all[rows, :] = gpre

        def one(lhs_ref, rhs, send_ref, keep_ref):
            value = dot(lhs_ref[...], rhs[...]).astype(BF16)

            def put(ref):
                for r in range(2):
                    ref[0, s[1] ^ r] = value[r * pd : (r + 1) * pd]

            @pl.when(step < ni + send)
            def _():
                put(send_ref)

            @pl.when(step >= ni + send)
            def _():
                put(keep_ref)

        @pl.when(step >= ni)
        def _():
            one(in_t_ref, gpre_all, sa_ref, ka_ref)
            one(cot_t_ref, act_all, sb_ref, kb_ref)

    def tile_spec(order):
        def place(i, s):
            slot = functools.reduce(
                lambda acc, j: jnp.where(i == ni + j, order[j], acc), range(1, cfg.n_p), order[0]
            )
            return slot ^ s[0], 0

        return pl.BlockSpec((2 * pd, cfg.m), place)

    rows_in = pl.BlockSpec((1, PT, D), lambda i, s: (jnp.minimum(i, ni - 1), 0, 0))
    rows_out = pl.BlockSpec((1, PT, f2), lambda i, s: (jnp.minimum(i, ni - 1), 0, 0))
    send_spec = pl.BlockSpec(
        (1, 2, pd, f2), lambda i, s: (jnp.clip(i - ni, 0, send - 1), 0, 0, 0)
    )
    keep_spec = pl.BlockSpec((1, 2, pd, f2), lambda i, s: (jnp.maximum(i - ni - send, 0), 0, 0, 0))
    send_shape = jax.ShapeDtypeStruct((send, 2, pd, f2), BF16)
    keep_shape = jax.ShapeDtypeStruct((keep, 2, pd, f2), BF16)
    return pl.pallas_call(
        kernel,
        grid_spec=pltpu.PrefetchScalarGridSpec(
            num_scalar_prefetch=1,
            grid=(ni + cfg.n_p,),
            in_specs=[
                rows_in,
                rows_in,
                tile_spec(order_a),
                tile_spec(order_b),
                row_spec(2 * cfg.n_t, f2),
            ]
            + [any_spec()] * n,
            out_specs=[
                rows_out,
                rows_out,
                row_spec(1, f2),
                send_spec,
                keep_spec,
                send_spec,
                keep_spec,
            ],
            scratch_shapes=[
                pltpu.VMEM((D, f2), BF16),
                pltpu.VMEM((D, f2), BF16),
                pltpu.VMEM((cfg.m, f2), BF16),
                pltpu.VMEM((cfg.m, f2), BF16),
                pltpu.SemaphoreType.DMA,
            ],
        ),
        out_shape=[
            jax.ShapeDtypeStruct((ni, PT, f2), BF16),
            jax.ShapeDtypeStruct((ni, PT, f2), BF16),
            jax.ShapeDtypeStruct((1, f2), F32),
            send_shape,
            keep_shape,
            send_shape,
            keep_shape,
        ],
        compiler_params=params(),
        cost_estimate=pl.CostEstimate(
            flops=8 * cfg.m * D * f2,
            bytes_accessed=8 * cfg.m * D + 8 * D * f2 + 4 * cfg.m * f2,
            transcendentals=2 * cfg.m * f2,
        ),
        name="mlp_chunk",
    )(scalars, mlp_in, cot, mlp_in_t, cot_t, fc1, *arrays)


def project_back(scalars, lefts, weights, part, cfg):
    flat, plan = [], []
    for arrays, wheres in weights:
        plan.append([(len(flat) + a, i) for a, i in wheres])
        flat += arrays
    n_t, f2, imgs = cfg.n_t, cfg.f2, cfg.imgs

    def kernel(s, *refs):
        left_refs = refs[:n_t]
        w_refs = refs[n_t : n_t + len(flat)]
        out_ref, w, sems = refs[n_t + len(flat) :]
        copies = [weight_copies(s, w_refs, plan[k], w.at[k], sems.at[k], cfg) for k in range(n_t)]

        @pl.when(pl.program_id(0) == 0)
        def _():
            for k in range(n_t):
                for copy in copies[k]:
                    copy.start()
            for k in range(n_t):
                for copy in copies[k]:
                    copy.wait()

        out = dot_nt(left_refs[0][0], w[0])
        for k in range(1, n_t):
            out = out + dot_nt(left_refs[k][0], w[k])
        out_ref[0] = out

    return pl.pallas_call(
        kernel,
        grid_spec=pltpu.PrefetchScalarGridSpec(
            num_scalar_prefetch=1,
            grid=(imgs,),
            in_specs=[pl.BlockSpec((1, PT, f2), lambda i, s: (part * imgs + i, 0, 0))] * n_t
            + [any_spec()] * len(flat),
            out_specs=image_spec(D),
            scratch_shapes=[
                pltpu.VMEM((n_t, D, f2), BF16),
                pltpu.SemaphoreType.DMA((n_t,)),
            ],
        ),
        out_shape=jax.ShapeDtypeStruct((imgs, PT, D), F32),
        compiler_params=params(),
        cost_estimate=pl.CostEstimate(
            flops=2 * imgs * PT * D * f2 * n_t,
            bytes_accessed=2 * n_t * D * f2 + 4 * imgs * PT * D,
            transcendentals=0,
        ),
        name="project_back",
    )(scalars, *lefts, *flat)


def plain_spec(width):
    return pl.BlockSpec((1, PT, width), lambda i: (i, 0, 0))


def plain_row(count=1):
    return pl.BlockSpec((count, D), lambda i: (0, 0))


def second_norm(x, part, other, shift_o, gain, shift, cfg):
    def kernel(x_ref, part_ref, other_ref, so_ref, gain_ref, shift_ref, hidden_ref, in_ref):
        hidden = x_ref[0].astype(F32) + (part_ref[0] + other_ref[0]) + so_ref[...]
        hidden_ref[0] = hidden
        normed, _ = norm(hidden)
        in_ref[0] = (normed * gain_ref[...] + shift_ref[...]).astype(BF16)

    return pl.pallas_call(
        kernel,
        grid=(cfg.imgs,),
        in_specs=[plain_spec(D)] * 3 + [plain_row()] * 3,
        out_specs=[plain_spec(D)] * 2,
        out_shape=[
            jax.ShapeDtypeStruct((cfg.imgs, PT, D), F32),
            jax.ShapeDtypeStruct((cfg.imgs, PT, D), BF16),
        ],
        compiler_params=params(),
        cost_estimate=pl.CostEstimate(
            flops=0, bytes_accessed=16 * cfg.imgs * PT * D, transcendentals=0
        ),
        name="second_norm",
    )(x, part, other, shift_o, gain, shift)


def second_norm_back(part, other, hidden, cot, gain, cfg):
    def kernel(part_ref, other_ref, hidden_ref, cot_ref, gain_ref, grad_ref, gradb_ref, sum_ref):
        @pl.when(pl.program_id(0) == 0)
        def _():
            sum_ref[...] = jnp.zeros_like(sum_ref)

        up = part_ref[0] + other_ref[0]
        normed, inverse = norm(hidden_ref[0])
        cot_f = cot_ref[0].astype(F32)
        grad = cot_f + norm_back(up, normed, inverse, gain_ref[...])
        grad_ref[0] = grad
        gradb_ref[0] = grad.astype(BF16)
        sum_ref[0:1, :] += jnp.sum(up * normed, axis=0, keepdims=True)
        sum_ref[1:2, :] += jnp.sum(up, axis=0, keepdims=True)
        sum_ref[2:3, :] += jnp.sum(grad, axis=0, keepdims=True)
        sum_ref[3:4, :] += jnp.sum(cot_f, axis=0, keepdims=True)

    return pl.pallas_call(
        kernel,
        grid=(cfg.imgs,),
        in_specs=[plain_spec(D)] * 4 + [plain_row()],
        out_specs=[plain_spec(D), plain_spec(D), plain_row(4)],
        out_shape=[
            jax.ShapeDtypeStruct((cfg.imgs, PT, D), F32),
            jax.ShapeDtypeStruct((cfg.imgs, PT, D), BF16),
            jax.ShapeDtypeStruct((4, D), F32),
        ],
        compiler_params=params(),
        cost_estimate=pl.CostEstimate(
            flops=0, bytes_accessed=20 * cfg.imgs * PT * D, transcendentals=0
        ),
        name="second_norm_back",
    )(part, other, hidden, cot, gain)


def first_norm_back(part, other, x, grad_hidden, gain, cfg):
    def kernel(part_ref, other_ref, x_ref, grad_ref, gain_ref, out_ref, sum_ref):
        @pl.when(pl.program_id(0) == 0)
        def _():
            sum_ref[...] = jnp.zeros_like(sum_ref)

        up = part_ref[0] + other_ref[0]
        normed, inverse = norm(x_ref[0].astype(F32))
        grad = grad_ref[0] + norm_back(up, normed, inverse, gain_ref[...])
        out_ref[0] = grad.astype(BF16)
        sum_ref[0:1, :] += jnp.sum(up * normed, axis=0, keepdims=True)
        sum_ref[1:2, :] += jnp.sum(up, axis=0, keepdims=True)

    return pl.pallas_call(
        kernel,
        grid=(cfg.imgs,),
        in_specs=[plain_spec(D)] * 4 + [plain_row()],
        out_specs=[plain_spec(D), plain_row(2)],
        out_shape=[
            jax.ShapeDtypeStruct((cfg.imgs, PT, D), BF16),
            jax.ShapeDtypeStruct((2, D), F32),
        ],
        compiler_params=params(),
        cost_estimate=pl.CostEstimate(
            flops=0, bytes_accessed=16 * cfg.imgs * PT * D, transcendentals=0
        ),
        name="first_norm_back",
    )(part, other, x, grad_hidden, gain)


def body(cfg, tokens, counts, gains, biases, fc1_bias, w_qkv, w_o, w_1, w_2, cotangent):
    n_t, n_dp, pd, f2, hc, imgs, ni = cfg.n_t, cfg.n_dp, cfg.pd, cfg.f2, cfg.hc, cfg.imgs, cfg.ni
    me = lax.axis_index("dp")
    z = lax.axis_index("tensor")
    core = me & 1
    scalars = jnp.stack([me >> 1, core, z]).astype(jnp.int32)
    ends = jnp.cumsum(counts[0]).astype(jnp.int32)
    starts = ends - counts[0]

    halves = jnp.stack(
        [
            jnp.concatenate(
                [
                    w_qkv.reshape(pd, 3, 2, hc).transpose(2, 0, 1, 3).reshape(2, pd, 3 * hc),
                    w_o.T.reshape(pd, 2, hc).transpose(1, 0, 2),
                ],
                axis=2,
            ),
            w_1.reshape(pd, 2, f2).transpose(1, 0, 2),
            w_2.T.reshape(pd, 2, f2).transpose(1, 0, 2),
        ],
        axis=1,
    )
    first_core = core == 0
    mine = jnp.where(first_core, halves[0], halves[1])
    theirs = swap_dp(jnp.where(first_core, halves[1], halves[0]), 1, cfg)
    unit_0 = jnp.stack([mine[0], theirs[0]])
    unit_1 = jnp.stack([mine[1], theirs[1]])
    unit_2 = jnp.stack([mine[2], theirs[2]])

    def turned(value, k):
        return value if k == 0 else turn_tensor(value, k, cfg)

    attn_blocks = [turned(unit_0, k) for k in range(n_t)]
    attn_weights = []
    for k in range(0, n_t, 2):
        arrays, where_a, where_b = gather_pair(attn_blocks[k], attn_blocks[k + 1], cfg)
        attn_weights += [(arrays, where_a), (arrays, where_b)]

    def paired(value):
        return jnp.concatenate([value, swap_dp(value, 1, cfg)])

    small = jnp.concatenate([gains, biases, fc1_bias.reshape(4, -1)])
    small = gather_small(small, cfg, me, z).reshape(n_dp * n_t, 12, -1)
    rows = small[:, :8].transpose(1, 0, 2).reshape(8, D)
    gain_all, shift_all = rows[:2], rows[2:]
    fc1_all = small[:, 8:].reshape(2 * n_t, f2)

    x_own = to_images(tokens, starts, ends, z, cfg).reshape(imgs, PT, D)
    x = paired(x_own)
    cot_own = to_images(cotangent, starts, ends, z, cfg).reshape(imgs, PT, D)
    cot = paired(cot_own)
    cot_t = cot.reshape(cfg.m, D).T

    attn_in, qkv, attended, lse, attn_out = attention_forward(
        scalars,
        x,
        gain_all[0:1],
        shift_all[0:1],
        shift_all[2].reshape(2 * n_t, hc),
        shift_all[3].reshape(2 * n_t, hc),
        attn_weights,
        cfg,
    )
    hidden, mlp_in_own = second_norm(
        x_own,
        attn_out[:imgs],
        swap_dp(attn_out[imgs:], 1, cfg),
        shift_all[4:5],
        gain_all[1:2],
        shift_all[1:2],
        cfg,
    )
    mlp_in = paired(mlp_in_own)
    mlp_in_t = mlp_in.reshape(cfg.m, D).T

    mlp_weights, acts, gpres, fc1_sums, mlp_grads = [], [], [], [], []
    for k in range(n_t):
        both = turned(jnp.stack([unit_1, unit_2]), k)
        weights = gather_pair(both[0], both[1], cfg)
        mlp_weights.append(weights)
        act, gpre, fc1_sum, send_1, keep_1, send_2, keep_2 = mlp_chunk(
            scalars, mlp_in, cot, mlp_in_t, cot_t, fc1_all, weights, k, cfg
        )
        acts.append(act)
        gpres.append(gpre)
        fc1_sums.append(fc1_sum)
        mlp_grads.append(scatter_pair(send_1, keep_1, send_2, keep_2, cfg))

    back = [(arrays, where_1) for arrays, where_1, _ in mlp_weights]
    out = [(arrays, where_2) for arrays, _, where_2 in mlp_weights]

    def summed(lefts, weights):
        pair_part = project_back(scalars, lefts, weights, 1, cfg)
        other = swap_dp(pair_part, 1, cfg)
        return project_back(scalars, lefts, weights, 0, cfg), other

    part, other = summed(gpres, back)
    grad_hidden, grad_hidden_b, sums_2 = second_norm_back(
        part, other, hidden, cot_own, gain_all[1:2], cfg
    )
    grad_hidden_b = paired(grad_hidden_b)
    gqkv, grad_in, dq, dv = attention_backward(
        scalars, grad_hidden_b, qkv, attended, lse, attn_weights, cfg
    )
    d_images, sums_1 = first_norm_back(
        grad_in[:imgs], swap_dp(grad_in[imgs:], 1, cfg), x_own, grad_hidden, gain_all[0:1], cfg
    )
    attn_in_t = attn_in.reshape(cfg.m, D).T
    grad_t = grad_hidden_b.reshape(cfg.m, D).T
    attn_grads = []
    for k in range(0, n_t, 2):
        pieces = attention_weights(scalars, attn_in_t, grad_t, gqkv, attended, k, cfg)
        attn_grads += list(scatter_pair(*pieces, cfg))

    part, other = summed(acts, out)
    mixed_own = (hidden + (part + other) + shift_all[5]).astype(BF16)
    mixed = to_blocks(mixed_own.reshape(imgs * PT, D), starts, ends, z, cfg)
    d_tokens = to_blocks(d_images.reshape(imgs * PT, D), starts, ends, z, cfg)

    total = jnp.stack([attn_grads[0], mlp_grads[0][0], mlp_grads[0][1]])
    for k in range(1, n_t):
        mlp_part = turn_tensor(jnp.stack(mlp_grads[k]).astype(BF16), -k, cfg)
        attn_part = turn_tensor(attn_grads[k].astype(BF16), -k, cfg)
        total = total + jnp.concatenate([attn_part[None], mlp_part]).astype(F32)
    mine = total[:, 0]
    theirs = swap_dp(total[:, 1], 1, cfg)
    half_0 = jnp.where(first_core, mine, theirs)
    half_1 = jnp.where(first_core, theirs, mine)
    d_qkv = jnp.stack(
        [half_0[0, :, : 3 * hc].reshape(pd, 3, hc), half_1[0, :, : 3 * hc].reshape(pd, 3, hc)],
        axis=2,
    ).reshape(pd, 3, 2 * hc)
    d_o = jnp.concatenate([half_0[0, :, 3 * hc :], half_1[0, :, 3 * hc :]], axis=1).T
    d_1 = jnp.concatenate([half_0[1], half_1[1]], axis=1)
    d_2 = jnp.concatenate([half_0[2], half_1[2]], axis=1).T

    order = (z - jnp.arange(n_t)) % n_t
    on_core = (jnp.arange(2) == core)[None, :, None]

    def placed(chunks):
        return jnp.where(on_core, jnp.take(chunks, order, axis=0)[:, None, :], 0.0)

    vectors = jnp.stack(
        [
            sums_1[0],
            sums_2[0],
            sums_1[1],
            sums_2[1],
            placed(dq).reshape(D),
            placed(dv).reshape(D),
            sums_2[2],
            sums_2[3],
        ]
    )
    vectors = vectors.reshape(8, n_dp, n_t, -1).transpose(1, 2, 0, 3)
    fc1_terms = placed(jnp.concatenate(fc1_sums)).reshape(n_dp, n_t, 4, -1)
    small = scatter_small(jnp.concatenate([vectors, fc1_terms], axis=2), cfg, me, z)
    return (
        mixed,
        d_tokens,
        d_qkv,
        d_o,
        d_1,
        d_2,
        small[:2],
        small[2:8],
        small[8:].reshape(-1),
    )


def solution(mesh):
    n_dp, n_t = mesh.shape["dp"], mesh.shape["tensor"]

    def program(tokens, *rest):
        cfg = Cfg(n_dp, n_t, tokens.shape[0])
        return body(cfg, tokens, *rest)

    both = ("dp", "tensor")
    return jax.shard_map(
        program,
        mesh=mesh,
        in_specs=(
            P(both, None),
            P("dp", None),
            P(None, both),
            P(None, both),
            P(both),
            P("dp", None, "tensor"),
            P("tensor", "dp"),
            P("dp", "tensor"),
            P("tensor", "dp"),
            P(both, None),
        ),
        out_specs=(
            P(both, None),
            P(both, None),
            P("dp", None, "tensor"),
            P("tensor", "dp"),
            P("dp", "tensor"),
            P("tensor", "dp"),
            P(None, both),
            P(None, both),
            P(both),
        ),
        check_vma=False,
    )
```

time: 1850 us -> 846 us (0.46)
  waiting for transfers between devices: 1060 us -> 284 us
  Pallas kernels: 0 us -> 244 us
  blocking collectives: 234 us -> 0 us
  matrix products: 221 us -> 39.7 us
  local copies, waits for them, and re-layouts: 237 us -> 85.3 us
  starting transfers between devices: 0.61 us -> 115 us
    reduce_scatter x8 -> x0, waiting for transfers between devices: 650 us -> none  [the longest x1 218 us: body(): lax.psum_scatter(jnp.dot(expand(attended, block_rows * lax.axis_size('ten...]
    all_gather x7 -> x0, waiting for transfers between devices: 410 us -> none  [the longest x1 106 us: body(): lax.all_gather(attn_norm.astype(jnp.bfloat16), 'tensor', axis=0, tiled=True)]
    ppermute x0 -> x88, waiting for transfers between devices: none -> 284 us  [the longest x64 152 us: swap_dp(): return lax.ppermute(value, 'dp', [(i, i ^ bit) for i in range(cfg.n_dp)])]
    pallas_call x0 -> x15, Pallas kernels: none -> 244 us  [the longest x4 79.1 us: mlp_chunk(): pl.pallas_call(kernel, grid_spec=pltpu.PrefetchScalarGridSpec(num_scalar_...]
    dot_general x40 -> x16, matrix products: 221 us -> 39.7 us  [dot(): lax.dot_general(a, b, (((1,), (0,)), ((), ())), preferred_element_type=F32)]
    all_gather x3 -> x0, blocking collectives: 146 us -> none  [the longest x1 71 us: body(): lax.all_gather(biases, ('dp', 'tensor'), axis=1, tiled=True)]
    gather x8 -> x3, local copies, waits for them, and re-layouts: 129 us -> 2.06 us  [placed(): return jnp.where(on_core, jnp.take(chunks, order, axis=0)[:, None, :], 0.0)]
    ppermute x0 -> x88, starting transfers between devices: none -> 115 us  [the longest x64 51 us: swap_dp(): return lax.ppermute(value, 'dp', [(i, i ^ bit) for i in range(cfg.n_dp)])]
  transfers between devices with their start and end apart: 15 -> 88, of which waited for: 12 -> 29; matrix products, arithmetic and copies ran while one was open for 19% -> 21% of each run, Pallas kernels for 0% -> 29%
where the time goes in v1:
time: 846 us; the launch traced here: 836 us
  waiting for transfers between devices  284 us (34%)
  Pallas kernels  244 us (29%)
  starting transfers between devices  115 us (14%)
  local copies, waits for them, and re-layouts  85.3 us (10%)
  other arithmetic  59.5 us (7%)
  matrix products  39.7 us (5%)
    ppermute x64, waiting for transfers between devices, swap_dp(): return lax.ppermute(value, 'dp', [(i, i ^ bit) for i in range(cfg.n_dp)])  152 us
    ppermute x12, waiting for transfers between devices, turn_tensor(): lax.ppermute(value, 'tensor', [(i, (i + shift) % cfg.n_t) for i in range(...  109 us
    pallas_call x4, Pallas kernels, mlp_chunk(): pl.pallas_call(kernel, grid_spec=pltpu.PrefetchScalarGridSpec(num_scalar_...  79.1 us
    ppermute x64, starting transfers between devices, swap_dp(): return lax.ppermute(value, 'dp', [(i, i ^ bit) for i in range(cfg.n_dp)])  51 us
    pallas_call x4, Pallas kernels, project_back(): pl.pallas_call(kernel, grid_spec=pltpu.PrefetchScalarGridSpec(num_scalar_...  43.2 us
    pallas_call x1, Pallas kernels, attention_backward(): pl.pallas_call(kernel, grid_spec=pltpu.PrefetchScalarGridSpec(num_scalar_...  40.2 us
    dot_general x16, matrix products, dot(): lax.dot_general(a, b, (((1,), (0,)), ((), ())), preferred_element_type=F32)  39.7 us
    pallas_call x1, Pallas kernels, attention_forward(): pl.pallas_call(kernel, grid_spec=pltpu.PrefetchScalarGridSpec(num_scalar_...  34.7 us
  transfers between devices with their start and end apart: 88, of which 29 were waited for; matrix products, arithmetic and copies ran while one was open for 21% of the time, Pallas kernels for 29%

profile of v1, /device:TPU:0, one launch (start us, length us, event | category | flops | bytes accessed | tf_op | source)
XLA Modules:
  0.0 835.8 jit_solution(1831693377212336075)
XLA Ops:
  2.1 3.0 collective-permute-start.3
  14.1 2.9 collective-permute-start.1
  34.0 4.3 collective-permute-start.4
  38.9 8.1 collective-permute-done.4
  53.2 2.5 collective-permute-start.15
  57.3 18.0 %collective-permute-done.14 = bf16[2,160,640]{2,1,0:T(8,128)(2,1)} collective-permute-done((bf16[2,160,640]{2,1,0:T(8,128)(2,1)}, bf16[2,160,640]{2,1,0:T(8,128)(2,1)}, u32[]{:S(2)}, u32[]{:S(2)}) %collective-permute-start.14) | collective-permute-done | bytes 409632 | tf_op jit(solution)/shard_map/ppermute | solution.py:89
  78.6 4.3 collective-permute-done.9
  92.1 7.2 collective-permute-done.17.rest_7_
  99.9 4.2 collective-permute-done.16.rest_6_
  106.5 10.4 %collective-permute-done.11.rest_2_ = bf16[2,2,160,640]{3,2,1,0:T(8,128)(2,1)S(1)} collective-permute-done((bf16[2,2,160,640]{3,2,1,0:T(8,128)(2,1)S(1)}, bf16[2,2,160,640]{3,2,1,0:T(8,128)(2,1)S(1)}, u32[]{:S(2)}, u32[]{:S(2)}) %collective-permute-start.11) | collective-permute-done | bytes 819232 | tf_op jit(solution)/shard_map/ppermute | solution.py:85
  118.2 3.4 collective-permute-done.10.rest_1_
  127.3 14.8 %collective-permute-start.23 = (bf16[416,1280]{1,0:T(8,128)(2,1)}, bf16[416,1280]{1,0:T(8,128)(2,1)}, u32[]{:S(2)}, u32[]{:S(2)}) collective-permute-start(bf16[416,1280]{1,0:T(8,128)(2,1)} %get-tuple-element.124), channel_id=1, source_target_pairs={{0,1},{1,2},{2,3},{4,5},{5,6},{6,7},{8,9},{9,10},{10,11},{12,13},{... | collective-permute-start | bytes 3194888 | tf_op jit(solution)/shard_map/ppermute | solution.py:94
  145.5 34.7 %attention_forward.1 = (bf16[4,272,1280]{2,1,0:T(8,128)(2,1)}, bf16[4,4,272,480]{3,2,1,0:T(8,128)(2,1)}, bf16[4,4,272,160]{3,2,1,0:T(8,128)(2,1)}, f32[4,272,8]{2,1,0:T(8,128)}, f32[4,272,1280]{2,1,0:T(8,128)}) custom-call(s32[3]{0:T(128)} %pad_add_fusion.s, bf16[4,272,1280]{2,1,0:T(8,128)(2,1)} %pad_maximum_fusion.x_ref, f32[1,1280]{1,0:T(1,128)} %slice.405.gain_ref, ...), custom_call_target="tpu_custom_call" | custom-call | flops 7130316800 | bytes 23265280 | tf_op jit(solution)/shard_map/attention_forward/pallas_call | solution.py:311
  180.3 5.8 fusion.102
  194.5 5.9 collective-permute-start.34
  200.4 3.0 fusion.7
  211.6 2.8 convolution_add_fusion.4
  214.4 50.0 %collective-permute-done.34.rest_0_.refs_14_ = bf16[2,2,160,640]{3,2,1,0:T(8,128)(2,1)} collective-permute-done((bf16[2,2,160,640]{3,2,1,0:T(8,128)(2,1)S(1)}, bf16[2,2,160,640]{3,2,1,0:T(8,128)(2,1)}, u32[]{:S(2)}, u32[]{:S(2)}) %collective-permute-start.34) | collective-permute-done | bytes 819232 | tf_op jit(solution)/shard_map/ppermute | solution.py:89
  265.4 3.3 fusion.4
  273.4 12.4 %collective-permute-done.41.rest_2_.refs_21_ = bf16[2,2,160,640]{3,2,1,0:T(8,128)(2,1)S(1)} collective-permute-done((bf16[2,2,160,640]{3,2,1,0:T(8,128)(2,1)}, bf16[2,2,160,640]{3,2,1,0:T(8,128)(2,1)S(1)}, u32[]{:S(2)}, u32[]{:S(2)}) %collective-permute-start.41) | collective-permute-done | bytes 819232 | tf_op jit(solution)/shard_map/ppermute | solution.py:85
  290.0 4.8 second_norm.1
  294.8 8.5 %collective-permute-done.36.rest_2_.refs_16_ = bf16[2,2,160,640]{3,2,1,0:T(8,128)(2,1)S(1)} collective-permute-done((bf16[2,2,160,640]{3,2,1,0:T(8,128)(2,1)}, bf16[2,2,160,640]{3,2,1,0:T(8,128)(2,1)S(1)}, u32[]{:S(2)}, u32[]{:S(2)}) %collective-permute-start.36) | collective-permute-done | bytes 819232 | tf_op jit(solution)/shard_map/ppermute | solution.py:85
  305.5 14.1 %collective-permute-done.31.rest_2_.refs_11_ = bf16[2,2,160,640]{3,2,1,0:T(8,128)(2,1)S(1)} collective-permute-done((bf16[2,2,160,640]{3,2,1,0:T(8,128)(2,1)}, bf16[2,2,160,640]{3,2,1,0:T(8,128)(2,1)S(1)}, u32[]{:S(2)}, u32[]{:S(2)}) %collective-permute-start.31) | collective-permute-done | bytes 819232 | tf_op jit(solution)/shard_map/ppermute | solution.py:85
  326.3 3.6 copy.76
  329.9 5.5 copy.77
  338.1 2.5 constant_dynamic-update-slice_fusion.in_ref
  340.6 5.4 copy.75
  347.1 19.8 %mlp_chunk.7 = (bf16[4,272,640]{2,1,0:T(8,128)(2,1)}, bf16[4,272,640]{2,1,0:T(8,128)(2,1)}, f32[1,640]{1,0:T(1,128)}, bf16[2,2,160,640]{3,2,1,0:T(8,128)(2,1)}, ...) custom-call(s32[3]{0:T(128)} %pad_add_fusion.s, ...), custom_call_target="tpu_custom_call" | custom-call | flops 7130316800 | bytes 20480000 | tf_op jit(solution)/shard_map/mlp_chunk/pallas_call | solution.py:600
  370.0 19.6 %mlp_chunk.6 = (bf16[4,272,640]{2,1,0:T(8,128)(2,1)}, bf16[4,272,640]{2,1,0:T(8,128)(2,1)}, f32[1,640]{1,0:T(1,128)}, bf16[2,2,160,640]{3,2,1,0:T(8,128)(2,1)}, ...) custom-call(s32[3]{0:T(128)} %pad_add_fusion.s, ...), custom_call_target="tpu_custom_call" | custom-call | flops 7130316800 | bytes 20480000 | tf_op jit(solution)/shard_map/mlp_chunk/pallas_call | solution.py:600
  391.0 19.6 %mlp_chunk.5 = (bf16[4,272,640]{2,1,0:T(8,128)(2,1)}, bf16[4,272,640]{2,1,0:T(8,128)(2,1)}, f32[1,640]{1,0:T(1,128)}, bf16[2,2,160,640]{3,2,1,0:T(8,128)(2,1)}, ...) custom-call(s32[3]{0:T(128)} %pad_add_fusion.s, ...), custom_call_target="tpu_custom_call" | custom-call | flops 7130316800 | bytes 20480000 | tf_op jit(solution)/shard_map/mlp_chunk/pallas_call | solution.py:600
  413.5 20.0 %mlp_chunk.4 = (bf16[4,272,640]{2,1,0:T(8,128)(2,1)}, bf16[4,272,640]{2,1,0:T(8,128)(2,1)}, f32[1,640]{1,0:T(1,128)}, bf16[2,2,160,640]{3,2,1,0:T(8,128)(2,1)}, ...) custom-call(s32[3]{0:T(128)} %pad_add_fusion.s, ...), custom_call_target="tpu_custom_call" | custom-call | flops 7130316800 | bytes 20480000 | tf_op jit(solution)/shard_map/mlp_chunk/pallas_call | solution.py:600
  433.6 10.7 %project_back.5 = f32[2,272,1280]{2,1,0:T(8,128)} custom-call(s32[3]{0:T(128)} %pad_add_fusion.s, bf16[4,272,640]{2,1,0:T(8,128)(2,1)} %get-tuple-element.65.refs_0_, bf16[4,272,640]{2,1,0:T(8,128)(2,1)} %get-tuple-element.66.refs_1_, bf16[4,272,640]{2,1,0:T(8,128)(2,1)} %get-tuple-element.67.refs_2_, bf16[4,272,640]{2,1,0:T(8,128)(2,1)} %get-tuple-element.68.refs_3_, ...), custom_call_target="tpu_custom_call" | custom-call | flops 3565158400 | bytes 9338880 | tf_op jit(solution)/shard_map/project_back/pallas_call | solution.py:676
  444.3 10.7 %project_back.4 = f32[2,272,1280]{2,1,0:T(8,128)} custom-call(s32[3]{0:T(128)} %pad_add_fusion.s, bf16[4,272,640]{2,1,0:T(8,128)(2,1)} %get-tuple-element.65.refs_0_, bf16[4,272,640]{2,1,0:T(8,128)(2,1)} %get-tuple-element.66.refs_1_, bf16[4,272,640]{2,1,0:T(8,128)(2,1)} %get-tuple-element.67.refs_2_, bf16[4,272,640]{2,1,0:T(8,128)(2,1)} %get-tuple-element.68.refs_3_, ...), custom_call_target="tpu_custom_call" | custom-call | flops 3565158400 | bytes 9338880 | tf_op jit(solution)/shard_map/project_back/pallas_call | solution.py:676
  455.1 10.7 %project_back.7 = f32[2,272,1280]{2,1,0:T(8,128)} custom-call(s32[3]{0:T(128)} %pad_add_fusion.s, bf16[4,272,640]{2,1,0:T(8,128)(2,1)} %get-tuple-element.69.refs_0_, bf16[4,272,640]{2,1,0:T(8,128)(2,1)} %get-tuple-element.70.refs_1_, bf16[4,272,640]{2,1,0:T(8,128)(2,1)} %get-tuple-element.71.refs_2_, bf16[4,272,640]{2,1,0:T(8,128)(2,1)} %get-tuple-element.72.refs_3_, ...), custom_call_target="tpu_custom_call" | custom-call | flops 3565158400 | bytes 9338880 | tf_op jit(solution)/shard_map/project_back/pallas_call | solution.py:676
  465.8 11.1 %project_back.6.part_ref = f32[2,272,1280]{2,1,0:T(8,128)} custom-call(s32[3]{0:T(128)} %pad_add_fusion.s, bf16[4,272,640]{2,1,0:T(8,128)(2,1)} %get-tuple-element.69.refs_0_, bf16[4,272,640]{2,1,0:T(8,128)(2,1)} %get-tuple-element.70.refs_1_, bf16[4,272,640]{2,1,0:T(8,128)(2,1)} %get-tuple-element.71.refs_2_, ...), custom_call_target="tpu_custom_call" | custom-call | flops 3565158400 | bytes 9338880 | tf_op jit(solution)/shard_map/project_back/pallas_call | solution.py:676
  487.8 11.7 %collective-permute-done.63 = bf16[2,2,160,640]{3,2,1,0:T(8,128)(2,1)S(1)} collective-permute-done((bf16[2,2,160,640]{3,2,1,0:T(8,128)(2,1)}, bf16[2,2,160,640]{3,2,1,0:T(8,128)(2,1)S(1)}, u32[]{:S(2)}, u32[]{:S(2)}) %collective-permute-start.63) | collective-permute-done | bytes 819232 | tf_op jit(solution)/shard_map/ppermute | solution.py:85
  501.1 16.0 %collective-permute-done.56 = bf16[2,2,160,640]{3,2,1,0:T(8,128)(2,1)S(1)} collective-permute-done((bf16[2,2,160,640]{3,2,1,0:T(8,128)(2,1)}, bf16[2,2,160,640]{3,2,1,0:T(8,128)(2,1)S(1)}, u32[]{:S(2)}, u32[]{:S(2)}) %collective-permute-start.56) | collective-permute-done | bytes 819232 | tf_op jit(solution)/shard_map/ppermute | solution.py:85
  517.7 8.1 collective-permute-done.78
  529.5 5.1 collective-permute-done.70
  538.3 3.4 collective-permute-done.62
  547.2 2.5 collective-permute-done.57
  558.4 6.4 second_norm_back.1
  571.9 4.0 convolution_add_fusion.1
  577.4 3.9 copy.78
  581.3 40.2 %attention_backward.1 = (bf16[4,4,272,480]{3,2,1,0:T(8,128)(2,1)}, f32[4,272,1280]{2,1,0:T(8,128)}, f32[4,160]{1,0:T(4,128)}, f32[4,160]{1,0:T(4,128)}) custom-call(s32[3]{0:T(128)} %pad_add_fusion.s, bf16[4,272,1280]{2,1,0:T(8,128)(2,1)} %copy-done.18, bf16[4,4,272,480]{3,2,1,0:T(8,128)(2,1)} %get-tuple-element.74.qkv_ref, ...), custom_call_target="tpu_custom_call" | custom-call | flops 9024307200 | bytes 23265280 | tf_op jit(solution)/shard_map/attention_backward/pallas_call | solution.py:414
  621.5 5.6 fusion.101
  627.6 14.7 %attention_weights.3 = (bf16[2,2,160,640]{3,2,1,0:T(8,128)(2,1)}, bf16[2,2,160,640]{3,2,1,0:T(8,128)(2,1)}, bf16[2,2,160,640]{3,2,1,0:T(8,128)(2,1)}, bf16[2,2,160,640]{3,2,1,0:T(8,128)(2,1)}) custom-call(s32[3]{0:T(128)} %pad_add_fusion.s, bf16[1280,1088]{1,0:T(8,128)(2,1)} %bitcast.318, bf16[1280,1088]{1,0:T(8,128)(2,1)} %bitcast.328, ...), custom_call_target="tpu_custom_call" | custom-call | flops 3565158400 | bytes 8847360 | tf_op jit(solution)/shard_map/attention_weights/pallas_call | solution.py:492
  642.3 15.4 %attention_weights.2 = (bf16[2,2,160,640]{3,2,1,0:T(8,128)(2,1)}, bf16[2,2,160,640]{3,2,1,0:T(8,128)(2,1)}, bf16[2,2,160,640]{3,2,1,0:T(8,128)(2,1)}, bf16[2,2,160,640]{3,2,1,0:T(8,128)(2,1)}) custom-call(s32[3]{0:T(128)} %pad_add_fusion.s, bf16[1280,1088]{1,0:T(8,128)(2,1)} %bitcast.319, bf16[1280,1088]{1,0:T(8,128)(2,1)} %bitcast.329, ...), custom_call_target="tpu_custom_call" | custom-call | flops 3565158400 | bytes 8847360 | tf_op jit(solution)/shard_map/attention_weights/pallas_call | solution.py:492
  659.8 3.5 fusion.2
  667.3 11.9 %collective-permute-done.66 = bf16[2,2,160,640]{3,2,1,0:T(8,128)(2,1)} collective-permute-done((bf16[2,2,160,640]{3,2,1,0:T(8,128)(2,1)}, bf16[2,2,160,640]{3,2,1,0:T(8,128)(2,1)}, u32[]{:S(2)}, u32[]{:S(2)}) %collective-permute-start.66) | collective-permute-done | bytes 819232 | tf_op jit(solution)/shard_map/ppermute | solution.py:85
  682.8 13.0 %collective-permute-done.52 = bf16[2,2,160,640]{3,2,1,0:T(8,128)(2,1)} collective-permute-done((bf16[2,2,160,640]{3,2,1,0:T(8,128)(2,1)}, bf16[2,2,160,640]{3,2,1,0:T(8,128)(2,1)}, u32[]{:S(2)}, u32[]{:S(2)}) %collective-permute-start.52) | collective-permute-done | bytes 819232 | tf_op jit(solution)/shard_map/ppermute | solution.py:85
  700.5 3.1 collective-permute-done.58
  705.0 7.4 collective-permute-done.53
  715.4 4.3 collective-permute-done.67
  728.6 5.8 first_norm_back.1
  737.9 2.9 collective-permute-done.83
  742.8 18.4 %collective-permute-done.65 = bf16[2,2,160,640]{3,2,1,0:T(8,128)(2,1)} collective-permute-done((bf16[2,2,160,640]{3,2,1,0:T(8,128)(2,1)}, bf16[2,2,160,640]{3,2,1,0:T(8,128)(2,1)}, u32[]{:S(2)}, u32[]{:S(2)}) %collective-permute-start.65) | collective-permute-done | bytes 819232 | tf_op jit(solution)/shard_map/ppermute | solution.py:89
  761.2 18.5 %collective-permute-done.68 = bf16[2,160,640]{2,1,0:T(8,128)(2,1)} collective-permute-done((bf16[2,160,640]{2,1,0:T(8,128)(2,1)}, bf16[2,160,640]{2,1,0:T(8,128)(2,1)}, u32[]{:S(2)}, u32[]{:S(2)}) %collective-permute-start.68) | collective-permute-done | bytes 409632 | tf_op jit(solution)/shard_map/ppermute | solution.py:89
  783.5 8.6 %collective-permute-start.86 = (f32[2,12,40]{2,1,0:T(8,128)S(1)}, f32[2,12,40]{2,1,0:T(8,128)S(1)}, u32[]{:S(2)}, u32[]{:S(2)}) collective-permute-start(f32[2,12,40]{2,1,0:T(8,128)S(1)} %select_bitcast_fusion.1), channel_id=1, source_target_pairs={{0,2},{1,3},{2,0},{3,1},{4,6},{5,7},{6,4},{7,5},{8,10},{9,11},{10,... | collective-permute-start | bytes 11528 | tf_op jit(solution)/shard_map/ppermute | solution.py:172
  794.2 2.3 collective-permute-start.87
  798.6 2.9 collective-permute-start.50
  813.6 14.4 %collective-permute-done.51 = bf16[416,1280]{1,0:T(8,128)(2,1)} collective-permute-done((bf16[416,1280]{1,0:T(8,128)(2,1)}, bf16[416,1280]{1,0:T(8,128)(2,1)}, u32[]{:S(2)}, u32[]{:S(2)}) %collective-permute-start.51) | collective-permute-done | bytes 1064992 | tf_op jit(solution)/shard_map/ppermute | solution.py:94
  830.3 2.4 fusion.11
  832.8 2.8 fusion.1
  (497 shorter events, 200.7 us)
Async XLA Ops:
  2.1 31.8 %collective-permute-start.3 = (f32[1,12,40]{2,1,0:T(8,128)S(1)}, f32[1,12,40]{2,1,0:T(8,128)S(1)}, u32[]{:S(2)}, u32[]{:S(2)}) collective-permute-start(f32[1,12,40]{2,1,0:T(8,128)S(1)} %maximum_bitcast_fusion.6), channel_id=1, source_target_pairs={{0,1},{1,0},{2,3},{3,2},{4,5},{5,4},{6,7},{7,6},{8,9},{9,8},{10,11... | collective-permute-start | bytes 5768 | tf_op jit(solution)/shard_map/ppermute | solution.py:142
  10.0 40.5 %collective-permute-start.8 = (bf16[3,160,640]{2,1,0:T(8,128)(2,1)}, bf16[3,160,640]{2,1,0:T(8,128)(2,1)}, u32[]{:S(2)}, u32[]{:S(2)}) collective-permute-start(bf16[3,160,640]{2,1,0:T(8,128)(2,1)} %get-tuple-element.133), channel_id=1, source_target_pairs={{0,4},{4,0},{8,12},{12,8},{16,20},{20,16},{24,28},{28,24},{1,5},{5... | collective-permute-start | bytes 1843208 | tf_op jit(solution)/shard_map/ppermute | solution.py:85
  14.1 73.2 %collective-permute-start.1 = (bf16[416,1280]{1,0:T(8,128)(2,1)}, bf16[416,1280]{1,0:T(8,128)(2,1)}, u32[]{:S(2)}, u32[]{:S(2)}) collective-permute-start(bf16[416,1280]{1,0:T(8,128)(2,1)} %get-tuple-element.126), channel_id=1, source_target_pairs={{0,1},{1,2},{2,3},{4,5},{5,6},{6,7},{8,9},{9,10},{10,11},{12,13},{... | collective-permute-start | bytes 3194888 | tf_op jit(solution)/shard_map/ppermute | solution.py:94
  17.0 66.6 %collective-permute-start = (bf16[416,1280]{1,0:T(8,128)(2,1)}, bf16[416,1280]{1,0:T(8,128)(2,1)}, u32[]{:S(2)}, u32[]{:S(2)}) collective-permute-start(bf16[416,1280]{1,0:T(8,128)(2,1)} %get-tuple-element.127), channel_id=1, source_target_pairs={{1,0},{2,1},{3,2},{5,4},{6,5},{7,6},{9,8},{10,9},{11,10},{13,12},{... | collective-permute-start | bytes 3194888 | tf_op jit(solution)/shard_map/ppermute | solution.py:94
  53.2 22.1 %collective-permute-start.14 = (bf16[2,160,640]{2,1,0:T(8,128)(2,1)}, bf16[2,160,640]{2,1,0:T(8,128)(2,1)}, u32[]{:S(2)}, u32[]{:S(2)}) collective-permute-start(bf16[2,160,640]{2,1,0:T(8,128)(2,1)} %get-tuple-element.141), channel_id=1, source_target_pairs={{0,2},{1,3},{2,0},{3,1},{4,6},{5,7},{6,4},{7,5},{8,10},{9,11},{10,... | collective-permute-start | bytes 1228808 | tf_op jit(solution)/shard_map/ppermute | solution.py:89
  53.2 23.6 %collective-permute-start.15 = (bf16[2,160,640]{2,1,0:T(8,128)(2,1)}, bf16[2,160,640]{2,1,0:T(8,128)(2,1)}, u32[]{:S(2)}, u32[]{:S(2)}) collective-permute-start(bf16[2,160,640]{2,1,0:T(8,128)(2,1)} %get-tuple-element.141), channel_id=1, source_target_pairs={{0,3},{1,0},{2,1},{3,2},{4,7},{5,4},{6,5},{7,6},{8,11},{9,8},{10,9... | collective-permute-start | bytes 1228808 | tf_op jit(solution)/shard_map/ppermute | solution.py:89
  56.4 26.5 %collective-permute-start.9 = (bf16[2,160,640]{2,1,0:T(8,128)(2,1)}, bf16[2,160,640]{2,1,0:T(8,128)(2,1)S(1)}, u32[]{:S(2)}, u32[]{:S(2)}) collective-permute-start(bf16[2,160,640]{2,1,0:T(8,128)(2,1)} %get-tuple-element.141), channel_id=1, source_target_pairs={{0,1},{1,2},{2,3},{3,0},{4,5},{5,6},{6,7},{7,4},{8,9},{9,10},{10,1... | collective-permute-start | bytes 1228808 | tf_op jit(solution)/shard_map/ppermute | solution.py:89
  83.6 33.3 %collective-permute-start.11 = (bf16[2,2,160,640]{3,2,1,0:T(8,128)(2,1)S(1)}, bf16[2,2,160,640]{3,2,1,0:T(8,128)(2,1)S(1)}, u32[]{:S(2)}, u32[]{:S(2)}) collective-permute-start(bf16[2,2,160,640]{3,2,1,0:T(8,128)(2,1)S(1)} %pad_maximum_fusion.4.rest_0_), channel_id=1, source_target_pairs={{0,16},{4,20},{8,24},{12,28},{16,0},{20,4},{24,8},{28,12},{1,17},{... | collective-permute-start | bytes 2457608 | tf_op jit(solution)/shard_map/ppermute | solution.py:85
  89.6 37.7 %collective-permute-start.2 = (bf16[2,272,1280]{2,1,0:T(8,128)(2,1)S(1)}, bf16[2,272,1280]{2,1,0:T(8,128)(2,1)S(1)}, u32[]{:S(2)}, u32[]{:S(2)}) collective-permute-start(bf16[2,272,1280]{2,1,0:T(8,128)(2,1)S(1)} %bitcast.287), channel_id=1, source_target_pairs={{0,4},{4,0},{8,12},{12,8},{16,20},{20,16},{24,28},{28,24},{1,5},{5... | collective-permute-start | bytes 4177928 | tf_op jit(solution)/shard_map/ppermute | solution.py:85
  89.7 31.9 %collective-permute-start.10 = (bf16[2,2,160,640]{3,2,1,0:T(8,128)(2,1)S(1)}, bf16[2,2,160,640]{3,2,1,0:T(8,128)(2,1)S(1)}, u32[]{:S(2)}, u32[]{:S(2)}) collective-permute-start(bf16[2,2,160,640]{3,2,1,0:T(8,128)(2,1)S(1)} %pad_maximum_fusion.4.rest_0_), channel_id=1, source_target_pairs={{0,8},{4,12},{8,0},{12,4},{16,24},{20,28},{24,16},{28,20},{1,9},{5... | collective-permute-start | bytes 2457608 | tf_op jit(solution)/shard_map/ppermute | solution.py:85
  99.3 44.7 %collective-permute-start.19 = (bf16[2,160,640]{2,1,0:T(8,128)(2,1)S(1)}, bf16[2,160,640]{2,1,0:T(8,128)(2,1)}, u32[]{:S(2)}, u32[]{:S(2)}) collective-permute-start(bf16[2,160,640]{2,1,0:T(8,128)(2,1)S(1)} %slice_bitcast_fusion.14), channel_id=1, source_target_pairs={{0,8},{4,12},{8,0},{12,4},{16,24},{20,28},{24,16},{28,20},{1,9},{5... | collective-permute-start | bytes 1228808 | tf_op jit(solution)/shard_map/ppermute | solution.py:85
  104.9 40.6 %collective-permute-start.18 = (bf16[2,160,640]{2,1,0:T(8,128)(2,1)}, bf16[2,160,640]{2,1,0:T(8,128)(2,1)}, u32[]{:S(2)}, u32[]{:S(2)}) collective-permute-start(bf16[2,160,640]{2,1,0:T(8,128)(2,1)} %slice_bitcast_fusion.15), channel_id=1, source_target_pairs={{0,16},{4,20},{8,24},{12,28},{16,0},{20,4},{24,8},{28,12},{1,17},{... | collective-permute-start | bytes 1228808 | tf_op jit(solution)/shard_map/ppermute | solution.py:85
  117.7 27.8 %collective-permute-start.13 = (bf16[2,160,640]{2,1,0:T(8,128)(2,1)}, bf16[2,160,640]{2,1,0:T(8,128)(2,1)}, u32[]{:S(2)}, u32[]{:S(2)}) collective-permute-start(bf16[2,160,640]{2,1,0:T(8,128)(2,1)} %slice_bitcast_fusion.16), channel_id=1, source_target_pairs={{0,8},{4,12},{8,0},{12,4},{16,24},{20,28},{24,16},{28,20},{1,9},{5... | collective-permute-start | bytes 1228808 | tf_op jit(solution)/shard_map/ppermute | solution.py:85
  122.5 23.0 %collective-permute-start.12 = (bf16[2,160,640]{2,1,0:T(8,128)(2,1)}, bf16[2,160,640]{2,1,0:T(8,128)(2,1)}, u32[]{:S(2)}, u32[]{:S(2)}) collective-permute-start(bf16[2,160,640]{2,1,0:T(8,128)(2,1)} %slice_bitcast_fusion.17), channel_id=1, source_target_pairs={{0,16},{4,20},{8,24},{12,28},{16,0},{20,4},{24,8},{28,12},{1,17},{... | collective-permute-start | bytes 1228808 | tf_op jit(solution)/shard_map/ppermute | solution.py:85
  127.3 73.0 %collective-permute-start.23 = (bf16[416,1280]{1,0:T(8,128)(2,1)}, bf16[416,1280]{1,0:T(8,128)(2,1)}, u32[]{:S(2)}, u32[]{:S(2)}) collective-permute-start(bf16[416,1280]{1,0:T(8,128)(2,1)} %get-tuple-element.124), channel_id=1, source_target_pairs={{0,1},{1,2},{2,3},{4,5},{5,6},{6,7},{8,9},{9,10},{10,11},{12,13},{... | collective-permute-start | bytes 3194888 | tf_op jit(solution)/shard_map/ppermute | solution.py:94
  144.0 59.3 %collective-permute-start.22 = (bf16[416,1280]{1,0:T(8,128)(2,1)}, bf16[416,1280]{1,0:T(8,128)(2,1)S(1)}, u32[]{:S(2)}, u32[]{:S(2)}) collective-permute-start(bf16[416,1280]{1,0:T(8,128)(2,1)} %get-tuple-element.125), channel_id=1, source_target_pairs={{1,0},{2,1},{3,2},{5,4},{6,5},{7,6},{9,8},{10,9},{11,10},{13,12},{... | collective-permute-start | bytes 3194888 | tf_op jit(solution)/shard_map/ppermute | solution.py:94
  186.1 102.5 %collective-permute-start.20 = (f32[2,272,1280]{2,1,0:T(8,128)}, f32[2,272,1280]{2,1,0:T(8,128)}, u32[]{:S(2)}, u32[]{:S(2)}) collective-permute-start(f32[2,272,1280]{2,1,0:T(8,128)} %get-tuple-element.120), channel_id=1, source_target_pairs={{0,4},{4,0},{8,12},{12,8},{16,20},{20,16},{24,28},{28,24},{1,5},{5... | collective-permute-start | bytes 8355848 | tf_op jit(solution)/shard_map/ppermute | solution.py:85
  186.9 24.2 %collective-permute-start.39 = (bf16[2,2,160,640]{3,2,1,0:T(8,128)(2,1)S(1)}, bf16[2,2,160,640]{3,2,1,0:T(8,128)(2,1)}, u32[]{:S(2)}, u32[]{:S(2)}) collective-permute-start(bf16[2,2,160,640]{3,2,1,0:T(8,128)(2,1)S(1)} %pad_maximum_fusion.6.rest_0_.refs_4_), channel_id=1, source_target_pairs={{0,3},{1,0},{2,1},{3,2},{4,7},{5,4},{6,5},{7,6},{8,11},{9,8},{10,9... | collective-permute-start | bytes 2457608 | tf_op jit(solution)/shard_map/ppermute | solution.py:89
  194.5 69.9 %collective-permute-start.34 = (bf16[2,2,160,640]{3,2,1,0:T(8,128)(2,1)S(1)}, bf16[2,2,160,640]{3,2,1,0:T(8,128)(2,1)}, u32[]{:S(2)}, u32[]{:S(2)}) collective-permute-start(bf16[2,2,160,640]{3,2,1,0:T(8,128)(2,1)S(1)} %pad_maximum_fusion.6.rest_0_.refs_4_), channel_id=1, source_target_pairs={{0,2},{1,3},{2,0},{3,1},{4,6},{5,7},{6,4},{7,5},{8,10},{9,11},{10,... | collective-permute-start | bytes 2457608 | tf_op jit(solution)/shard_map/ppermute | solution.py:89
  200.4 64.5 %collective-permute-start.29 = (bf16[2,2,160,640]{3,2,1,0:T(8,128)(2,1)S(1)}, bf16[2,2,160,640]{3,2,1,0:T(8,128)(2,1)}, u32[]{:S(2)}, u32[]{:S(2)}) collective-permute-start(bf16[2,2,160,640]{3,2,1,0:T(8,128)(2,1)S(1)} %pad_maximum_fusion.6.rest_0_.refs_4_), channel_id=1, source_target_pairs={{0,1},{1,2},{2,3},{3,0},{4,5},{5,6},{6,7},{7,4},{8,9},{9,10},{10,1... | collective-permute-start | bytes 2457608 | tf_op jit(solution)/shard_map/ppermute | solution.py:89
  203.4 65.4 %collective-permute-start.26 = (bf16[2,2,160,640]{3,2,1,0:T(8,128)(2,1)S(1)}, bf16[2,2,160,640]{3,2,1,0:T(8,128)(2,1)S(1)}, u32[]{:S(2)}, u32[]{:S(2)}) collective-permute-start(bf16[2,2,160,640]{3,2,1,0:T(8,128)(2,1)S(1)} %pad_maximum_fusion.6.rest_0_.refs_4_), channel_id=1, source_target_pairs={{0,16},{4,20},{8,24},{12,28},{16,0},{20,4},{24,8},{28,12},{1,17},{... | collective-permute-start | bytes 2457608 | tf_op jit(solution)/shard_map/ppermute | solution.py:85
  211.0 60.0 %collective-permute-start.25 = (bf16[2,2,160,640]{3,2,1,0:T(8,128)(2,1)S(1)}, bf16[2,2,160,640]{3,2,1,0:T(8,128)(2,1)S(1)}, u32[]{:S(2)}, u32[]{:S(2)}) collective-permute-start(bf16[2,2,160,640]{3,2,1,0:T(8,128)(2,1)S(1)} %pad_maximum_fusion.6.rest_0_.refs_4_), channel_id=1, source_target_pairs={{0,8},{4,12},{8,0},{12,4},{16,24},{20,28},{24,16},{28,20},{1,9},{5... | collective-permute-start | bytes 2457608 | tf_op jit(solution)/shard_map/ppermute | solution.py:85
  264.9 21.4 %collective-permute-start.40 = (bf16[2,2,160,640]{3,2,1,0:T(8,128)(2,1)}, bf16[2,2,160,640]{3,2,1,0:T(8,128)(2,1)S(1)}, u32[]{:S(2)}, u32[]{:S(2)}) collective-permute-start(bf16[2,2,160,640]{3,2,1,0:T(8,128)(2,1)} %collective-permute-done.39.rest_0_.refs_19_), channel_id=1, source_target_pairs={{0,8},{4,12},{8,0},{12,4},{16,24},{20,28},{24,16},{28,20},{1,9},{5... | collective-permute-start | bytes 2457608 | tf_op jit(solution)/shard_map/ppermute | solution.py:85
  268.8 34.5 %collective-permute-start.36 = (bf16[2,2,160,640]{3,2,1,0:T(8,128)(2,1)}, bf16[2,2,160,640]{3,2,1,0:T(8,128)(2,1)S(1)}, u32[]{:S(2)}, u32[]{:S(2)}) collective-permute-start(bf16[2,2,160,640]{3,2,1,0:T(8,128)(2,1)} %collective-permute-done.34.rest_0_.refs_14_), channel_id=1, source_target_pairs={{0,16},{4,20},{8,24},{12,28},{16,0},{20,4},{24,8},{28,12},{1,17},{... | collective-permute-start | bytes 2457608 | tf_op jit(solution)/shard_map/ppermute | solution.py:85
  271.1 33.1 %collective-permute-start.35 = (bf16[2,2,160,640]{3,2,1,0:T(8,128)(2,1)}, bf16[2,2,160,640]{3,2,1,0:T(8,128)(2,1)S(1)}, u32[]{:S(2)}, u32[]{:S(2)}) collective-permute-start(bf16[2,2,160,640]{3,2,1,0:T(8,128)(2,1)} %collective-permute-done.34.rest_0_.refs_14_), channel_id=1, source_target_pairs={{0,8},{4,12},{8,0},{12,4},{16,24},{20,28},{24,16},{28,20},{1,9},{5... | collective-permute-start | bytes 2457608 | tf_op jit(solution)/shard_map/ppermute | solution.py:85
  285.7 37.0 %collective-permute-start.24 = (bf16[2,272,1280]{2,1,0:T(8,128)(2,1)}, bf16[2,272,1280]{2,1,0:T(8,128)(2,1)}, u32[]{:S(2)}, u32[]{:S(2)}) collective-permute-start(bf16[2,272,1280]{2,1,0:T(8,128)(2,1)} %bitcast.39.cot_ref), channel_id=1, source_target_pairs={{0,4},{4,0},{8,12},{12,8},{16,20},{20,16},{24,28},{28,24},{1,5},{5... | collective-permute-start | bytes 4177928 | tf_op jit(solution)/shard_map/ppermute | solution.py:85
  286.3 33.3 %collective-permute-start.31 = (bf16[2,2,160,640]{3,2,1,0:T(8,128)(2,1)}, bf16[2,2,160,640]{3,2,1,0:T(8,128)(2,1)S(1)}, u32[]{:S(2)}, u32[]{:S(2)}) collective-permute-start(bf16[2,2,160,640]{3,2,1,0:T(8,128)(2,1)} %collective-permute-done.29.rest_0_.refs_9_), channel_id=1, source_target_pairs={{0,16},{4,20},{8,24},{12,28},{16,0},{20,4},{24,8},{28,12},{1,17},{... | collective-permute-start | bytes 2457608 | tf_op jit(solution)/shard_map/ppermute | solution.py:85
  288.6 32.8 %collective-permute-start.30 = (bf16[2,2,160,640]{3,2,1,0:T(8,128)(2,1)}, bf16[2,2,160,640]{3,2,1,0:T(8,128)(2,1)S(1)}, u32[]{:S(2)}, u32[]{:S(2)}) collective-permute-start(bf16[2,2,160,640]{3,2,1,0:T(8,128)(2,1)} %collective-permute-done.29.rest_0_.refs_9_), channel_id=1, source_target_pairs={{0,8},{4,12},{8,0},{12,4},{16,24},{20,28},{24,16},{28,20},{1,9},{5... | collective-permute-start | bytes 2457608 | tf_op jit(solution)/shard_map/ppermute | solution.py:85
  303.3 33.3 %collective-permute-start.21 = (bf16[2,272,1280]{2,1,0:T(8,128)(2,1)}, bf16[2,272,1280]{2,1,0:T(8,128)(2,1)}, u32[]{:S(2)}, u32[]{:S(2)}) collective-permute-start(bf16[2,272,1280]{2,1,0:T(8,128)(2,1)} %get-tuple-element.64), channel_id=1, source_target_pairs={{0,4},{4,0},{8,12},{12,8},{16,20},{20,16},{24,28},{28,24},{1,5},{5... | collective-permute-start | bytes 4177928 | tf_op jit(solution)/shard_map/ppermute | solution.py:85
  304.2 106.5 %collective-permute-start.28 = (bf16[2,160,640]{2,1,0:T(8,128)(2,1)}, bf16[2,160,640]{2,1,0:T(8,128)(2,1)S(1)}, u32[]{:S(2)}, u32[]{:S(2)}) collective-permute-start(bf16[2,160,640]{2,1,0:T(8,128)(2,1)} %slice_bitcast_fusion.12), channel_id=1, source_target_pairs={{0,8},{4,12},{8,0},{12,4},{16,24},{20,28},{24,16},{28,20},{1,9},{5... | collective-permute-start | bytes 1228808 | tf_op jit(solution)/shard_map/ppermute | solution.py:85
  319.6 92.7 %collective-permute-start.27 = (bf16[2,160,640]{2,1,0:T(8,128)(2,1)}, bf16[2,160,640]{2,1,0:T(8,128)(2,1)}, u32[]{:S(2)}, u32[]{:S(2)}) collective-permute-start(bf16[2,160,640]{2,1,0:T(8,128)(2,1)} %slice_bitcast_fusion.13), channel_id=1, source_target_pairs={{0,16},{4,20},{8,24},{12,28},{16,0},{20,4},{24,8},{28,12},{1,17},{... | collective-permute-start | bytes 1228808 | tf_op jit(solution)/shard_map/ppermute | solution.py:85
  321.4 24.7 %collective-permute-start.43 = (bf16[2,160,640]{2,1,0:T(8,128)(2,1)}, bf16[2,160,640]{2,1,0:T(8,128)(2,1)}, u32[]{:S(2)}, u32[]{:S(2)}) collective-permute-start(bf16[2,160,640]{2,1,0:T(8,128)(2,1)} %slice_bitcast_fusion.6), channel_id=1, source_target_pairs={{0,8},{4,12},{8,0},{12,4},{16,24},{20,28},{24,16},{28,20},{1,9},{5... | collective-permute-start | bytes 1228808 | tf_op jit(solution)/shard_map/ppermute | solution.py:85
  322.7 23.9 %collective-permute-start.42 = (bf16[2,160,640]{2,1,0:T(8,128)(2,1)}, bf16[2,160,640]{2,1,0:T(8,128)(2,1)}, u32[]{:S(2)}, u32[]{:S(2)}) collective-permute-start(bf16[2,160,640]{2,1,0:T(8,128)(2,1)} %slice_bitcast_fusion.7), channel_id=1, source_target_pairs={{0,16},{4,20},{8,24},{12,28},{16,0},{20,4},{24,8},{28,12},{1,17},{... | collective-permute-start | bytes 1228808 | tf_op jit(solution)/shard_map/ppermute | solution.py:85
  336.6 30.3 %collective-permute-start.38 = (bf16[2,160,640]{2,1,0:T(8,128)(2,1)S(1)}, bf16[2,160,640]{2,1,0:T(8,128)(2,1)S(1)}, u32[]{:S(2)}, u32[]{:S(2)}) collective-permute-start(bf16[2,160,640]{2,1,0:T(8,128)(2,1)S(1)} %copy-done.66), channel_id=1, source_target_pairs={{0,8},{4,12},{8,0},{12,4},{16,24},{20,28},{24,16},{28,20},{1,9},{5... | collective-permute-start | bytes 1228808 | tf_op jit(solution)/shard_map/ppermute | solution.py:85
  346.1 22.5 %collective-permute-start.37 = (bf16[2,160,640]{2,1,0:T(8,128)(2,1)}, bf16[2,160,640]{2,1,0:T(8,128)(2,1)S(1)}, u32[]{:S(2)}, u32[]{:S(2)}) collective-permute-start(bf16[2,160,640]{2,1,0:T(8,128)(2,1)} %slice_bitcast_fusion.9), channel_id=1, source_target_pairs={{0,16},{4,20},{8,24},{12,28},{16,0},{20,4},{24,8},{28,12},{1,17},{... | collective-permute-start | bytes 1228808 | tf_op jit(solution)/shard_map/ppermute | solution.py:85
  346.6 43.1 %collective-permute-start.33 = (bf16[2,160,640]{2,1,0:T(8,128)(2,1)S(1)}, bf16[2,160,640]{2,1,0:T(8,128)(2,1)S(1)}, u32[]{:S(2)}, u32[]{:S(2)}) collective-permute-start(bf16[2,160,640]{2,1,0:T(8,128)(2,1)S(1)} %copy-done.64), channel_id=1, source_target_pairs={{0,8},{4,12},{8,0},{12,4},{16,24},{20,28},{24,16},{28,20},{1,9},{5... | collective-permute-start | bytes 1228808 | tf_op jit(solution)/shard_map/ppermute | solution.py:85
  366.9 23.3 %collective-permute-start.32 = (bf16[2,160,640]{2,1,0:T(8,128)(2,1)S(1)}, bf16[2,160,640]{2,1,0:T(8,128)(2,1)S(1)}, u32[]{:S(2)}, u32[]{:S(2)}) collective-permute-start(bf16[2,160,640]{2,1,0:T(8,128)(2,1)S(1)} %copy-done.65), channel_id=1, source_target_pairs={{0,16},{4,20},{8,24},{12,28},{16,0},{20,4},{24,8},{28,12},{1,17},{... | collective-permute-start | bytes 1228808 | tf_op jit(solution)/shard_map/ppermute | solution.py:85
  368.6 109.5 %collective-permute-start.77 = (bf16[2,2,160,640]{3,2,1,0:T(8,128)(2,1)}, bf16[2,2,160,640]{3,2,1,0:T(8,128)(2,1)}, u32[]{:S(2)}, u32[]{:S(2)}) collective-permute-start(bf16[2,2,160,640]{3,2,1,0:T(8,128)(2,1)} %get-tuple-element.103), channel_id=1, source_target_pairs={{0,8},{4,12},{8,0},{12,4},{16,24},{20,28},{24,16},{28,20},{1,9},{5... | collective-permute-start | bytes 2457608 | tf_op jit(solution)/shard_map/ppermute | solution.py:85
  389.7 90.4 %collective-permute-start.79 = (bf16[2,2,160,640]{3,2,1,0:T(8,128)(2,1)}, bf16[2,2,160,640]{3,2,1,0:T(8,128)(2,1)}, u32[]{:S(2)}, u32[]{:S(2)}) collective-permute-start(bf16[2,2,160,640]{3,2,1,0:T(8,128)(2,1)} %get-tuple-element.105), channel_id=1, source_target_pairs={{0,16},{4,20},{8,24},{12,28},{16,0},{20,4},{24,8},{28,12},{1,17},{... | collective-permute-start | bytes 2457608 | tf_op jit(solution)/shard_map/ppermute | solution.py:85
  390.3 91.7 %collective-permute-start.69 = (bf16[2,2,160,640]{3,2,1,0:T(8,128)(2,1)}, bf16[2,2,160,640]{3,2,1,0:T(8,128)(2,1)}, u32[]{:S(2)}, u32[]{:S(2)}) collective-permute-start(bf16[2,2,160,640]{3,2,1,0:T(8,128)(2,1)} %get-tuple-element.97), channel_id=1, source_target_pairs={{0,8},{4,12},{8,0},{12,4},{16,24},{20,28},{24,16},{28,20},{1,9},{5... | collective-permute-start | bytes 2457608 | tf_op jit(solution)/shard_map/ppermute | solution.py:85
  410.7 74.1 %collective-permute-start.71 = (bf16[2,2,160,640]{3,2,1,0:T(8,128)(2,1)}, bf16[2,2,160,640]{3,2,1,0:T(8,128)(2,1)}, u32[]{:S(2)}, u32[]{:S(2)}) collective-permute-start(bf16[2,2,160,640]{3,2,1,0:T(8,128)(2,1)} %get-tuple-element.99), channel_id=1, source_target_pairs={{0,16},{4,20},{8,24},{12,28},{16,0},{20,4},{24,8},{28,12},{1,17},{... | collective-permute-start | bytes 2457608 | tf_op jit(solution)/shard_map/ppermute | solution.py:85
  412.3 73.9 %collective-permute-start.61 = (bf16[2,2,160,640]{3,2,1,0:T(8,128)(2,1)}, bf16[2,2,160,640]{3,2,1,0:T(8,128)(2,1)}, u32[]{:S(2)}, u32[]{:S(2)}) collective-permute-start(bf16[2,2,160,640]{3,2,1,0:T(8,128)(2,1)} %get-tuple-element.91), channel_id=1, source_target_pairs={{0,8},{4,12},{8,0},{12,4},{16,24},{20,28},{24,16},{28,20},{1,9},{5... | collective-permute-start | bytes 2457608 | tf_op jit(solution)/shard_map/ppermute | solution.py:85
  478.0 21.5 %collective-permute-start.63 = (bf16[2,2,160,640]{3,2,1,0:T(8,128)(2,1)}, bf16[2,2,160,640]{3,2,1,0:T(8,128)(2,1)S(1)}, u32[]{:S(2)}, u32[]{:S(2)}) collective-permute-start(bf16[2,2,160,640]{3,2,1,0:T(8,128)(2,1)} %get-tuple-element.93), channel_id=1, source_target_pairs={{0,16},{4,20},{8,24},{12,28},{16,0},{20,4},{24,8},{28,12},{1,17},{... | collective-permute-start | bytes 2457608 | tf_op jit(solution)/shard_map/ppermute | solution.py:85
  482.0 35.1 %collective-permute-start.56 = (bf16[2,2,160,640]{3,2,1,0:T(8,128)(2,1)}, bf16[2,2,160,640]{3,2,1,0:T(8,128)(2,1)S(1)}, u32[]{:S(2)}, u32[]{:S(2)}) collective-permute-start(bf16[2,2,160,640]{3,2,1,0:T(8,128)(2,1)} %get-tuple-element.87), channel_id=1, source_target_pairs={{0,16},{4,20},{8,24},{12,28},{16,0},{20,4},{24,8},{28,12},{1,17},{... | collective-permute-start | bytes 2457608 | tf_op jit(solution)/shard_map/ppermute | solution.py:85
  484.8 72.0 %collective-permute-start.47 = (f32[2,272,1280]{2,1,0:T(8,128)S(1)}, f32[2,272,1280]{2,1,0:T(8,128)S(1)}, u32[]{:S(2)}, u32[]{:S(2)}) collective-permute-start(f32[2,272,1280]{2,1,0:T(8,128)S(1)} %copy-done.27), channel_id=1, source_target_pairs={{0,4},{4,0},{8,12},{12,8},{16,20},{20,16},{24,28},{28,24},{1,5},{5... | collective-permute-start | bytes 8355848 | tf_op jit(solution)/shard_map/ppermute | solution.py:85
  486.2 64.5 %collective-permute-start.44 = (f32[2,272,1280]{2,1,0:T(8,128)S(1)}, f32[2,272,1280]{2,1,0:T(8,128)S(1)}, u32[]{:S(2)}, u32[]{:S(2)}) collective-permute-start(f32[2,272,1280]{2,1,0:T(8,128)S(1)} %copy-done.28), channel_id=1, source_target_pairs={{0,4},{4,0},{8,12},{12,8},{16,20},{20,16},{24,28},{28,24},{1,5},{5... | collective-permute-start | bytes 8355848 | tf_op jit(solution)/shard_map/ppermute | solution.py:85
  499.5 26.3 %collective-permute-start.78 = (bf16[2,160,640]{2,1,0:T(8,128)(2,1)S(1)}, bf16[2,160,640]{2,1,0:T(8,128)(2,1)S(1)}, u32[]{:S(2)}, u32[]{:S(2)}) collective-permute-start(bf16[2,160,640]{2,1,0:T(8,128)(2,1)S(1)} %fusion.52), channel_id=1, source_target_pairs={{0,16},{4,20},{8,24},{12,28},{16,0},{20,4},{24,8},{28,12},{1,17},{... | collective-permute-start | bytes 1228808 | tf_op jit(solution)/shard_map/ppermute | solution.py:85
  500.2 27.6 %collective-permute-start.80 = (bf16[2,160,640]{2,1,0:T(8,128)(2,1)S(1)}, bf16[2,160,640]{2,1,0:T(8,128)(2,1)S(1)}, u32[]{:S(2)}, u32[]{:S(2)}) collective-permute-start(bf16[2,160,640]{2,1,0:T(8,128)(2,1)S(1)} %fusion.53), channel_id=1, source_target_pairs={{0,8},{4,12},{8,0},{12,4},{16,24},{20,28},{24,16},{28,20},{1,9},{5... | collective-permute-start | bytes 1228808 | tf_op jit(solution)/shard_map/ppermute | solution.py:85
  568.8 91.0 %collective-permute-start.46 = (bf16[416,1280]{1,0:T(8,128)(2,1)}, bf16[416,1280]{1,0:T(8,128)(2,1)}, u32[]{:S(2)}, u32[]{:S(2)}) collective-permute-start(bf16[416,1280]{1,0:T(8,128)(2,1)} %convolution_convert_fusion.2), channel_id=1, source_target_pairs={{1,0},{2,1},{3,2},{5,4},{6,5},{7,6},{9,8},{10,9},{11,10},{13,12},{... | collective-permute-start | bytes 3194888 | tf_op jit(solution)/shard_map/ppermute | solution.py:94
  627.1 99.6 %collective-permute-start.49 = (f32[2,272,1280]{2,1,0:T(8,128)}, f32[2,272,1280]{2,1,0:T(8,128)S(1)}, u32[]{:S(2)}, u32[]{:S(2)}) collective-permute-start(f32[2,272,1280]{2,1,0:T(8,128)} %get-tuple-element.118), channel_id=1, source_target_pairs={{0,4},{4,0},{8,12},{12,8},{16,20},{20,16},{24,28},{28,24},{1,5},{5... | collective-permute-start | bytes 8355848 | tf_op jit(solution)/shard_map/ppermute | solution.py:85
  657.7 21.5 %collective-permute-start.66 = (bf16[2,2,160,640]{3,2,1,0:T(8,128)(2,1)}, bf16[2,2,160,640]{3,2,1,0:T(8,128)(2,1)}, u32[]{:S(2)}, u32[]{:S(2)}) collective-permute-start(bf16[2,2,160,640]{3,2,1,0:T(8,128)(2,1)} %get-tuple-element.95), channel_id=1, source_target_pairs={{0,8},{4,12},{8,0},{12,4},{16,24},{20,28},{24,16},{28,20},{1,9},{5... | collective-permute-start | bytes 2457608 | tf_op jit(solution)/shard_map/ppermute | solution.py:85
  658.8 37.0 %collective-permute-start.52 = (bf16[2,2,160,640]{3,2,1,0:T(8,128)(2,1)}, bf16[2,2,160,640]{3,2,1,0:T(8,128)(2,1)}, u32[]{:S(2)}, u32[]{:S(2)}) collective-permute-start(bf16[2,2,160,640]{3,2,1,0:T(8,128)(2,1)} %get-tuple-element.83), channel_id=1, source_target_pairs={{0,8},{4,12},{8,0},{12,4},{16,24},{20,28},{24,16},{28,20},{1,9},{5... | collective-permute-start | bytes 2457608 | tf_op jit(solution)/shard_map/ppermute | solution.py:85
  664.7 34.0 %collective-permute-start.74 = (bf16[2,2,160,640]{3,2,1,0:T(8,128)(2,1)}, bf16[2,2,160,640]{3,2,1,0:T(8,128)(2,1)}, u32[]{:S(2)}, u32[]{:S(2)}) collective-permute-start(bf16[2,2,160,640]{3,2,1,0:T(8,128)(2,1)} %get-tuple-element.101), channel_id=1, source_target_pairs={{0,16},{4,20},{8,24},{12,28},{16,0},{20,4},{24,8},{28,12},{1,17},{... | collective-permute-start | bytes 2457608 | tf_op jit(solution)/shard_map/ppermute | solution.py:85
  665.6 37.9 %collective-permute-start.58 = (bf16[2,2,160,640]{3,2,1,0:T(8,128)(2,1)}, bf16[2,2,160,640]{3,2,1,0:T(8,128)(2,1)S(1)}, u32[]{:S(2)}, u32[]{:S(2)}) collective-permute-start(bf16[2,2,160,640]{3,2,1,0:T(8,128)(2,1)} %get-tuple-element.89), channel_id=1, source_target_pairs={{0,16},{4,20},{8,24},{12,28},{16,0},{20,4},{24,8},{28,12},{1,17},{... | collective-permute-start | bytes 2457608 | tf_op jit(solution)/shard_map/ppermute | solution.py:85
  679.2 58.5 %collective-permute-start.81 = (bf16[2,2,160,640]{3,2,1,0:T(8,128)(2,1)}, bf16[2,2,160,640]{3,2,1,0:T(8,128)(2,1)}, u32[]{:S(2)}, u32[]{:S(2)}) collective-permute-start(bf16[2,2,160,640]{3,2,1,0:T(8,128)(2,1)} %pad_maximum_fusion.9), channel_id=1, source_target_pairs={{0,1},{1,2},{2,3},{3,0},{4,5},{5,6},{6,7},{7,4},{8,9},{9,10},{10,1... | collective-permute-start | bytes 2457608 | tf_op jit(solution)/shard_map/ppermute | solution.py:89
  695.8 45.9 %collective-permute-start.73 = (bf16[2,2,160,640]{3,2,1,0:T(8,128)(2,1)}, bf16[2,2,160,640]{3,2,1,0:T(8,128)(2,1)}, u32[]{:S(2)}, u32[]{:S(2)}) collective-permute-start(bf16[2,2,160,640]{3,2,1,0:T(8,128)(2,1)} %pad_maximum_fusion.8), channel_id=1, source_target_pairs={{0,2},{1,3},{2,0},{3,1},{4,6},{5,7},{6,4},{7,5},{8,10},{9,11},{10,... | collective-permute-start | bytes 2457608 | tf_op jit(solution)/shard_map/ppermute | solution.py:89
  719.7 41.5 %collective-permute-start.65 = (bf16[2,2,160,640]{3,2,1,0:T(8,128)(2,1)}, bf16[2,2,160,640]{3,2,1,0:T(8,128)(2,1)}, u32[]{:S(2)}, u32[]{:S(2)}) collective-permute-start(bf16[2,2,160,640]{3,2,1,0:T(8,128)(2,1)} %pad_maximum_fusion.7), channel_id=1, source_target_pairs={{0,3},{1,0},{2,1},{3,2},{4,7},{5,4},{6,5},{7,6},{8,11},{9,8},{10,9... | collective-permute-start | bytes 2457608 | tf_op jit(solution)/shard_map/ppermute | solution.py:89
  726.7 53.0 %collective-permute-start.68 = (bf16[2,160,640]{2,1,0:T(8,128)(2,1)}, bf16[2,160,640]{2,1,0:T(8,128)(2,1)}, u32[]{:S(2)}, u32[]{:S(2)}) collective-permute-start(bf16[2,160,640]{2,1,0:T(8,128)(2,1)} %fusion.23), channel_id=1, source_target_pairs={{0,2},{1,3},{2,0},{3,1},{4,6},{5,7},{6,4},{7,5},{8,10},{9,11},{10,... | collective-permute-start | bytes 1228808 | tf_op jit(solution)/shard_map/ppermute | solution.py:89
  737.7 42.0 %collective-permute-start.76 = (bf16[2,160,640]{2,1,0:T(8,128)(2,1)S(1)}, bf16[2,160,640]{2,1,0:T(8,128)(2,1)S(1)}, u32[]{:S(2)}, u32[]{:S(2)}) collective-permute-start(bf16[2,160,640]{2,1,0:T(8,128)(2,1)S(1)} %copy-done.63), channel_id=1, source_target_pairs={{0,1},{1,2},{2,3},{3,0},{4,5},{5,6},{6,7},{7,4},{8,9},{9,10},{10,1... | collective-permute-start | bytes 1228808 | tf_op jit(solution)/shard_map/ppermute | solution.py:89
  740.7 38.9 %collective-permute-start.60 = (bf16[2,160,640]{2,1,0:T(8,128)(2,1)S(1)}, bf16[2,160,640]{2,1,0:T(8,128)(2,1)S(1)}, u32[]{:S(2)}, u32[]{:S(2)}) collective-permute-start(bf16[2,160,640]{2,1,0:T(8,128)(2,1)S(1)} %fusion.26), channel_id=1, source_target_pairs={{0,3},{1,0},{2,1},{3,2},{4,7},{5,4},{6,5},{7,6},{8,11},{9,8},{10,9... | collective-permute-start | bytes 1228808 | tf_op jit(solution)/shard_map/ppermute | solution.py:89
  741.7 40.1 %collective-permute-start.84 = (f32[2,4,12,40]{3,2,1,0:T(8,128)S(1)}, f32[2,4,12,40]{3,2,1,0:T(8,128)S(1)}, u32[]{:S(2)}, u32[]{:S(2)}) collective-permute-start(f32[2,4,12,40]{3,2,1,0:T(8,128)S(1)} %slice_select_fusion), channel_id=1, source_target_pairs={{0,8},{4,12},{8,0},{12,4},{16,24},{20,28},{24,16},{28,20},{1,9},{5... | collective-permute-start | bytes 46088 | tf_op jit(solution)/shard_map/ppermute | solution.py:85
  783.0 21.6 %collective-permute-start.82 = (f32[3,160,640]{2,1,0:T(8,128)}, f32[3,160,640]{2,1,0:T(8,128)}, u32[]{:S(2)}, u32[]{:S(2)}) collective-permute-start(f32[3,160,640]{2,1,0:T(8,128)} %slice_bitcast_fusion), channel_id=1, source_target_pairs={{0,4},{4,0},{8,12},{12,8},{16,20},{20,16},{24,28},{28,24},{1,5},{5... | collective-permute-start | bytes 3686408 | tf_op jit(solution)/shard_map/ppermute | solution.py:85
  798.6 31.8 %collective-permute-start.50 = (bf16[416,1280]{1,0:T(8,128)(2,1)}, bf16[416,1280]{1,0:T(8,128)(2,1)}, u32[]{:S(2)}, u32[]{:S(2)}) collective-permute-start(bf16[416,1280]{1,0:T(8,128)(2,1)} %convolution_convert_fusion.1), channel_id=1, source_target_pairs={{0,1},{1,2},{2,3},{4,5},{5,6},{6,7},{8,9},{9,10},{10,11},{12,13},{... | collective-permute-start | bytes 3194888 | tf_op jit(solution)/shard_map/ppermute | solution.py:94
  801.5 26.5 %collective-permute-start.51 = (bf16[416,1280]{1,0:T(8,128)(2,1)}, bf16[416,1280]{1,0:T(8,128)(2,1)}, u32[]{:S(2)}, u32[]{:S(2)}) collective-permute-start(bf16[416,1280]{1,0:T(8,128)(2,1)} %convolution_convert_fusion), channel_id=1, source_target_pairs={{1,0},{2,1},{3,2},{5,4},{6,5},{7,6},{9,8},{10,9},{11,10},{13,12},{... | collective-permute-start | bytes 3194888 | tf_op jit(solution)/shard_map/ppermute | solution.py:94
  (115 other events, 1363.7 us)

commit v2 on v1

v2 whole, which is shorter than its diff:
```python
import math

import jax
import jax.numpy as jnp
from jax import lax
from jax.experimental import pallas as pl
from jax.experimental.pallas import tpu as pltpu
from jax.sharding import Mesh
from jax.sharding import PartitionSpec as P

D = 1280
HD = 80
HEADS = 16
FF = 5120
TOK_IMG = 257
IMG_DEV = 8
TOTAL = IMG_DEV * TOK_IMG
EPS = 1e-06
PT = 272
F32 = jnp.float32
BF16 = jnp.bfloat16
NEG = -1e30
VMEM_LIMIT = 56 * 1024 * 1024


class Cfg:
    def __init__(self, n_dp, n_t, block_rows):
        self.n_dp, self.n_t, self.block = n_dp, n_t, block_rows
        self.n_p = n_dp // 2
        self.imgs = IMG_DEV // n_t
        self.ni = 2 * self.imgs
        self.rows = self.imgs * TOK_IMG
        self.m = self.ni * PT
        self.pd = D // n_dp
        self.hh = HEADS // n_t // 2
        self.hc = self.hh * HD
        self.f2 = FF // n_t // 2
        assert 4 * self.hc == self.f2
        self.caps = self._caps()

    def _caps(self):
        n, b, r = self.n_t, self.block, self.rows
        low = [max(t, TOTAL - (n - t) * b) for t in range(n + 1)]
        high = [min(t * b, TOTAL - (n - t)) for t in range(n + 1)]
        caps = {}
        for t in range(n):
            for dest in range(n):
                size = min(high[t + 1], r * (dest + 1)) - max(low[t], r * dest)
                size = min(size, b, r)
                if size > 0 and dest != t:
                    caps[dest - t] = max(caps.get(dest - t, 0), size)
        return {s: min(-(-c // 16) * 16, b, r) for s, c in sorted(caps.items())}


def dot(a, b):
    return lax.dot_general(a, b, (((1,), (0,)), ((), ())), preferred_element_type=F32)


def dot_nt(a, b):
    return lax.dot_general(a, b, (((1,), (1,)), ((), ())), preferred_element_type=F32)


def dot_tn(a, b):
    return lax.dot_general(a, b, (((0,), (0,)), ((), ())), preferred_element_type=F32)


def norm(values):
    mean = jnp.mean(values, axis=-1, keepdims=True)
    centred = values - mean
    spread = jnp.mean(centred * centred, axis=-1, keepdims=True)
    inverse = lax.rsqrt(spread + EPS)
    return centred * inverse, inverse


def norm_back(upstream, normed, inverse, gain):
    scaled = upstream * gain
    return inverse * (
        scaled
        - jnp.mean(scaled, axis=-1, keepdims=True)
        - normed * jnp.mean(scaled * normed, axis=-1, keepdims=True)
    )


CHIPS = ("p", "t")
ALL = ("p", "c", "t")


def swap_core(value):
    return lax.ppermute(value, "c", [(0, 1), (1, 0)])


def step_tensor(value, shift, cfg):
    pairs = [(i, i + shift) for i in range(cfg.n_t) if 0 <= i + shift < cfg.n_t]
    return lax.ppermute(value, "t", pairs)


def scatter_chips(value):
    return lax.psum_scatter(value, CHIPS, scatter_dimension=0, tiled=False)


def gather_small(value, cfg, where):
    for axis, size in (("t", cfg.n_t), ("c", 2), ("p", cfg.n_p)):
        value = value[None]
        bit = 1
        while bit < size:
            other = lax.ppermute(value, axis, [(i, i ^ bit) for i in range(size)])
            first = (where[axis] & bit) == 0
            value = jnp.concatenate([jnp.where(first, value, other), jnp.where(first, other, value)])
            bit *= 2
    return value


def scatter_small(value, cfg, where):
    for axis, size in (("p", cfg.n_p), ("c", 2), ("t", cfg.n_t)):
        bit = size // 2
        while bit >= 1:
            half = value.shape[0] // 2
            first = (where[axis] & bit) == 0
            keep = jnp.where(first, value[:half], value[half:])
            send = jnp.where(first, value[half:], value[:half])
            value = keep + lax.ppermute(send, axis, [(i, i ^ bit) for i in range(size)])
            bit //= 2
        value = value[0]
    return value


def pick(positions, limit):
    return (positions[:, None] == jnp.arange(limit, dtype=jnp.int32)[None, :]).astype(BF16)


def window_start(starts, t, dest, size, cfg):
    return jnp.clip(cfg.rows * dest - starts[t], 0, cfg.block - size)


def to_images(block, starts, ends, z, cfg):
    slot = jnp.arange(cfg.imgs * PT, dtype=jnp.int32)
    within = slot % PT
    place = cfg.rows * z + (slot // PT) * TOK_IMG + within
    valid = within < TOK_IMG
    owner = jnp.sum((place[:, None] >= ends[None, :]).astype(jnp.int32), axis=1)
    padded = jnp.where(valid & (owner == z), place - starts[z], -1)
    total = dot(pick(padded, cfg.block), block)
    for shift, size in cfg.caps.items():
        dest = jnp.clip(z + shift, 0, cfg.n_t - 1)
        sent = lax.dynamic_slice_in_dim(block, window_start(starts, z, dest, size, cfg), size)
        got = step_tensor(sent, shift, cfg)
        source = jnp.clip(z - shift, 0, cfg.n_t - 1)
        offset = place - starts[source] - window_start(starts, source, z, size, cfg)
        offset = jnp.where(valid & (owner == z - shift), offset, -1)
        total = total + dot(pick(offset, size), got)
    return total.astype(BF16)


def to_blocks(images, starts, ends, z, cfg):
    row = jnp.arange(cfg.block, dtype=jnp.int32)
    place = starts[z] + row
    valid = place < ends[z]
    owner = place // cfg.rows
    local = place - cfg.rows * z
    slots = (local // TOK_IMG) * PT + local % TOK_IMG
    total = dot(pick(jnp.where(valid & (owner == z), slots, -1), cfg.imgs * PT), images)
    for shift, size in cfg.caps.items():
        block_to = jnp.clip(z - shift, 0, cfg.n_t - 1)
        begin = jnp.clip(starts[block_to] - cfg.rows * z, 0, cfg.rows - size)
        want = begin + jnp.arange(size, dtype=jnp.int32)
        want = (want // TOK_IMG) * PT + want % TOK_IMG
        sent = dot(pick(want, cfg.imgs * PT), images).astype(BF16)
        got = step_tensor(sent, -shift, cfg)
        source = jnp.clip(z + shift, 0, cfg.n_t - 1)
        begin_there = jnp.clip(starts[z] - cfg.rows * source, 0, cfg.rows - size)
        offset = place - cfg.rows * source - begin_there
        offset = jnp.where(valid & (owner == z + shift), offset, -1)
        total = total + dot(pick(offset, size), got)
    return total.astype(BF16)


def params(**more):
    return pltpu.CompilerParams(vmem_limit_bytes=VMEM_LIMIT, **more)


def fixed(shape):
    return pl.BlockSpec(
        shape, lambda i, *s: (0,) * len(shape), pipeline_mode=pl.Buffered(1)
    )


def image_spec(width):
    return pl.BlockSpec((1, PT, width), lambda i, *s: (i, 0, 0))


def chunk_image_spec(n_t, width):
    return pl.BlockSpec((n_t, 1, PT, width), lambda i, *s: (0, i, 0, 0))


def row_spec(count=1, width=D):
    return pl.BlockSpec((count, width), lambda i, *s: (0, 0))


MESH = pl.DeviceIdType.MESH


def neighbours(cfg):
    p, t = lax.axis_index("p"), lax.axis_index("t")
    found = [{"t": lax.rem(t + k, cfg.n_t)} for k in range(1, cfg.n_t)]
    return found + [{"p": p ^ m} for m in range(1, cfg.n_p)]


def enter(cfg):
    barrier = pltpu.get_barrier_semaphore()
    found = neighbours(cfg)
    for device in found:
        pl.semaphore_signal(barrier, inc=1, device_id=device, device_id_type=MESH)
    pl.semaphore_wait(barrier, len(found))


def gather_and_attend(x, gain, shift, query_bias, value_bias, blocks, cfg):
    n_t, n_p, ni, hc, hh, f2, pd = cfg.n_t, cfg.n_p, cfg.ni, cfg.hc, cfg.hh, cfg.f2, cfg.pd

    def kernel(
        x_ref, gain_ref, shift_ref, qb_ref, vb_ref, blk_ref,
        in_ref, qkv_ref, att_ref, lse_ref, out_ref, g0_ref, g_ref,
        w, z_send, z_recv, p_send, p_recv, own_sem, out_sem,
    ):
        p, core, z = (lax.axis_index(axis) for axis in ALL)

        def own(group):
            return blk_ref.at[0] if group == 0 else blk_ref.at[pl.ds(1, 2)]

        def place(group, k, m):
            t = lax.rem(z - k + n_t, n_t)
            rows = pl.ds(pl.multiple_of((p ^ m) * 2 * pd, 16), 2 * pd)
            return w.at[t, rows, :] if group == 0 else g_ref.at[:, t, rows, :]

        def remote(source, target, sems, index, device):
            return pltpu.make_async_remote_copy(
                src_ref=source,
                dst_ref=target,
                send_sem=sems[0].at[index],
                recv_sem=sems[1].at[index],
                device_id=device,
                device_id_type=MESH,
            )

        def z_copy(group, k):
            return remote(
                own(group), place(group, 0, 0), (z_send, z_recv), (group, k),
                {"t": lax.rem(z + k, n_t)},
            )

        def p_copy(group, k, m):
            source = own(group) if k == 0 else place(group, k, 0)
            return remote(
                source, place(group, k, 0), (p_send, p_recv), (group, k, m), {"p": p ^ m}
            )

        def d_copies(group, k):
            if n_p != 4:
                return []
            t = lax.rem(z - k + n_t, n_t)

            def rows(m):
                return pl.ds(pl.multiple_of((p ^ m) * 2 * pd, 16), 2 * pd)

            if group == 0:
                via = 1 + k % 2
                ref = w.at[t, rows(via), :]
                return [remote(ref, ref, (p_send, p_recv), (group, k, 3), {"p": p ^ (3 - via)})]
            ref_1, ref_2 = g_ref.at[0, t, rows(1), :], g_ref.at[1, t, rows(2), :]
            return [
                remote(ref_1, ref_1, (p_send, p_recv), (group, k, 3), {"p": p ^ 2}),
                remote(ref_2, ref_2, (p_send, p_recv), (group, k, 0), {"p": p ^ 1}),
            ]

        direct = (1, 2) if n_p == 4 else tuple(range(1, n_p))

        def send_z(group):
            for k in range(1, n_t):
                z_copy(group, k).start()

        def send_p(group, k):
            if k > 0:
                z_copy(group, k).wait_recv()
            for m in direct:
                p_copy(group, k, m).start()

        def send_d(group, k):
            for m in direct:
                p_copy(group, k, m).wait_recv()
            for copy in d_copies(group, k):
                copy.start()

        def finish(group):
            for k in range(n_t):
                for copy in d_copies(group, k):
                    copy.wait_recv()
                    copy.wait_send()
                for m in direct:
                    p_copy(group, k, m).wait_send()
                if k > 0:
                    z_copy(group, k).wait_send()

        keep_0 = pltpu.make_async_copy(own(0), place(0, 0, 0), own_sem.at[0])
        keep_1 = pltpu.make_async_copy(own(1), place(1, 0, 0), own_sem.at[1])
        keep_0.start()
        keep_1.start()
        enter(cfg)
        send_z(0)
        send_p(0, 0)
        for k in range(1, n_t):
            send_p(0, k)
            if k == 1:
                send_z(1)
            send_d(0, k - 1)
        send_p(1, 0)
        send_d(0, n_t - 1)
        finish(0)
        keep_0.wait()
        kept = pltpu.make_async_copy(w, g0_ref, out_sem)
        kept.start()

        steps = []
        for k in range(1, n_t):
            steps += [lambda k=k: send_p(1, k), lambda k=k: send_d(1, k - 1)]
        steps.append(lambda: send_d(1, n_t - 1))
        early = 2 * len(steps) // 5
        keyed = lax.broadcasted_iota(jnp.int32, (PT, PT), 1) < TOK_IMG

        def image(i, carry):
            normed, _ = norm(x_ref[i].astype(F32))
            attn_in = (normed * gain_ref[...] + shift_ref[...]).astype(BF16)
            in_ref[i] = attn_in
            for k in range(n_t):
                block = 2 * k + core
                qkv = dot(attn_in, w[k, :, : 3 * hc])
                query = (qkv[:, :hc] + qb_ref[pl.ds(block, 1), :]).astype(BF16)
                keys = qkv[:, hc : 2 * hc].astype(BF16)
                values = (qkv[:, 2 * hc :] + vb_ref[pl.ds(block, 1), :]).astype(BF16)
                qkv_ref[k, i, :, :hc] = query
                qkv_ref[k, i, :, hc : 2 * hc] = keys
                qkv_ref[k, i, :, 2 * hc :] = values
                for h in range(hh):
                    cols = slice(h * HD, (h + 1) * HD)
                    scores = dot_nt(query[:, cols], keys[:, cols]) * (HD**-0.5)
                    scores = jnp.where(keyed, scores, NEG)
                    top = jnp.max(scores, axis=-1, keepdims=True)
                    expo = jnp.exp(scores - top)
                    summed = jnp.sum(expo, axis=-1, keepdims=True)
                    probs = (expo / summed).astype(BF16)
                    att_ref[k, i, :, cols] = dot(probs, values[:, cols]).astype(BF16)
                    j = k * hh + h
                    lse_ref[i, :, j : j + 1] = top + jnp.log(summed)
                part = dot_nt(att_ref[k, i], w[k, :, 3 * hc :])
                if k == 0:
                    out_ref[i] = part
                else:
                    out_ref[i] += part
            for j in range(early):

                @pl.when(i == (j + 1) * ni // early - 1)
                def _(j=j):
                    steps[j]()

            return carry

        lax.fori_loop(0, ni, image, 0)
        for step in steps[early:]:
            step()
        finish(1)
        keep_1.wait()
        kept.wait()

    vmem = pl.BlockSpec(memory_space=pltpu.VMEM)
    anywhere = pl.BlockSpec(memory_space=pl.ANY)
    dma = pltpu.SemaphoreType.DMA
    return pl.pallas_call(
        kernel,
        in_specs=[vmem] * 5 + [anywhere],
        out_specs=[vmem] * 5 + [anywhere] * 2,
        out_shape=[
            jax.ShapeDtypeStruct((ni, PT, D), BF16),
            jax.ShapeDtypeStruct((n_t, ni, PT, 3 * hc), BF16),
            jax.ShapeDtypeStruct((n_t, ni, PT, hc), BF16),
            jax.ShapeDtypeStruct((ni, PT, n_t * hh), F32),
            jax.ShapeDtypeStruct((ni, PT, D), F32),
            jax.ShapeDtypeStruct((n_t, D, f2), BF16),
            jax.ShapeDtypeStruct((2, n_t, D, f2), BF16),
        ],
        scratch_shapes=[
            pltpu.VMEM((n_t, D, f2), BF16),
            dma((2, n_t)),
            dma((2, n_t)),
            dma((2, n_t, n_p)),
            dma((2, n_t, n_p)),
            dma((2,)),
            dma,
        ],
        compiler_params=params(collective_id=0, has_side_effects=True),
        cost_estimate=pl.CostEstimate(
            flops=2 * cfg.m * D * f2 * n_t,
            bytes_accessed=2 * n_t * D * f2 + 12 * cfg.m * D,
            transcendentals=cfg.m * PT * n_t * hh,
        ),
        name="gather_and_attend",
    )(x, gain, shift, query_bias, value_bias, blocks)


def attention_backward(grad_hidden, qkv, attended, lse, weights, cfg):
    n_t, hc, hh = cfg.n_t, cfg.hc, cfg.hh
    scale = HD**-0.5

    def kernel(gh_ref, qkv_ref, att_ref, lse_ref, w_ref, gqkv_ref, out_ref, dq_ref, dv_ref):
        @pl.when(pl.program_id(0) == 0)
        def _():
            dq_ref[...] = jnp.zeros_like(dq_ref)
            dv_ref[...] = jnp.zeros_like(dv_ref)

        keyed = lax.broadcasted_iota(jnp.int32, (PT, PT), 1) < TOK_IMG
        grad_hidden_b = gh_ref[0]
        out = jnp.zeros((PT, D), F32)
        for k in range(n_t):
            w = w_ref[k]
            grad_att = dot(grad_hidden_b, w[:, 3 * hc :]).astype(BF16)
            for h in range(hh):
                cols = slice(h * HD, (h + 1) * HD)
                key_cols = slice(hc + h * HD, hc + (h + 1) * HD)
                value_cols = slice(2 * hc + h * HD, 2 * hc + (h + 1) * HD)
                query = qkv_ref[k, 0, :, cols]
                keys = qkv_ref[k, 0, :, key_cols]
                values = qkv_ref[k, 0, :, value_cols]
                grad = grad_att[:, cols]
                j = k * hh + h
                scores = dot_nt(query, keys) * scale - lse_ref[0, :, j : j + 1]
                probs = jnp.exp(jnp.where(keyed, scores, NEG))
                delta = jnp.sum(
                    grad.astype(F32) * att_ref[k, 0, :, cols].astype(F32), axis=-1, keepdims=True
                )
                grad_v = dot_tn(probs.astype(BF16), grad)
                grad_s = (probs * (dot_nt(grad, values) - delta) * scale).astype(BF16)
                grad_q = dot(grad_s, keys)
                grad_k = dot_tn(grad_s, query)
                dq_ref[k : k + 1, cols] += jnp.sum(grad_q, axis=0, keepdims=True)
                dv_ref[k : k + 1, cols] += jnp.sum(grad_v, axis=0, keepdims=True)
                gqkv_ref[k, 0, :, cols] = grad_q.astype(BF16)
                gqkv_ref[k, 0, :, key_cols] = grad_k.astype(BF16)
                gqkv_ref[k, 0, :, value_cols] = grad_v.astype(BF16)
            out = out + dot_nt(gqkv_ref[k, 0], w[:, : 3 * hc])
        out_ref[0] = out

    return pl.pallas_call(
        kernel,
        grid=(cfg.ni,),
        in_specs=[
            image_spec(D),
            chunk_image_spec(n_t, 3 * hc),
            chunk_image_spec(n_t, hc),
            image_spec(n_t * hh),
            fixed((n_t, D, cfg.f2)),
        ],
        out_specs=[
            chunk_image_spec(n_t, 3 * hc),
            image_spec(D),
            row_spec(n_t, hc),
            row_spec(n_t, hc),
        ],
        out_shape=[
            jax.ShapeDtypeStruct((n_t, cfg.ni, PT, 3 * hc), BF16),
            jax.ShapeDtypeStruct((cfg.ni, PT, D), F32),
            jax.ShapeDtypeStruct((n_t, hc), F32),
            jax.ShapeDtypeStruct((n_t, hc), F32),
        ],
        compiler_params=params(),
        cost_estimate=pl.CostEstimate(
            flops=2 * cfg.m * D * cfg.f2 * n_t + 10 * cfg.m * PT * HD * n_t * hh,
            bytes_accessed=2 * n_t * D * cfg.f2 + 12 * cfg.m * D,
            transcendentals=cfg.m * PT * n_t * hh,
        ),
        name="attention_backward",
    )(grad_hidden, qkv, attended, lse, weights)


def attention_weights(attn_in_t, grad_t, gqkv, attended, cfg):
    hc, n_p, n_t = cfg.hc, cfg.n_p, cfg.n_t

    def kernel(in_ref, gt_ref, gqkv_ref, att_ref, out_ref):
        left = dot(in_ref[...], gqkv_ref[0]).astype(BF16)
        right = dot(gt_ref[...], att_ref[0]).astype(BF16)
        out_ref[:, 0, :, : 3 * hc] = left.reshape(n_p, 2 * cfg.pd, 3 * hc)
        out_ref[:, 0, :, 3 * hc :] = right.reshape(n_p, 2 * cfg.pd, hc)

    return pl.pallas_call(
        kernel,
        grid=(n_t,),
        in_specs=[
            fixed((D, cfg.m)),
            fixed((D, cfg.m)),
            pl.BlockSpec((1, cfg.m, 3 * hc), lambda i: (i, 0, 0)),
            pl.BlockSpec((1, cfg.m, hc), lambda i: (i, 0, 0)),
        ],
        out_specs=pl.BlockSpec((n_p, 1, 2 * cfg.pd, cfg.f2), lambda i: (0, i, 0, 0)),
        out_shape=jax.ShapeDtypeStruct((n_p, n_t, 2 * cfg.pd, cfg.f2), BF16),
        compiler_params=params(),
        cost_estimate=pl.CostEstimate(
            flops=2 * cfg.m * D * cfg.f2 * n_t,
            bytes_accessed=4 * cfg.m * D + 2 * D * cfg.f2 * n_t,
            transcendentals=0,
        ),
        name="attention_weights",
    )(
        attn_in_t,
        grad_t,
        gqkv.reshape(n_t, cfg.m, 3 * hc),
        attended.reshape(n_t, cfg.m, hc),
    )


def mlp_pass(scalars, mlp_in, cot, mlp_in_t, cot_t, fc1, weights, cfg):
    n_p, n_t, m, pd, w = cfg.n_p, cfg.n_t, cfg.m, cfg.pd, cfg.f2

    def kernel(
        s, in_ref, cot_ref, in_t_ref, cot_t_ref, fc1_ref, w1_ref, w2_ref,
        act_ref, sum_ref, grad_ref, back_ref, gpre_all,
    ):
        step = pl.program_id(0)
        w1, w2 = w1_ref[0, 0], w2_ref[0, 0]
        total = jnp.zeros((1, w), F32)
        for i in range(cfg.ni):
            rows = slice(i * PT, (i + 1) * PT)
            pre = dot(in_ref[rows, :], w1) + fc1_ref[pl.ds(2 * step + s[0], 1), :]
            phi = 0.5 * (1.0 + lax.erf(pre * (1.0 / math.sqrt(2.0))))
            act_ref[0, rows, :] = (pre * phi).astype(BF16)
            slope = phi + pre * jnp.exp(-0.5 * pre * pre) * (1.0 / math.sqrt(2.0 * math.pi))
            gpre = dot(cot_ref[rows, :], w2) * slope
            total = total + jnp.sum(gpre, axis=0, keepdims=True)
            gpre_all[rows, :] = gpre.astype(BF16)
        sum_ref[0] = total
        grad_ref[:, 0, 0] = dot(in_t_ref[...], gpre_all[...]).astype(BF16).reshape(n_p, 2 * pd, w)
        grad_ref[:, 0, 1] = dot(cot_t_ref[...], act_ref[0]).astype(BF16).reshape(n_p, 2 * pd, w)
        back = dot_nt(gpre_all[...], w1)

        @pl.when(step == 0)
        def _():
            back_ref[...] = back

        @pl.when(step > 0)
        def _():
            back_ref[...] += back

    def half_spec(unit):
        return pl.BlockSpec((1, 1, D, w), lambda i, s: (unit, i, 0, 0))

    full = fixed((m, D))
    return pl.pallas_call(
        kernel,
        grid_spec=pltpu.PrefetchScalarGridSpec(
            num_scalar_prefetch=1,
            grid=(n_t,),
            in_specs=[full, full, fixed((D, m)), fixed((D, m)), row_spec(2 * n_t, w)]
            + [half_spec(0), half_spec(1)],
            out_specs=[
                pl.BlockSpec((1, m, w), lambda i, s: (i, 0, 0)),
                pl.BlockSpec((1, 1, w), lambda i, s: (i, 0, 0)),
                pl.BlockSpec((n_p, 1, 2, 2 * pd, w), lambda i, s: (0, i, 0, 0, 0)),
                pl.BlockSpec((m, D), lambda i, s: (0, 0)),
            ],
            scratch_shapes=[pltpu.VMEM((m, w), BF16)],
        ),
        out_shape=[
            jax.ShapeDtypeStruct((n_t, m, w), BF16),
            jax.ShapeDtypeStruct((n_t, 1, w), F32),
            jax.ShapeDtypeStruct((n_p, n_t, 2, 2 * pd, w), BF16),
            jax.ShapeDtypeStruct((m, D), F32),
        ],
        compiler_params=params(),
        cost_estimate=pl.CostEstimate(
            flops=10 * m * D * w * n_t,
            bytes_accessed=12 * m * D + 8 * D * w * n_t + 2 * m * w * n_t,
            transcendentals=2 * m * w * n_t,
        ),
        name="mlp_pass",
    )(scalars, mlp_in, cot, mlp_in_t, cot_t, fc1, weights, weights)


def mlp_output(act, weights, cfg):
    n_t, m, f2 = cfg.n_t, cfg.m, cfg.f2

    def kernel(act_ref, w_ref, out_ref):
        total = dot_nt(act_ref[0], w_ref[0, 0])

        @pl.when(pl.program_id(0) == 0)
        def _():
            out_ref[...] = total

        @pl.when(pl.program_id(0) > 0)
        def _():
            out_ref[...] += total

    return pl.pallas_call(
        kernel,
        grid=(n_t,),
        in_specs=[
            pl.BlockSpec((1, m, f2), lambda i: (i, 0, 0)),
            pl.BlockSpec((1, 1, D, f2), lambda i: (1, i, 0, 0)),
        ],
        out_specs=pl.BlockSpec((m, D), lambda i: (0, 0)),
        out_shape=jax.ShapeDtypeStruct((m, D), F32),
        compiler_params=params(),
        cost_estimate=pl.CostEstimate(
            flops=2 * m * D * f2 * n_t,
            bytes_accessed=4 * m * D + 2 * D * f2 * n_t,
            transcendentals=0,
        ),
        name="mlp_output",
    )(act, weights)


def second_norm(x, part, other, shift_o, gain, shift, cfg):
    def kernel(x_ref, part_ref, other_ref, so_ref, gain_ref, shift_ref, hidden_ref, in_ref):
        hidden = x_ref[0].astype(F32) + (part_ref[0] + other_ref[0]) + so_ref[...]
        hidden_ref[0] = hidden
        normed, _ = norm(hidden)
        in_ref[0] = (normed * gain_ref[...] + shift_ref[...]).astype(BF16)

    return pl.pallas_call(
        kernel,
        grid=(cfg.imgs,),
        in_specs=[image_spec(D)] * 3 + [row_spec()] * 3,
        out_specs=[image_spec(D)] * 2,
        out_shape=[
            jax.ShapeDtypeStruct((cfg.imgs, PT, D), F32),
            jax.ShapeDtypeStruct((cfg.imgs, PT, D), BF16),
        ],
        compiler_params=params(),
        cost_estimate=pl.CostEstimate(
            flops=0, bytes_accessed=16 * cfg.imgs * PT * D, transcendentals=0
        ),
        name="second_norm",
    )(x, part, other, shift_o, gain, shift)


def second_norm_back(part, other, hidden, cot, gain, cfg):
    def kernel(part_ref, other_ref, hidden_ref, cot_ref, gain_ref, grad_ref, gradb_ref, sum_ref):
        @pl.when(pl.program_id(0) == 0)
        def _():
            sum_ref[...] = jnp.zeros_like(sum_ref)

        up = part_ref[0] + other_ref[0]
        normed, inverse = norm(hidden_ref[0])
        cot_f = cot_ref[0].astype(F32)
        grad = cot_f + norm_back(up, normed, inverse, gain_ref[...])
        grad_ref[0] = grad
        gradb_ref[0] = grad.astype(BF16)
        sum_ref[0:1, :] += jnp.sum(up * normed, axis=0, keepdims=True)
        sum_ref[1:2, :] += jnp.sum(up, axis=0, keepdims=True)
        sum_ref[2:3, :] += jnp.sum(grad, axis=0, keepdims=True)
        sum_ref[3:4, :] += jnp.sum(cot_f, axis=0, keepdims=True)

    return pl.pallas_call(
        kernel,
        grid=(cfg.imgs,),
        in_specs=[image_spec(D)] * 4 + [row_spec()],
        out_specs=[image_spec(D), image_spec(D), row_spec(4)],
        out_shape=[
            jax.ShapeDtypeStruct((cfg.imgs, PT, D), F32),
            jax.ShapeDtypeStruct((cfg.imgs, PT, D), BF16),
            jax.ShapeDtypeStruct((4, D), F32),
        ],
        compiler_params=params(),
        cost_estimate=pl.CostEstimate(
            flops=0, bytes_accessed=20 * cfg.imgs * PT * D, transcendentals=0
        ),
        name="second_norm_back",
    )(part, other, hidden, cot, gain)


def first_norm_back(part, other, x, grad_hidden, gain, cfg):
    def kernel(part_ref, other_ref, x_ref, grad_ref, gain_ref, out_ref, sum_ref):
        @pl.when(pl.program_id(0) == 0)
        def _():
            sum_ref[...] = jnp.zeros_like(sum_ref)

        up = part_ref[0] + other_ref[0]
        normed, inverse = norm(x_ref[0].astype(F32))
        grad = grad_ref[0] + norm_back(up, normed, inverse, gain_ref[...])
        out_ref[0] = grad.astype(BF16)
        sum_ref[0:1, :] += jnp.sum(up * normed, axis=0, keepdims=True)
        sum_ref[1:2, :] += jnp.sum(up, axis=0, keepdims=True)

    return pl.pallas_call(
        kernel,
        grid=(cfg.imgs,),
        in_specs=[image_spec(D)] * 4 + [row_spec()],
        out_specs=[image_spec(D), row_spec(2)],
        out_shape=[
            jax.ShapeDtypeStruct((cfg.imgs, PT, D), BF16),
            jax.ShapeDtypeStruct((2, D), F32),
        ],
        compiler_params=params(),
        cost_estimate=pl.CostEstimate(
            flops=0, bytes_accessed=16 * cfg.imgs * PT * D, transcendentals=0
        ),
        name="first_norm_back",
    )(part, other, x, grad_hidden, gain)


def body(cfg, tokens, counts, gains, biases, fc1_bias, w_qkv, w_o, w_1, w_2, cotangent):
    n_t, n_p, pd, f2, hc, imgs, m = cfg.n_t, cfg.n_p, cfg.pd, cfg.f2, cfg.hc, cfg.imgs, cfg.m
    where = {axis: lax.axis_index(axis) for axis in ALL}
    core, z = where["c"], where["t"]
    scalars = core[None].astype(jnp.int32)
    ends = jnp.cumsum(counts[0]).astype(jnp.int32)
    starts = ends - counts[0]
    first_core = core == 0

    def traded(halves):
        mine = jnp.where(first_core, halves[0], halves[1])
        theirs = swap_core(jnp.where(first_core, halves[1], halves[0]))
        rows = jnp.where(
            first_core, jnp.stack([mine, theirs], axis=-3), jnp.stack([theirs, mine], axis=-3)
        )
        return rows.reshape(rows.shape[:-3] + (2 * pd, rows.shape[-1]))

    blocks = traded(
        jnp.stack(
            [
                jnp.concatenate(
                    [
                        w_qkv.reshape(pd, 3, 2, hc).transpose(2, 0, 1, 3).reshape(2, pd, 3 * hc),
                        w_o.T.reshape(pd, 2, hc).transpose(1, 0, 2),
                    ],
                    axis=2,
                ),
                w_1.reshape(pd, 2, f2).transpose(1, 0, 2),
                w_2.T.reshape(pd, 2, f2).transpose(1, 0, 2),
            ],
            axis=1,
        )
    )

    def paired(value):
        return jnp.concatenate([value, swap_core(value)])

    small = jnp.concatenate([gains, biases, fc1_bias.reshape(4, -1)])
    small = gather_small(small, cfg, where).reshape(cfg.n_dp * n_t, 12, -1)
    rows = small[:, :8].transpose(1, 0, 2).reshape(8, D)
    gain_all, shift_all = rows[:2], rows[2:]
    fc1_all = small[:, 8:].reshape(2 * n_t, f2)

    x_own = to_images(tokens, starts, ends, z, cfg).reshape(imgs, PT, D)
    x = paired(x_own)
    cot_own = to_images(cotangent, starts, ends, z, cfg).reshape(imgs, PT, D)
    cot = paired(cot_own).reshape(m, D)
    cot_t = cot.T

    attn_in, qkv, attended, lse, attn_out, attn_w, mlp_w = gather_and_attend(
        x,
        gain_all[0:1],
        shift_all[0:1],
        shift_all[2].reshape(2 * n_t, hc),
        shift_all[3].reshape(2 * n_t, hc),
        blocks,
        cfg,
    )
    hidden, mlp_in_own = second_norm(
        x_own,
        attn_out[:imgs],
        swap_core(attn_out[imgs:]),
        shift_all[4:5],
        gain_all[1:2],
        shift_all[1:2],
        cfg,
    )
    mlp_in = paired(mlp_in_own).reshape(m, D)
    mlp_in_t = mlp_in.T

    act, fc1_sums, mlp_grads, back = mlp_pass(
        scalars, mlp_in, cot, mlp_in_t, cot_t, fc1_all, mlp_w, cfg
    )
    mlp_grads = scatter_chips(mlp_grads.reshape(n_p * n_t, 2, 2 * pd, f2))

    back = back.reshape(2, imgs, PT, D)
    grad_hidden, grad_hidden_b, sums_2 = second_norm_back(
        back[0], swap_core(back[1]), hidden, cot_own, gain_all[1:2], cfg
    )
    grad_hidden_b = paired(grad_hidden_b)
    gqkv, grad_in, dq, dv = attention_backward(
        grad_hidden_b, qkv, attended, lse, attn_w, cfg
    )
    d_images, sums_1 = first_norm_back(
        grad_in[:imgs], swap_core(grad_in[imgs:]), x_own, grad_hidden, gain_all[0:1], cfg
    )
    attn_grads = attention_weights(
        attn_in.reshape(m, D).T, grad_hidden_b.reshape(m, D).T, gqkv, attended, cfg
    )
    attn_grads = scatter_chips(attn_grads.reshape(n_p * n_t, 2 * pd, f2))

    out = mlp_output(act, mlp_w, cfg).reshape(2, imgs, PT, D)
    mixed_own = (hidden + (out[0] + swap_core(out[1])) + shift_all[5]).astype(BF16)
    mixed = to_blocks(mixed_own.reshape(imgs * PT, D), starts, ends, z, cfg)
    d_tokens = to_blocks(d_images.reshape(imgs * PT, D), starts, ends, z, cfg)

    def untraded(rows):
        rows = rows.reshape(rows.shape[:-2] + (2, pd, rows.shape[-1]))
        mine = jnp.where(first_core, rows[..., 0, :, :], rows[..., 1, :, :])
        theirs = swap_core(jnp.where(first_core, rows[..., 1, :, :], rows[..., 0, :, :]))
        return (
            jnp.where(first_core, mine, theirs).astype(F32),
            jnp.where(first_core, theirs, mine).astype(F32),
        )

    half_0, half_1 = untraded(attn_grads)
    d_qkv = jnp.stack(
        [half_0[:, : 3 * hc].reshape(pd, 3, hc), half_1[:, : 3 * hc].reshape(pd, 3, hc)], axis=2
    ).reshape(pd, 3, 2 * hc)
    d_o = jnp.concatenate([half_0[:, 3 * hc :], half_1[:, 3 * hc :]], axis=1).T
    both = jnp.concatenate(untraded(mlp_grads), axis=-1)
    d_1, d_2 = both[0], both[1].T

    def placed(chunks):
        on_core = (jnp.arange(2) == core)[None, :, None]
        return jnp.where(on_core, chunks[:, None, :], 0.0)

    vectors = jnp.stack(
        [
            sums_1[0],
            sums_2[0],
            sums_1[1],
            sums_2[1],
            placed(dq).reshape(D),
            placed(dv).reshape(D),
            sums_2[2],
            sums_2[3],
        ]
    )
    vectors = vectors.reshape(8, n_p, 2, n_t, -1).transpose(1, 2, 3, 0, 4)
    fc1_terms = placed(fc1_sums[:, 0]).reshape(n_p, 2, n_t, 4, -1)
    small = scatter_small(jnp.concatenate([vectors, fc1_terms], axis=3), cfg, where)
    return (
        mixed,
        d_tokens,
        d_qkv,
        d_o,
        d_1,
        d_2,
        small[:2],
        small[2:8],
        small[8:].reshape(-1),
    )


def solution(mesh):
    n_dp, n_t = mesh.shape["dp"], mesh.shape["tensor"]
    split = Mesh(mesh.devices.reshape(n_dp // 2, 2, n_t), ALL)

    def program(tokens, *rest):
        cfg = Cfg(n_dp, n_t, tokens.shape[0])
        return body(cfg, tokens, *rest)

    dp = ("p", "c")
    return jax.shard_map(
        program,
        mesh=split,
        in_specs=(
            P(ALL, None),
            P(dp, None),
            P(None, ALL),
            P(None, ALL),
            P(ALL),
            P(dp, None, "t"),
            P("t", dp),
            P(dp, "t"),
            P("t", dp),
            P(ALL, None),
        ),
        out_specs=(
            P(ALL, None),
            P(ALL, None),
            P(dp, None, "t"),
            P("t", dp),
            P(dp, "t"),
            P("t", dp),
            P(None, ALL),
            P(None, ALL),
            P(ALL),
        ),
        check_vma=False,
    )
```

time: 846 us -> 977 us (1.15)
  waiting for transfers between devices: 284 us -> 391 us
  Pallas kernels: 244 us -> 338 us
  starting transfers between devices: 115 us -> 74.2 us
  other arithmetic: 59.5 us -> 29.8 us
  between operations: 8.04 us -> 20.6 us
    reduce_scatter x0 -> x2, waiting for transfers between devices: none -> 316 us  [scatter_chips(): return lax.psum_scatter(value, CHIPS, scatter_dimension=0, tiled=False)]
    ppermute x88 -> x29, waiting for transfers between devices: 284 us -> 74.4 us  [the longest x8 29 us: step_tensor(): return lax.ppermute(value, 't', pairs)]
    pallas_call x15 -> x8, Pallas kernels: 244 us -> 338 us  [the longest x1 192 us: gather_and_attend(): pl.pallas_call(kernel, in_specs=[vmem] * 5 + [anywhere], out_specs=[vmem]...]
    ppermute x88 -> x29, starting transfers between devices: 115 us -> 74.2 us  [the longest x8 56.4 us: step_tensor(): return lax.ppermute(value, 't', pairs)]
    another operation x21 -> x2, other arithmetic: 16.4 us -> 0.89 us  [the longest x9 9 us: body(): mlp_part = turn_tensor(jnp.stack(mlp_grads[k]).astype(BF16), -k, cfg)]
    convert_element_type x16 -> x2, other arithmetic: 16.6 us -> 3.58 us  [the longest x1 3.4 us: body(): (hidden + (out[0] + swap_core(out[1])) + shift_all[5]).astype(BF16)]
    squeeze x17 -> x0, local copies, waits for them, and re-layouts: 10.4 us -> none  [the longest x6 4.83 us: gather_pair(): diag_a = swap_dp(from_x[0], 4, cfg)]
    reshape x7 -> x6, local copies, waits for them, and re-layouts: 21.2 us -> 26.4 us  [the longest x1 10.4 us: body(): attn_grads = scatter_chips(attn_grads.reshape(n_p * n_t, 2 * pd, f2))]
  transfers between devices with their start and end apart: 88 -> 31, of which waited for: 29 -> 13; matrix products, arithmetic and copies ran while one was open for 21% -> 10% of each run, Pallas kernels for 29% -> 3%
where the time goes in v2:
time: 977 us; the launch traced here: 969 us
  waiting for transfers between devices  391 us (40%)
  Pallas kernels  338 us (35%)
  local copies, waits for them, and re-layouts  83.1 us (9%)
  starting transfers between devices  74.2 us (8%)
  matrix products  32 us (3%)
  other arithmetic  29.8 us (3%)
  between operations  20.6 us (2%)
    reduce_scatter x2, waiting for transfers between devices, scatter_chips(): return lax.psum_scatter(value, CHIPS, scatter_dimension=0, tiled=False)  316 us
    pallas_call x1, Pallas kernels, gather_and_attend(): pl.pallas_call(kernel, in_specs=[vmem] * 5 + [anywhere], out_specs=[vmem]...  192 us
    pallas_call x1, Pallas kernels, mlp_pass(): pl.pallas_call(kernel, grid_spec=pltpu.PrefetchScalarGridSpec(num_scalar_...  58.1 us
    ppermute x8, starting transfers between devices, step_tensor(): return lax.ppermute(value, 't', pairs)  56.4 us
    pallas_call x1, Pallas kernels, attention_backward(): pl.pallas_call(kernel, grid=(cfg.ni,), in_specs=[image_spec(D), chunk_ima...  38.6 us
    dot_general x16, matrix products, dot(): lax.dot_general(a, b, (((1,), (0,)), ((), ())), preferred_element_type=F32)  32 us
    ppermute x8, waiting for transfers between devices, step_tensor(): return lax.ppermute(value, 't', pairs)  29 us
    ppermute x5, waiting for transfers between devices, scatter_small(): value = keep + lax.ppermute(send, axis, [(i, i ^ bit) for i in range(size)])  22.9 us
  transfers between devices with their start and end apart: 31, of which 13 were waited for; matrix products, arithmetic and copies ran while one was open for 10% of the time, Pallas kernels for 3%

profile of v2, /device:TPU:0, one launch (start us, length us, event | category | flops | bytes accessed | tf_op | source)
XLA Modules:
  0.0 968.9 jit_solution(1507453013867908795)
XLA Ops:
  10.7 3.5 constant_dynamic-slice_fusion.2
  15.5 6.6 collective-permute-start.1
  24.6 2.5 subtract_select_fusion.2
  27.2 2.8 fusion.6
  31.3 12.9 %collective-permute-done.3 = f32[1,12,40]{2,1,0:T(8,128)S(1)} collective-permute-done((f32[1,12,40]{2,1,0:T(8,128)S(1)}, f32[1,12,40]{2,1,0:T(8,128)S(1)}, u32[]{:S(2)}, u32[]{:S(2)}) %collective-permute-start.3) | collective-permute-done | bytes 1952 | tf_op jit(solution)/shard_map/ppermute | solution.py:106
  44.2 3.8 collective-permute-start.4
  50.0 1.5 pad_maximum_fusion.3
  51.6 1.6 collective-permute-start.6
  53.1 3.1 convolution_add_fusion.6
  56.2 2.2 fusion.3
  58.8 1.5 select_bitcast_fusion.1
  60.2 1.6 copy.115
  62.3 1.6 collective-permute-start.7
  63.8 4.1 collective-permute-done.7
  71.5 1.4 copy.116
  72.9 2.9 maximum_select_fusion
  75.8 2.0 copy.117
  77.9 3.1 pad_maximum_fusion.x_ref
  81.0 192.2 %gather_and_attend.1 = (bf16[4,272,1280]{2,1,0:T(8,128)(2,1)}, bf16[4,4,272,480]{3,2,1,0:T(8,128)(2,1)}, bf16[4,4,272,160]{3,2,1,0:T(8,128)(2,1)}, f32[4,272,8]{...) custom-call(bf16[4,272,1280]{2,1,0:T(8,128)(2,1)} %pad_maximum_fusion.x_re, ...), custom_call_target="tpu_custom_call" | custom-call | flops 7130316800 | bytes 23265280 | tf_op jit(solution)/shard_map/gather_and_attend/pallas_call | solution.py:375
  273.3 5.7 fusion.70
  280.8 34.7 %collective-permute-start.12 = (bf16[416,1280]{1,0:T(8,128)(2,1)S(1)}, bf16[416,1280]{1,0:T(8,128)(2,1)S(1)}, u32[]{:S(2)}, u32[]{:S(2)}) collective-permute-start(bf16[416,1280]{1,0:T(8,128)(2,1)S(1)} %get-tuple-element.103), channel_id=1, source_target_pairs={{0,1},{1,2},{2,3},{4,5},{5,6},{6,7},{8,9},{9,10},{10,11},{12,13},{... | collective-permute-start | bytes 3194888 | tf_op jit(solution)/shard_map/ppermute | solution.py:94
  316.9 20.8 %collective-permute-done.11 = bf16[416,1280]{1,0:T(8,128)(2,1)S(1)} collective-permute-done((bf16[416,1280]{1,0:T(8,128)(2,1)S(1)}, bf16[416,1280]{1,0:T(8,128)(2,1)S(1)}, u32[]{:S(2)}, u32[]{:S(2)}) %collective-permute-start.11) | collective-permute-done | bytes 1064992 | tf_op jit(solution)/shard_map/ppermute | solution.py:94
  342.2 5.0 second_norm.1
  349.2 2.0 pad_maximum_fusion.2
  351.2 3.7 copy.119
  354.9 2.0 pad_maximum_fusion.1
  356.9 3.6 copy.118
  360.6 58.1 %mlp_pass.1 = (bf16[4,1088,640]{2,1,0:T(8,128)(2,1)}, f32[4,1,640]{2,1,0:T(1,128)}, bf16[4,4,2,320,640]{4,3,2,1,0:T(8,128)(2,1)}, f32[1088,1280]{1,0:T(8,128)}) custom-call(s32[1]{0:T(128)} %bitcast.30.s, bf16[1088,1280]{1,0:T(8,128)(2,1)} %bitcast.173, bf16[1088,1280]{1,0:T(8,128)(2,1)} %bitcast.171, bf16[1280,1088]{1,0:T(8,128)(2,1)} %bitcast.185, ...), custom_call_target="tpu_custom_call" | custom-call | flops 35651584000 | bytes 48496640 | tf_op jit(solution)/shard_map/mlp_pass/pallas_call | solution.py:552
  418.7 4.5 fusion.68
  423.4 5.0 collective-permute-done.17.other_ref
  428.4 1.5 copy-done.8
  429.9 6.7 second_norm_back.1
  436.8 3.3 copy.120
  440.2 1.4 constant_dynamic-update-slice_fusion.1
  441.6 1.4 constant_dynamic-update-slice_fusion.gh_ref
  443.1 3.6 copy.121
  446.7 38.6 %attention_backward.1 = (bf16[4,4,272,480]{3,2,1,0:T(8,128)(2,1)}, f32[4,272,1280]{2,1,0:T(8,128)}, f32[4,160]{1,0:T(4,128)}, f32[4,160]{1,0:T(4,128)}) custom-call(bf16[4,272,1280]{2,1,0:T(8,128)(2,1)} %copy-done.4, bf16[4,4,272,480]{3,2,1,0:T(8,128)(2,1)} %get-tuple-element.38.qkv_ref, bf16[4,4,272,160]{3,2,1,0:T(8,128)(2,1)} %get-tuple-element.39.att_ref, ...), custom_call_target="tpu_custom_call" | custom-call | flops 9024307200 | bytes 23265280 | tf_op jit(solution)/shard_map/attention_backward/pallas_call | solution.py:449
  485.2 15.7 %attention_weights.1 = bf16[4,4,320,640]{3,2,1,0:T(8,128)(2,1)} custom-call(bf16[1280,1088]{1,0:T(8,128)(2,1)} %bitcast.182, bf16[1280,1088]{1,0:T(8,128)(2,1)} %bitcast.184, bf16[4,1088,480]{2,1,0:T(8,128)(2,1)} %bitcast.214, bf16[4,1088,160]{2,1,0:T(8,128)(2,1)} %bitcast.215), custom_call_target="tpu_custom_call" | custom-call | flops 7130316800 | bytes 12124160 | tf_op jit(solution)/shard_map/attention_weights/pallas_call | solution.py:490
  500.9 10.4 %copy.122 = bf16[16,320,640]{1,2,0:T(8,128)(2,1)} copy(bf16[16,320,640]{2,1,0:T(8,128)(2,1)} %bitcast.174) | data formatting | bytes 13107200 | tf_op jit(solution)/shard_map/reshape | solution.py:794
  512.1 15.8 %mlp_output.1 = f32[1088,1280]{1,0:T(8,128)} custom-call(bf16[4,1088,640]{2,1,0:T(8,128)(2,1)} %get-tuple-element.35.act_ref, bf16[2,4,1280,640]{3,2,1,0:T(8,128)(2,1)} %get-tuple-element.34.w1_ref.w2_ref.w_ref), custom_call_target="tpu_custom_call" | custom-call | flops 7130316800 | bytes 12124160 | tf_op jit(solution)/shard_map/mlp_output/pallas_call | solution.py:597
  527.8 5.5 fusion.69
  533.7 6.0 fusion.67
  546.2 1.9 subtract_select_fusion
  548.5 3.4 add_convert_fusion
  551.9 2.1 convolution_convert_fusion.3
  554.0 5.2 collective-permute-start.15
  560.7 3.0 fusion.7
  564.6 5.8 first_norm_back.1
  573.6 2.5 collective-permute-start.24
  576.1 2.4 convolution_convert_fusion.2
  578.6 1.5 collective-permute-start.16
  580.9 1.9 collective-permute-start.25
  582.8 8.1 collective-permute-done.15
  590.8 2.3 convolution_add_fusion.1
  594.5 3.1 collective-permute-start.27
  600.0 4.6 collective-permute-start.20
  604.6 3.1 collective-permute-done.27
  607.8 2.3 fusion.2
  610.2 19.0 %collective-permute-done.28 = f32[1,12,40]{2,1,0:T(8,128)S(1)} collective-permute-done((f32[1,12,40]{2,1,0:T(8,128)S(1)}, f32[1,12,40]{2,1,0:T(8,128)S(1)}, u32[]{:S(2)}, u32[]{:S(2)}) %collective-permute-start.28) | collective-permute-done | bytes 1952 | tf_op jit(solution)/shard_map/ppermute | solution.py:121
  631.0 2.3 fusion.8
  634.6 2.8 fusion.1
  637.5 39.0 %reduce-scatter.3.cloned.1.call-done = bf16[1,320,640]{1,2,0:T(8,128)(2,1)} async-done(((bf16[16,320,640]{1,2,0:T(8,128)(2,1)}), bf16[1,320,640]{1,2,0:T(8,128)(2,1)}) %reduce-scatter.3.cloned.1.call-update) | async-done | bytes 409616 | tf_op jit(solution)/shard_map/reduce_scatter | solution.py:98
  677.9 277.1 %reduce-scatter.5.cloned.1.call-done = bf16[1,2,320,640]{3,2,1,0:T(8,128)(2,1)} async-done(((bf16[16,2,320,640]{3,2,1,0:T(8,128)(2,1)}), bf16[1,2,320,640]{3,2,1,0:T(8,128)(2,1)}) %reduce-scatter.5.cloned.1.call-update) | async-done | bytes 819216 | tf_op jit(solution)/shard_map/reduce_scatter | solution.py:98
  957.5 1.7 reshape.408
  (214 shorter events, 47.0 us)
Async XLA Ops:
  7.2 669.3 %reduce-scatter.3.cloned.1.call-start = ((), (), s32[]{:S(2)}) async-start(), calls=%async_computation.2 | async-start | bytes 8355840 | tf_op jit(solution)/shard_map/reduce_scatter | solution.py:98
  8.1 16.5 %copy-start.37 = (s32[4,1]{0,1:T(1,128)}, s32[4,1]{0,1:T(1,128)S(1)}, u32[]{:S(2)}) copy-start(s32[4,1]{0,1:T(1,128)S(1)} %reduce-window.4) | copy-start | bytes 52
  10.6 11.4 %copy-start.36 = (f32[160]{0:T(256)S(1)}, f32[160]{0:T(256)}, u32[]{:S(2)}) copy-start(f32[160]{0:T(256)} %param.14) | copy-start | bytes 1924
  10.6 11.5 %copy-start.23 = (f32[6,40]{1,0:T(8,128)S(1)}, f32[6,40]{1,0:T(8,128)}, u32[]{:S(2)}) copy-start(f32[6,40]{1,0:T(8,128)} %param.13) | copy-start | bytes 2884
  10.6 11.5 %copy-start.32 = (f32[2,40]{1,0:T(2,128)S(1)}, f32[2,40]{1,0:T(2,128)}, u32[]{:S(2)}) copy-start(f32[2,40]{1,0:T(2,128)} %param.12) | copy-start | bytes 964
  10.7 16.5 %copy-start.10 = (bf16[648,1280]{1,0:T(8,128)(2,1)S(1)}, bf16[648,1280]{1,0:T(8,128)(2,1)}, u32[]{:S(2)}) copy-start(bf16[648,1280]{1,0:T(8,128)(2,1)} %param.10) | copy-start | bytes 4976644
  14.2 39.0 %collective-permute-start = (bf16[416,1280]{1,0:T(8,128)(2,1)}, bf16[416,1280]{1,0:T(8,128)(2,1)}, u32[]{:S(2)}, u32[]{:S(2)}) collective-permute-start(bf16[416,1280]{1,0:T(8,128)(2,1)} %get-tuple-element.106), channel_id=1, source_target_pairs={{1,0},{2,1},{3,2},{5,4},{6,5},{7,6},{9,8},{10,9},{11,10},{13,12},{... | collective-permute-start | bytes 3194888 | tf_op jit(solution)/shard_map/ppermute | solution.py:94
  15.5 40.8 %collective-permute-start.1 = (bf16[416,1280]{1,0:T(8,128)(2,1)}, bf16[416,1280]{1,0:T(8,128)(2,1)}, u32[]{:S(2)}, u32[]{:S(2)}) collective-permute-start(bf16[416,1280]{1,0:T(8,128)(2,1)} %get-tuple-element.105), channel_id=1, source_target_pairs={{0,1},{1,2},{2,3},{4,5},{5,6},{6,7},{8,9},{9,10},{10,11},{12,13},{... | collective-permute-start | bytes 3194888 | tf_op jit(solution)/shard_map/ppermute | solution.py:94
  22.1 22.1 %collective-permute-start.3 = (f32[1,12,40]{2,1,0:T(8,128)S(1)}, f32[1,12,40]{2,1,0:T(8,128)S(1)}, u32[]{:S(2)}, u32[]{:S(2)}) collective-permute-start(f32[1,12,40]{2,1,0:T(8,128)S(1)} %maximum_bitcast_fusion.4), channel_id=1, source_target_pairs={{0,1},{1,0},{2,3},{3,2},{4,5},{5,4},{6,7},{7,6},{8,9},{9,8},{10,11... | collective-permute-start | bytes 5768 | tf_op jit(solution)/shard_map/ppermute | solution.py:106
  27.2 2.9 copy-start.30
  27.2 3.0 copy-start.18
  30.2 17.9 %copy-start.16 = (bf16[1280,160]{0,1:T(8,128)(2,1)S(1)}, bf16[1280,160]{0,1:T(8,128)(2,1)}, u32[]{:S(2)}) copy-start(bf16[1280,160]{0,1:T(8,128)(2,1)} %param.18) | copy-start | bytes 1228804
  30.4 18.0 %copy-start.17 = (bf16[160,1280]{1,0:T(8,128)(2,1)S(1)}, bf16[160,1280]{1,0:T(8,128)(2,1)}, u32[]{:S(2)}) copy-start(bf16[160,1280]{1,0:T(8,128)(2,1)} %param.17) | copy-start | bytes 1228804
  44.2 5.6 collective-permute-start.4
  49.9 1.6 collective-permute-start.5
  50.0 3.2 copy-start.20
  51.6 10.6 %collective-permute-start.6 = (f32[1,2,4,12,40]{4,3,2,1,0:T(8,128)S(1)}, f32[1,2,4,12,40]{4,3,2,1,0:T(8,128)S(1)}, u32[]{:S(2)}, u32[]{:S(2)}) collective-permute-start(f32[1,2,4,12,40]{4,3,2,1,0:T(8,128)S(1)} %maximum_bitcast_fusion.2), channel_id=1, source_target_pairs={{0,8},{8,0},{16,24},{24,16},{1,9},{9,1},{17,25},{25,17},{2,10},{10... | collective-permute-start | bytes 46088 | tf_op jit(solution)/shard_map/ppermute | solution.py:106
  53.1 3.1 copy-start.28
  58.5 19.4 %copy-start = (bf16[544,1280]{1,0:T(8,128)(2,1)}, bf16[544,1280]{1,0:T(8,128)(2,1)S(1)}, u32[]{:S(2)}) copy-start(bf16[544,1280]{1,0:T(8,128)(2,1)S(1)} %fusion.3) | copy-start | bytes 4177924
  58.5 19.4 %collective-permute-start.2 = (bf16[2,272,1280]{2,1,0:T(8,128)(2,1)S(1)}, bf16[2,272,1280]{2,1,0:T(8,128)(2,1)}, u32[]{:S(2)}, u32[]{:S(2)}) collective-permute-start(bf16[2,272,1280]{2,1,0:T(8,128)(2,1)S(1)} %bitcast.164), channel_id=1, source_target_pairs={{0,4},{4,0},{1,5},{5,1},{2,6},{6,2},{3,7},{7,3},{8,12},{12,8},{9,1... | collective-permute-start | bytes 4177928 | tf_op jit(solution)/shard_map/ppermute | solution.py:89
  61.9 9.6 collective-permute-start.8
  62.3 5.7 collective-permute-start.7
  273.3 5.7 copy-start.11
  279.0 36.6 %copy-start.31 = (s32[544]{0:T(1024)S(1)}, s32[544]{0:T(1024)}, u32[]{:S(2)}) copy-start(s32[544]{0:T(1024)} %copy-done.30) | copy-start | bytes 6532
  279.0 63.2 %collective-permute-start.9 = (f32[2,272,1280]{2,1,0:T(8,128)}, f32[2,272,1280]{2,1,0:T(8,128)}, u32[]{:S(2)}, u32[]{:S(2)}) collective-permute-start(f32[2,272,1280]{2,1,0:T(8,128)} %get-tuple-element.99), channel_id=1, source_target_pairs={{0,4},{4,0},{1,5},{5,1},{2,6},{6,2},{3,7},{7,3},{8,12},{12,8},{9,1... | collective-permute-start | bytes 8355848 | tf_op jit(solution)/shard_map/ppermute | solution.py:89
  279.5 58.2 %collective-permute-start.11 = (bf16[416,1280]{1,0:T(8,128)(2,1)S(1)}, bf16[416,1280]{1,0:T(8,128)(2,1)S(1)}, u32[]{:S(2)}, u32[]{:S(2)}) collective-permute-start(bf16[416,1280]{1,0:T(8,128)(2,1)S(1)} %get-tuple-element.104), channel_id=1, source_target_pairs={{1,0},{2,1},{3,2},{5,4},{6,5},{7,6},{9,8},{10,9},{11,10},{13,12},{... | collective-permute-start | bytes 3194888 | tf_op jit(solution)/shard_map/ppermute | solution.py:94
  280.8 56.9 %copy-start.21 = (s32[544]{0:T(1024)S(1)}, s32[544]{0:T(1024)}, u32[]{:S(2)}) copy-start(s32[544]{0:T(1024)} %get-tuple-element.132) | copy-start | bytes 6532
  280.8 58.0 %collective-permute-start.12 = (bf16[416,1280]{1,0:T(8,128)(2,1)S(1)}, bf16[416,1280]{1,0:T(8,128)(2,1)S(1)}, u32[]{:S(2)}, u32[]{:S(2)}) collective-permute-start(bf16[416,1280]{1,0:T(8,128)(2,1)S(1)} %get-tuple-element.103), channel_id=1, source_target_pairs={{0,1},{1,2},{2,3},{4,5},{5,6},{6,7},{8,9},{9,10},{10,11},{12,13},{... | collective-permute-start | bytes 3194888 | tf_op jit(solution)/shard_map/ppermute | solution.py:94
  316.9 22.0 %copy-start.29 = (s32[544]{0:T(1024)S(1)}, s32[544]{0:T(1024)}, u32[]{:S(2)}) copy-start(s32[544]{0:T(1024)} %get-tuple-element.131) | copy-start | bytes 6532
  339.9 7.3 copy-start.5
  339.9 9.3 collective-permute-start.13
  347.2 7.7 collective-permute-start.10
  351.2 3.7 copy-start.2
  356.9 3.7 copy-start.3
  423.2 5.1 collective-permute-start.17
  429.9 6.9 copy-start.9
  436.6 5.0 collective-permute-start.18
  443.1 3.6 copy-start.4
  511.3 443.7 %reduce-scatter.5.cloned.1.call-start = ((), (), s32[]{:S(2)}) async-start(), calls=%async_computation.3 | async-start | bytes 13926400 | tf_op jit(solution)/shard_map/reduce_scatter | solution.py:98
  533.3 15.1 %collective-permute-start.14 = (f32[2,272,1280]{2,1,0:T(8,128)}, f32[2,272,1280]{2,1,0:T(8,128)}, u32[]{:S(2)}, u32[]{:S(2)}) collective-permute-start(f32[2,272,1280]{2,1,0:T(8,128)} %bitcast.37), channel_id=1, source_target_pairs={{0,4},{4,0},{1,5},{5,1},{2,6},{6,2},{3,7},{7,3},{8,12},{12,8},{9,1... | collective-permute-start | bytes 8355848 | tf_op jit(solution)/shard_map/ppermute | solution.py:89
  533.7 6.2 copy-start.38
  533.7 14.5 %copy-start.24 = (f32[4,1,640]{2,1,0:T(1,128)S(1)}, f32[4,1,640]{2,1,0:T(1,128)}, u32[]{:S(2)}) copy-start(f32[4,1,640]{2,1,0:T(1,128)} %get-tuple-element.52) | copy-start | bytes 30724
  533.7 14.8 %copy-start.1 = (f32[2,272,1280]{2,1,0:T(8,128)S(1)}, f32[2,272,1280]{2,1,0:T(8,128)}, u32[]{:S(2)}) copy-start(f32[2,272,1280]{2,1,0:T(8,128)} %get-tuple-element.32.hidden_ref) | copy-start | bytes 8355844
  539.7 24.8 %collective-permute-start.19 = (f32[2,272,1280]{2,1,0:T(8,128)}, f32[2,272,1280]{2,1,0:T(8,128)}, u32[]{:S(2)}, u32[]{:S(2)}) collective-permute-start(f32[2,272,1280]{2,1,0:T(8,128)} %get-tuple-element.93), channel_id=1, source_target_pairs={{0,4},{4,0},{1,5},{5,1},{2,6},{6,2},{3,7},{7,3},{8,12},{12,8},{9,1... | collective-permute-start | bytes 8355848 | tf_op jit(solution)/shard_map/ppermute | solution.py:89
  543.0 8.8 copy-start.33
  551.9 7.2 copy-start.22
  554.0 36.9 %collective-permute-start.15 = (bf16[416,1280]{1,0:T(8,128)(2,1)}, bf16[416,1280]{1,0:T(8,128)(2,1)}, u32[]{:S(2)}, u32[]{:S(2)}) collective-permute-start(bf16[416,1280]{1,0:T(8,128)(2,1)} %convolution_convert_fusion.3), channel_id=1, source_target_pairs={{0,1},{1,2},{2,3},{4,5},{5,6},{6,7},{8,9},{9,10},{10,11},{12,13},{... | collective-permute-start | bytes 3194888 | tf_op jit(solution)/shard_map/ppermute | solution.py:94
  560.7 3.0 copy-start.26
  560.7 3.1 copy-start.25
  573.6 7.2 collective-permute-start.24
  578.6 29.2 %collective-permute-start.16 = (bf16[416,1280]{1,0:T(8,128)(2,1)S(1)}, bf16[416,1280]{1,0:T(8,128)(2,1)S(1)}, u32[]{:S(2)}, u32[]{:S(2)}) collective-permute-start(bf16[416,1280]{1,0:T(8,128)(2,1)S(1)} %convolution_convert_fusion.2), channel_id=1, source_target_pairs={{1,0},{2,1},{3,2},{5,4},{6,5},{7,6},{9,8},{10,9},{11,10},{13,12},{... | collective-permute-start | bytes 3194888 | tf_op jit(solution)/shard_map/ppermute | solution.py:94
  580.9 12.4 %copy-start.12 = (bf16[2,272,1280]{2,1,0:T(8,128)(2,1)S(1)}, bf16[2,272,1280]{2,1,0:T(8,128)(2,1)}, u32[]{:S(2)}) copy-start(bf16[2,272,1280]{2,1,0:T(8,128)(2,1)} %get-tuple-element.44) | copy-start | bytes 4177924
  580.9 12.4 %copy-start.35 = (s32[416]{0:T(512)S(1)}, s32[416]{0:T(512)}, u32[]{:S(2)}) copy-start(s32[416]{0:T(512)} %fusion.56) | copy-start | bytes 4996
  580.9 12.3 %collective-permute-start.25 = (f32[1,2,4,12,40]{4,3,2,1,0:T(8,128)S(1)}, f32[1,2,4,12,40]{4,3,2,1,0:T(8,128)S(1)}, u32[]{:S(2)}, u32[]{:S(2)}) collective-permute-start(f32[1,2,4,12,40]{4,3,2,1,0:T(8,128)S(1)} %slice_select_fusion), channel_id=1, source_target_pairs={{0,8},{8,0},{16,24},{24,16},{1,9},{9,1},{17,25},{25,17},{2,10},{10... | collective-permute-start | bytes 46088 | tf_op jit(solution)/shard_map/ppermute | solution.py:121
  593.2 1.3 collective-permute-start.26
  593.3 4.3 copy-start.34
  594.5 13.3 %copy-start.27 = (s32[648]{0:T(1024)S(1)}, s32[648]{0:T(1024)}, u32[]{:S(2)}) copy-start(s32[648]{0:T(1024)} %subtract_select_fusion) | copy-start | bytes 7780
  594.5 13.2 %collective-permute-start.27 = (f32[2,12,40]{2,1,0:T(8,128)S(1)}, f32[2,12,40]{2,1,0:T(8,128)S(1)}, u32[]{:S(2)}, u32[]{:S(2)}) collective-permute-start(f32[2,12,40]{2,1,0:T(8,128)S(1)} %select_bitcast_fusion.4), channel_id=1, source_target_pairs={{0,2},{1,3},{2,0},{3,1},{4,6},{5,7},{6,4},{7,5},{8,10},{9,11},{10,... | collective-permute-start | bytes 11528 | tf_op jit(solution)/shard_map/ppermute | solution.py:121
  598.7 32.3 %collective-permute-start.21 = (bf16[416,1280]{1,0:T(8,128)(2,1)S(1)}, bf16[416,1280]{1,0:T(8,128)(2,1)}, u32[]{:S(2)}, u32[]{:S(2)}) collective-permute-start(bf16[416,1280]{1,0:T(8,128)(2,1)S(1)} %convolution_convert_fusion), channel_id=1, source_target_pairs={{1,0},{2,1},{3,2},{5,4},{6,5},{7,6},{9,8},{10,9},{11,10},{13,12},{... | collective-permute-start | bytes 3194888 | tf_op jit(solution)/shard_map/ppermute | solution.py:94
  600.0 33.3 %collective-permute-start.20 = (bf16[416,1280]{1,0:T(8,128)(2,1)S(1)}, bf16[416,1280]{1,0:T(8,128)(2,1)S(1)}, u32[]{:S(2)}, u32[]{:S(2)}) collective-permute-start(bf16[416,1280]{1,0:T(8,128)(2,1)S(1)} %convolution_convert_fusion.1), channel_id=1, source_target_pairs={{0,1},{1,2},{2,3},{4,5},{5,6},{6,7},{8,9},{9,10},{10,11},{12,13},{... | collective-permute-start | bytes 3194888 | tf_op jit(solution)/shard_map/ppermute | solution.py:94
  607.7 21.4 %collective-permute-start.28 = (f32[1,12,40]{2,1,0:T(8,128)S(1)}, f32[1,12,40]{2,1,0:T(8,128)S(1)}, u32[]{:S(2)}, u32[]{:S(2)}) collective-permute-start(f32[1,12,40]{2,1,0:T(8,128)S(1)} %slice_select_fusion.1), channel_id=1, source_target_pairs={{0,1},{1,0},{2,3},{3,2},{4,5},{5,4},{6,7},{7,6},{8,9},{9,8},{10,11... | collective-permute-start | bytes 5768 | tf_op jit(solution)/shard_map/ppermute | solution.py:121
  676.5 279.7 %copy-start.6 = (bf16[1,320,640]{1,2,0:T(8,128)(2,1)S(1)}, bf16[1,320,640]{1,2,0:T(8,128)(2,1)}, u32[]{:S(2)}) copy-start(bf16[1,320,640]{1,2,0:T(8,128)(2,1)} %reduce-scatter.3.cloned.1.call-done) | copy-start | bytes 1228804
  677.8 278.4 %collective-permute-start.22 = (bf16[160,640]{0,1:T(8,128)(2,1)S(1)}, bf16[160,640]{0,1:T(8,128)(2,1)S(1)}, u32[]{:S(2)}, u32[]{:S(2)}) collective-permute-start(bf16[160,640]{0,1:T(8,128)(2,1)S(1)} %select_bitcast_fusion.2), channel_id=1, source_target_pairs={{0,4},{4,0},{1,5},{5,1},{2,6},{6,2},{3,7},{7,3},{8,12},{12,8},{9,1... | collective-permute-start | bytes 614408 | tf_op jit(solution)/shard_map/ppermute | solution.py:89
  956.1 4.0 collective-permute-start.23
  (6 other events, 11.2 us)
Sparse Core Ops, SparseCore 0:
  511.4 165.0 reduce-scatter.2
  678.9 275.9 reduce-scatter.4

commit v3 on v0

v3 whole, which is shorter than its diff:
```python
import math

import jax
import jax.numpy as jnp
from jax import lax
from jax.experimental import pallas as pl
from jax.experimental.pallas import tpu as pltpu
from jax.sharding import Mesh
from jax.sharding import PartitionSpec as P

D = 1280
HD = 80
HEADS = 16
FF = 5120
TOK_IMG = 257
IMG_DEV = 8
TOTAL = IMG_DEV * TOK_IMG
EPS = 1e-06
PT = 272
F32 = jnp.float32
BF16 = jnp.bfloat16
NEG = -1e30
VMEM_LIMIT = 61 * 1024 * 1024


class Cfg:
    def __init__(self, n_dp, n_t, block_rows):
        self.n_dp, self.n_t, self.block = n_dp, n_t, block_rows
        self.n_p = n_dp // 2
        self.imgs = IMG_DEV // n_t
        self.ni = 2 * self.imgs
        self.rows = self.imgs * TOK_IMG
        self.m = self.ni * PT
        self.pd = D // n_dp
        self.hh = HEADS // n_t // 2
        self.hc = self.hh * HD
        self.f2 = FF // n_t // 2
        assert 4 * self.hc == self.f2
        self.caps = self._caps()

    def _caps(self):
        n, b, r = self.n_t, self.block, self.rows
        low = [max(t, TOTAL - (n - t) * b) for t in range(n + 1)]
        high = [min(t * b, TOTAL - (n - t)) for t in range(n + 1)]
        caps = {}
        for t in range(n):
            for dest in range(n):
                size = min(high[t + 1], r * (dest + 1)) - max(low[t], r * dest)
                size = min(size, b, r)
                if size > 0 and dest != t:
                    caps[dest - t] = max(caps.get(dest - t, 0), size)
        return {s: min(-(-c // 16) * 16, b) for s, c in sorted(caps.items())}


def dot(a, b):
    return lax.dot_general(a, b, (((1,), (0,)), ((), ())), preferred_element_type=F32)


def dot_nt(a, b):
    return lax.dot_general(a, b, (((1,), (1,)), ((), ())), preferred_element_type=F32)


def dot_tn(a, b):
    return lax.dot_general(a, b, (((0,), (0,)), ((), ())), preferred_element_type=F32)


def norm(values):
    mean = jnp.mean(values, axis=-1, keepdims=True)
    centred = values - mean
    spread = jnp.mean(centred * centred, axis=-1, keepdims=True)
    inverse = lax.rsqrt(spread + EPS)
    return centred * inverse, inverse


def norm_back(upstream, normed, inverse, gain):
    scaled = upstream * gain
    return inverse * (
        scaled
        - jnp.mean(scaled, axis=-1, keepdims=True)
        - normed * jnp.mean(scaled * normed, axis=-1, keepdims=True)
    )


ALL = ("p", "c", "t")


def params(**more):
    return pltpu.CompilerParams(vmem_limit_bytes=VMEM_LIMIT, **more)


def fixed(shape):
    return pl.BlockSpec(
        shape, lambda i, *s: (0,) * len(shape), pipeline_mode=pl.Buffered(1)
    )


MESH = pl.DeviceIdType.MESH


def enter(cfg):
    p, c, t = (lax.axis_index(axis) for axis in ALL)
    found = [{"c": 1 - c}]
    found += [{"t": lax.rem(t + k, cfg.n_t)} for k in range(1, cfg.n_t)]
    found += [{"p": p ^ m} for m in range(1, cfg.n_p)]
    barrier = pltpu.get_barrier_semaphore()
    for device in found:
        pl.semaphore_signal(barrier, inc=1, device_id=device, device_id_type=MESH)
    pl.semaphore_wait(barrier, len(found))


def greet_pair():
    barrier = pltpu.get_barrier_semaphore()
    other = {"c": 1 - lax.axis_index("c")}
    pl.semaphore_signal(barrier, inc=1, device_id=other, device_id_type=MESH)
    pl.semaphore_wait(barrier, 1)


def remote(source, target, sems, index, device):
    return pltpu.make_async_remote_copy(
        src_ref=source,
        dst_ref=target,
        send_sem=sems[0].at[index],
        recv_sem=sems[1].at[index],
        device_id=device,
        device_id_type=MESH,
    )


class Layout:
    def __init__(self, counts_ref, cfg):
        self.counts, self.cfg = counts_ref, cfg
        self.z = lax.axis_index("t")

    def start(self, block):
        total = 0
        for j in range(self.cfg.n_t):
            total = total + jnp.where(block > j, self.counts[0, j], 0)
        return total

    def end(self, block):
        return self.start(block + 1)

    def has(self, block):
        return (block >= 0) & (block < self.cfg.n_t)

    def window(self, block, dest, size):
        return jnp.clip(self.cfg.rows * dest - self.start(block), 0, self.cfg.block - size)

    def window_back(self, dest, block, size):
        return jnp.clip(self.start(block) - self.cfg.rows * dest, 0, max(0, self.cfg.rows - size))


def one_hot(positions, limit):
    columns = lax.broadcasted_iota(jnp.int32, (positions.shape[0], limit), 1)
    return jnp.where(columns == positions, 1.0, 0.0).astype(BF16)


def row_ids(count):
    return lax.broadcasted_iota(jnp.int32, (count, 1), 0)


def gather_and_attend(counts, tokens, cotangent, small, halves, cfg):
    n_t, n_p, ni, hc, hh, f2, pd, imgs, m = (
        cfg.n_t, cfg.n_p, cfg.ni, cfg.hc, cfg.hh, cfg.f2, cfg.pd, cfg.imgs, cfg.m,
    )
    n_dev = 2 * n_p * n_t
    piece = D // n_dev
    caps = list(cfg.caps.items())
    widest = max(size for _, size in caps)

    def kernel(
        counts_ref, tok_ref, ct_ref, small_ref, half_ref,
        x_ref, cot_ref, in_ref, qkv_ref, att_ref, lse_ref, out_ref, vec_ref, fc1_ref, g0_ref, g_ref,
        w, sent, got, parts, q_bias, v_bias,
        z_send, z_recv, p_send, p_recv, r_send, r_recv, c_send, c_recv, v_send, v_recv, own_sem, out_sem,
    ):
        p, core, z = (lax.axis_index(axis) for axis in ALL)
        layout = Layout(counts_ref, cfg)
        pair = {"c": 1 - core}

        def part_rows(plane, member):
            return pl.ds(pl.multiple_of((plane * 2 + member) * pd, 16), pd)

        def place(group, k, mask):
            rows = pl.ds(pl.multiple_of((p ^ mask) * 2 * pd, 16), 2 * pd)
            return w.at[k, rows, :] if group == 0 else g_ref.at[:, k, rows, :]

        def half(group, member):
            return half_ref.at[member, 0] if group == 0 else half_ref.at[member, pl.ds(1, 2)]

        def half_place(group):
            rows = part_rows(p, core)
            return w.at[0, rows, :] if group == 0 else g_ref.at[:, 0, rows, :]

        def keep(group):
            return pltpu.make_async_copy(half(group, core), half_place(group), own_sem.at[group])

        def trade(group):
            return remote(half(group, 1 - core), half_place(group), (c_send, c_recv), group, pair)

        def z_copy(group, k):
            target = {"t": lax.rem(z + 1, n_t)}
            return remote(place(group, k - 1, 0), place(group, k, 0), (z_send, z_recv), (group, k), target)

        def p_copy(group, k, mask):
            ref = place(group, k, 0)
            return remote(ref, ref, (p_send, p_recv), (group, k, mask), {"p": p ^ mask})

        def d_copies(group, k):
            if n_p != 4:
                return []

            def rows(mask):
                return pl.ds(pl.multiple_of((p ^ mask) * 2 * pd, 16), 2 * pd)

            if group == 0:
                via = 1 + k % 2
                ref = w.at[k, rows(via), :]
                return [remote(ref, ref, (p_send, p_recv), (group, k, 3), {"p": p ^ (3 - via)})]
            ref_1, ref_2 = g_ref.at[0, k, rows(1), :], g_ref.at[1, k, rows(2), :]
            return [
                remote(ref_1, ref_1, (p_send, p_recv), (group, k, 3), {"p": p ^ 2}),
                remote(ref_2, ref_2, (p_send, p_recv), (group, k, 0), {"p": p ^ 1}),
            ]

        direct = (1, 2) if n_p == 4 else tuple(range(1, n_p))

        def have_own(group):
            keep(group).wait()
            trade(group).wait()

        def send_p(group, k):
            if k > 0:
                z_copy(group, k).wait_recv()
            if k + 1 < n_t:
                z_copy(group, k + 1).start()
            for mask in direct:
                p_copy(group, k, mask).start()

        def send_d(group, k):
            for mask in direct:
                p_copy(group, k, mask).wait_recv()
            for copy in d_copies(group, k):
                copy.start()

        def finish(group):
            for k in range(n_t):
                for copy in d_copies(group, k):
                    copy.wait_recv()
                    copy.wait_send()
                for mask in direct:
                    p_copy(group, k, mask).wait_send()
                if k > 0:
                    z_copy(group, k).wait_send()

        def row_copy(which, s):
            shift, size = caps[s]
            rows = pl.ds(0, size)
            return remote(
                sent.at[which, s, rows], got.at[which, s, rows], (r_send, r_recv), (which, s),
                {"t": jnp.clip(z + shift, 0, n_t - 1)},
            )

        def send_rows(which, block_ref):
            for s, (shift, size) in enumerate(caps):

                @pl.when(layout.has(z + shift))
                def _(s=s, shift=shift, size=size):
                    begin = layout.window(z, z + shift, size)
                    picked = dot(one_hot(begin + row_ids(size), cfg.block), block_ref[...])
                    sent[which, s, :size] = picked.astype(BF16)
                    row_copy(which, s).start()

        def take_rows(which, block_ref, images_ref):
            for i in range(imgs):
                row = row_ids(PT)
                position = cfg.rows * z + i * TOK_IMG + row
                valid = row < TOK_IMG
                mine = valid & (position < layout.end(z))
                spots = jnp.where(mine, position - layout.start(z), -1)
                images_ref[i] = dot(one_hot(spots, cfg.block), block_ref[...]).astype(BF16)
            for s, (shift, size) in enumerate(caps):
                source = z - shift

                @pl.when(layout.has(source))
                def _(s=s, size=size, source=source):
                    row_copy(which, s).wait_recv()
                    for i in range(imgs):
                        row = row_ids(PT)
                        position = cfg.rows * z + i * TOK_IMG + row
                        mine = (row < TOK_IMG) & (position < layout.end(source))
                        mine = mine & (position >= layout.start(source))
                        spots = position - layout.start(source) - layout.window(source, z, size)
                        picked = dot(one_hot(jnp.where(mine, spots, -1), size), got[which, s, :size])
                        images_ref[i] += picked.astype(BF16)

                @pl.when(layout.has(z + shift))
                def _(s=s):
                    row_copy(which, s).wait_send()

        def pair_rows(which, images_ref):
            mine, other = pl.ds(0, imgs), pl.ds(imgs, imgs)
            return remote(images_ref.at[mine], images_ref.at[other], (c_send, c_recv), 2 + which, pair)

        device = (2 * p + core) * n_t + z

        def part_copies(stage):
            if stage == 0:
                ref = parts.at[device]
                targets = [(k, {"t": lax.rem(z + k, n_t)}) for k in range(1, n_t)]
            elif stage == 1:
                ref = parts.at[pl.ds((2 * p + core) * n_t, n_t)]
                targets = [(n_t, pair)]
            else:
                ref = parts.at[pl.ds(2 * p * n_t, 2 * n_t)]
                targets = [(n_t + mask, {"p": p ^ mask}) for mask in range(1, n_p)]
            return [remote(ref, ref, (v_send, v_recv), index, target) for index, target in targets]

        def part_stage(stage):
            if stage > 0:
                for copy in part_copies(stage - 1):
                    copy.wait()
            if stage < 3:
                for copy in part_copies(stage):
                    copy.start()

        def spread():
            for d in range(n_dev):
                vec_ref[:, d * piece : (d + 1) * piece] = parts[d, :8, :piece]
            for k in range(n_t):
                block = 2 * lax.rem(z - k + n_t, n_t) + core
                for j in range(hc // piece):
                    cols = slice(j * piece, (j + 1) * piece)
                    owner = block * (hc // piece) + j
                    q_bias[k : k + 1, cols] = parts[owner, 4:5, :piece]
                    v_bias[k : k + 1, cols] = parts[owner, 5:6, :piece]
                for j in range(f2 // (4 * piece)):
                    owner = block * (f2 // (4 * piece)) + j
                    for r in range(4):
                        begin = (4 * j + r) * piece
                        fc1_ref[k : k + 1, begin : begin + piece] = parts[owner, 8 + r : 9 + r, :piece]

        for group in range(2):
            keep(group).start()
        parts[device] = small_ref[...]
        enter(cfg)
        for group in range(2):
            trade(group).start()
        part_stage(0)
        send_rows(0, tok_ref)
        have_own(0)
        send_p(0, 0)
        part_stage(1)
        send_rows(1, ct_ref)
        part_stage(2)
        send_p(0, 1)
        send_d(0, 0)
        take_rows(0, tok_ref, x_ref)
        pair_rows(0, x_ref).start()
        have_own(1)
        part_stage(3)
        spread()
        for k in range(2, n_t):
            send_p(0, k)
            send_d(0, k - 1)
        send_p(1, 0)
        take_rows(1, ct_ref, cot_ref)
        pair_rows(1, cot_ref).start()
        send_d(0, n_t - 1)
        pair_rows(0, x_ref).wait()
        finish(0)
        kept = pltpu.make_async_copy(w, g0_ref, out_sem)
        kept.start()

        steps = []
        for k in range(1, n_t):
            steps += [lambda k=k: send_p(1, k), lambda k=k: send_d(1, k - 1)]
        steps.append(lambda: send_d(1, n_t - 1))
        early = 2 * len(steps) // 5
        keyed = lax.broadcasted_iota(jnp.int32, (PT, PT), 1) < TOK_IMG

        def image(i, carry):
            normed, _ = norm(x_ref[i].astype(F32))
            attn_in = (normed * vec_ref[0:1, :] + vec_ref[2:3, :]).astype(BF16)
            in_ref[i] = attn_in
            for k in range(n_t):
                qkv = dot(attn_in, w[k, :, : 3 * hc])
                query = (qkv[:, :hc] + q_bias[k : k + 1, :]).astype(BF16)
                keys = qkv[:, hc : 2 * hc].astype(BF16)
                values = (qkv[:, 2 * hc :] + v_bias[k : k + 1, :]).astype(BF16)
                qkv_ref[k, i, :, :hc] = query
                qkv_ref[k, i, :, hc : 2 * hc] = keys
                qkv_ref[k, i, :, 2 * hc :] = values
                for h in range(hh):
                    cols = slice(h * HD, (h + 1) * HD)
                    scores = dot_nt(query[:, cols], keys[:, cols]) * (HD**-0.5)
                    scores = jnp.where(keyed, scores, NEG)
                    top = jnp.max(scores, axis=-1, keepdims=True)
                    expo = jnp.exp(scores - top)
                    summed = jnp.sum(expo, axis=-1, keepdims=True)
                    probs = (expo / summed).astype(BF16)
                    att_ref[k, i, :, cols] = dot(probs, values[:, cols]).astype(BF16)
                    lse_ref[k, i, :, h : h + 1] = top + jnp.log(summed)
                part = dot_nt(att_ref[k, i], w[k, :, 3 * hc :])
                if k == 0:
                    out_ref[i] = part
                else:
                    out_ref[i] += part
            for j in range(early):

                @pl.when(i == (j + 1) * ni // early - 1)
                def _(j=j):
                    steps[j]()

            return carry

        lax.fori_loop(0, ni, image, 0)
        pair_rows(1, cot_ref).wait()
        for step in steps[early:]:
            step()
        finish(1)
        kept.wait()

    vmem = pl.BlockSpec(memory_space=pltpu.VMEM)
    smem = pl.BlockSpec(memory_space=pltpu.SMEM)
    anywhere = pl.BlockSpec(memory_space=pl.ANY)
    dma = pltpu.SemaphoreType.DMA
    return pl.pallas_call(
        kernel,
        in_specs=[smem, vmem, vmem, vmem, anywhere],
        out_specs=[vmem] * 9 + [anywhere] * 2,
        out_shape=[
            jax.ShapeDtypeStruct((ni, PT, D), BF16),
            jax.ShapeDtypeStruct((ni, PT, D), BF16),
            jax.ShapeDtypeStruct((ni, PT, D), BF16),
            jax.ShapeDtypeStruct((n_t, ni, PT, 3 * hc), BF16),
            jax.ShapeDtypeStruct((n_t, ni, PT, hc), BF16),
            jax.ShapeDtypeStruct((n_t, ni, PT, hh), F32),
            jax.ShapeDtypeStruct((ni, PT, D), F32),
            jax.ShapeDtypeStruct((8, D), F32),
            jax.ShapeDtypeStruct((n_t, f2), F32),
            jax.ShapeDtypeStruct((n_t, D, f2), BF16),
            jax.ShapeDtypeStruct((2, n_t, D, f2), BF16),
        ],
        scratch_shapes=[
            pltpu.VMEM((n_t, D, f2), BF16),
            pltpu.VMEM((2, len(caps), widest, D), BF16),
            pltpu.VMEM((2, len(caps), widest, D), BF16),
            pltpu.VMEM((n_dev, 16, 128), F32),
            pltpu.VMEM((n_t, hc), F32),
            pltpu.VMEM((n_t, hc), F32),
            dma((2, n_t)),
            dma((2, n_t)),
            dma((2, n_t, n_p)),
            dma((2, n_t, n_p)),
            dma((2, len(caps))),
            dma((2, len(caps))),
            dma((4,)),
            dma((4,)),
            dma((n_t + n_p,)),
            dma((n_t + n_p,)),
            dma((2,)),
            dma,
        ],
        compiler_params=params(collective_id=0, has_side_effects=True),
        cost_estimate=pl.CostEstimate(
            flops=2 * m * D * f2 * n_t,
            bytes_accessed=2 * n_t * D * f2 + 12 * m * D,
            transcendentals=m * PT * n_t * hh,
        ),
        name="gather_and_attend",
    )(counts, tokens, cotangent, small, halves)


def reduce_and_attend_back(
    counts, grad_hidden, attn_in, qkv, attended, lse, weights, mlp_grads, residual, x, mixed, vectors, sums, fc1_sums, cfg
):
    n_t, n_p, ni, hc, hh, f2, pd, m, imgs = (
        cfg.n_t, cfg.n_p, cfg.ni, cfg.hc, cfg.hh, cfg.f2, cfg.pd, cfg.m, cfg.imgs,
    )
    scale = HD**-0.5
    square = n_p == 4
    plane = (2, 2) if square else (n_p,)
    jobs = [((k, k), k) for k in range(n_t)] + [((k, k + 1), None) for k in range(0, n_t, 2)]
    n_jobs = len(jobs)
    n_got = 2 if square else n_p - 1
    n_dev = 2 * n_p * n_t
    width = D // n_dev
    caps = list(cfg.caps.items())
    widest = max(size for _, size in caps)
    to_z = {}
    for n, (chunks, _) in enumerate(jobs):
        for part in range(2):
            if chunks[part] > 0:
                to_z[n, part] = len(to_z)

    def kernel(
        counts_ref, gh_ref, in_ref, qkv_ref, att_ref, lse_ref, w_ref, g_ref, res_ref, x_ref, mix_ref, vec_ref,
        sums_ref, fsum_ref,
        half_ref, mixed_ref, dtok_ref, small_ref, own_grads, rows_got, in_other, got_z,
        gqkv, stage, held, got, got_2, total, out, dq, dv,
        images, sent, taken, block, res_in, other_in, parts, parts_p, parts_c, parts_t,
        stage_sem, held_sem, s_send, s_recv, t_send, t_recv, z_send, z_recv, r_send, r_recv, c_send, c_recv,
        v_send, v_recv, in_sem, out_sem,
    ):
        p, core, z = (lax.axis_index(axis) for axis in ALL)
        py, px = p >> 1, p & 1
        pair = {"c": 1 - core}
        step = pl.program_id(0)
        layout = Layout(counts_ref, cfg)

        def pieces(n, part, *index):
            (chunks, k) = jobs[n]
            if k is None:
                return own_grads.at[(chunks[part], *index)]
            return g_ref.at[(*index, k, part)]

        def first_copies(n):
            if square:
                return [
                    remote(pieces(n, 0, slice(None), px ^ 1), got.at[n, 0], (s_send, s_recv), (n, 0, 0), {"p": p ^ 1}),
                    remote(pieces(n, 1, py ^ 1, slice(None)), got.at[n, 1], (s_send, s_recv), (n, 1, 0), {"p": p ^ 2}),
                ]
            return [
                remote(pieces(n, part, p ^ q), got.at[n, part, q - 1], (s_send, s_recv), (n, part, q - 1), {"p": p ^ q})
                for part in range(2)
                for q in range(1, n_p)
            ]

        def second_copies(n):
            if not square:
                return []
            return [
                remote(got.at[n, 0, py ^ 1], got_2.at[n, 0], (t_send, t_recv), (n, 0), {"p": p ^ 2}),
                remote(got.at[n, 1, px ^ 1], got_2.at[n, 1], (t_send, t_recv), (n, 1), {"p": p ^ 1}),
            ]

        def z_copy(n, part):
            k = jobs[n][0][part]
            source = got.at[n, part, (py, px)[part] if square else 0]
            target = {"t": lax.rem(z - k + n_t, n_t)}
            index = to_z[n, part]
            return remote(source, got_z.at[index], (z_send, z_recv), index, target)

        def loads(n):
            if square:
                sources = [pieces(n, 0, slice(None), px), pieces(n, 1, py, slice(None))]
            else:
                sources = [pieces(n, 0, p), pieces(n, 1, p)]
            return [
                pltpu.make_async_copy(
                    source, held.at[n % 2, part] if square else held.at[n % 2, part, 0], held_sem.at[n % 2, part]
                )
                for part, source in enumerate(sources)
            ]

        def begin(n):
            for copy in first_copies(n):
                copy.start()

        def fetch(n):
            for copy in loads(n):
                copy.start()

        def middle(n):
            for copy in loads(n):
                copy.wait()
            for copy in first_copies(n):
                copy.wait_recv()
            if square:
                for part, here in enumerate((py, px)):
                    there = here ^ 1
                    both = held[n % 2, part, there].astype(F32) + got[n, part, there].astype(F32)
                    got[n, part, there] = both.astype(BF16)
                for copy in second_copies(n):
                    copy.start()

        def last(n):
            for copy in second_copies(n):
                copy.wait_recv()
            chunks, k = jobs[n]
            for part, here in enumerate((py, px)):
                if square:
                    whole = held[n % 2, part, here].astype(F32) + got[n, part, here].astype(F32)
                    whole = whole + got_2[n, part].astype(F32)
                else:
                    whole = held[n % 2, part, 0].astype(F32)
                    for q in range(n_p - 1):
                        whole = whole + got[n, part, q].astype(F32)
                if chunks[part] == 0:
                    total[0 if k is None else 1 + part] = whole
                else:
                    got[n, part, here if square else 0] = whole.astype(BF16)
                    z_copy(n, part).start()

        def tick(n):
            middle(n)
            if n > 0:
                last(n - 1)
                if n + 1 < n_jobs:
                    fetch(n + 1)
            if n + 2 < n_jobs:
                begin(n + 2)

        def stage_copy(k):
            return pltpu.make_async_copy(stage, own_grads.at[k], stage_sem)

        def finish():
            last(n_jobs - 1)
            for n in range(n_jobs):
                for copy in first_copies(n) + second_copies(n):
                    copy.wait_send()
                for part in range(2):
                    if (n, part) in to_z:
                        z_copy(n, part).wait()
            reads = [
                pltpu.make_async_copy(got_z.at[index], got.at[n, part, 0], z_recv.at[index])
                for (n, part), index in to_z.items()
            ]
            for read in reads:
                read.start()
            for read in reads:
                read.wait()
            for unit in range(3):
                whole = total[unit]
                for n, part in to_z:
                    if unit == (0 if jobs[n][1] is None else 1 + part):
                        whole = whole + got[n, part, 0].astype(F32)
                total[unit] = whole

            def rows(member):
                return total.at[:, pl.ds(pl.multiple_of(member * pd, 16), pd), :]

            kept = pltpu.make_async_copy(rows(core), half_ref.at[core], out_sem)
            traded = remote(rows(1 - core), half_ref.at[core], (c_send, c_recv), 1, pair)
            kept.start()
            traded.start()
            kept.wait()
            traded.wait()

        def row_copy(which, s):
            shift, size = caps[s]
            return remote(
                sent.at[s, pl.ds(0, size)], rows_got.at[which, s, pl.ds(0, size)], (r_send, r_recv), (which, s),
                {"t": jnp.clip(z - shift, 0, n_t - 1)},
            )

        def of_images(positions, valid):
            rows = None
            for i in range(imgs):
                spots = positions - i * TOK_IMG
                spots = jnp.where(valid & (spots >= 0) & (spots < TOK_IMG), spots, -1)
                picked = dot(one_hot(spots, PT), images[i])
                rows = picked if rows is None else rows + picked
            return rows.astype(BF16)

        def send_rows(which):
            for s, (shift, size) in enumerate(caps):

                @pl.when(layout.has(z - shift))
                def _(s=s, shift=shift, size=size):
                    want = layout.window_back(z, z - shift, size) + row_ids(size)
                    sent[s, :size] = of_images(want, want >= 0)
                    row_copy(which, s).start()

        def take_rows(which, target):
            row = row_ids(cfg.block)
            position = layout.start(z) + row
            valid = position < layout.end(z)
            block[...] = of_images(position - cfg.rows * z, valid)
            for s, (shift, size) in enumerate(caps):
                source = z + shift

                @pl.when(layout.has(source))
                def _(s=s, size=size, source=source):
                    row_copy(which, s).wait_recv()
                    load = pltpu.make_async_copy(
                        rows_got.at[which, s, pl.ds(0, size)], taken.at[pl.ds(0, size)], in_sem.at[0]
                    )
                    load.start()
                    load.wait()
                    local = position - cfg.rows * source
                    mine = valid & (local >= 0) & (local < cfg.rows)
                    spots = jnp.where(mine, local - layout.window_back(source, z, size), -1)
                    block[...] += dot(one_hot(spots, size), taken[:size]).astype(BF16)

                @pl.when(layout.has(z - shift))
                def _(s=s):
                    row_copy(which, s).wait_send()

            store = pltpu.make_async_copy(block, target, in_sem.at[0])
            store.start()
            store.wait()

        device = (2 * p + core) * n_t + z

        def gather_parts(gain, shift):
            parts[...] = jnp.zeros_like(parts)
            rows = [gain, sums_ref[0:1, :], shift, sums_ref[1:2, :], sums_ref[2:3, :], sums_ref[3:4, :]]
            for d in range(n_dev):
                cols = slice(d * width, (d + 1) * width)
                for r, value in zip((0, 1, 2, 3, 6, 7), rows):
                    parts[d, r : r + 1, :width] = value[:, cols]
            for k in range(n_t):
                chunk = 2 * lax.rem(z - k + n_t, n_t) + core
                for j in range(hc // width):
                    cols = slice(j * width, (j + 1) * width)
                    owner = chunk * (hc // width) + j
                    parts[owner, 4:5, :width] = dq[k : k + 1, cols]
                    parts[owner, 5:6, :width] = dv[k : k + 1, cols]
                for j in range(f2 // (4 * width)):
                    owner = chunk * (f2 // (4 * width)) + j
                    for r in range(4):
                        begin_at = (4 * j + r) * width
                        parts[owner, 8 + r : 9 + r, :width] = fsum_ref[k, :, begin_at : begin_at + width]

        def plane_parts(index):
            return pl.ds(2 * index * n_t, 2 * n_t)

        def core_parts(member):
            return pl.ds((2 * p + member) * n_t, n_t)

        def part_copies(hop):
            if hop == 0:
                return [
                    remote(parts.at[plane_parts(p ^ q)], parts_p.at[q - 1], (v_send, v_recv), q - 1, {"p": p ^ q})
                    for q in range(1, n_p)
                ]
            if hop == 1:
                return [remote(parts.at[core_parts(1 - core)], parts_c, (v_send, v_recv), n_p - 1, pair)]
            copies = []
            for k in range(1, n_t):
                to = lax.rem(z + k, n_t)
                source = parts.at[(2 * p + core) * n_t + to]
                copies.append(remote(source, parts_t.at[k], (v_send, v_recv), n_p - 1 + k, {"t": to}))
            return copies

        def part_hop(hop):
            if hop > 0:
                for copy in part_copies(hop - 1):
                    copy.wait()
            if hop == 1:
                for q in range(n_p - 1):
                    parts[plane_parts(p)] += parts_p[q]
            if hop == 2:
                parts[core_parts(core)] += parts_c[...]
            if hop == 3:
                mine = parts[device]
                for k in range(1, n_t):
                    mine = mine + parts_t[k]
                small_ref[...] = mine
            if hop < 3:
                for copy in part_copies(hop):
                    copy.start()

        def in_copy():
            return remote(out.at[pl.ds(imgs, imgs)], in_other, (c_send, c_recv), 0, pair)

        def first_norm_back():
            in_copy().wait()
            gain, shift = jnp.zeros((1, D), F32), jnp.zeros((1, D), F32)
            for i in range(imgs):
                reads = [
                    pltpu.make_async_copy(res_ref.at[i], res_in, in_sem.at[0]),
                    pltpu.make_async_copy(in_other.at[i], other_in, in_sem.at[1]),
                    pltpu.make_async_copy(x_ref.at[i], taken.at[pl.ds(0, PT)], in_sem.at[2]),
                ]
                for read in reads:
                    read.start()
                for read in reads:
                    read.wait()
                up = out[i] + other_in[...]
                normed, inverse = norm(taken[:PT].astype(F32))
                grad = res_in[...] + norm_back(up, normed, inverse, vec_ref[0:1, :])
                images[i] = grad.astype(BF16)
                gain = gain + jnp.sum(up * normed, axis=0, keepdims=True)
                shift = shift + jnp.sum(up, axis=0, keepdims=True)
            gather_parts(gain, shift)

        @pl.when(step == 0)
        def _():
            fetch(0)
            fetch(1)
            read = pltpu.make_async_copy(mix_ref, images, in_sem.at[0])
            read.start()
            enter(cfg)
            begin(0)
            begin(1)
            read.wait()
            send_rows(0)

        keyed = lax.broadcasted_iota(jnp.int32, (PT, PT), 1) < TOK_IMG
        total_q, total_v = jnp.zeros((1, hc), F32), jnp.zeros((1, hc), F32)
        for i in range(ni):
            grad_att = dot(gh_ref[i], w_ref[0, :, 3 * hc :]).astype(BF16)
            sums_q, sums_v = [], []
            for h in range(hh):
                cols = slice(h * HD, (h + 1) * HD)
                key_cols = slice(hc + h * HD, hc + (h + 1) * HD)
                value_cols = slice(2 * hc + h * HD, 2 * hc + (h + 1) * HD)
                query = qkv_ref[0, i, :, cols]
                keys = qkv_ref[0, i, :, key_cols]
                values = qkv_ref[0, i, :, value_cols]
                grad = grad_att[:, cols]
                scores = dot_nt(query, keys) * scale - lse_ref[0, i, :, h : h + 1]
                probs = jnp.exp(jnp.where(keyed, scores, NEG))
                delta = jnp.sum(
                    grad.astype(F32) * att_ref[0, i, :, cols].astype(F32), axis=-1, keepdims=True
                )
                grad_v = dot_tn(probs.astype(BF16), grad)
                grad_s = (probs * (dot_nt(grad, values) - delta) * scale).astype(BF16)
                grad_q = dot(grad_s, keys)
                grad_k = dot_tn(grad_s, query)
                sums_q.append(jnp.sum(grad_q, axis=0, keepdims=True))
                sums_v.append(jnp.sum(grad_v, axis=0, keepdims=True))
                gqkv[i, :, cols] = grad_q.astype(BF16)
                gqkv[i, :, key_cols] = grad_k.astype(BF16)
                gqkv[i, :, value_cols] = grad_v.astype(BF16)
            total_q = total_q + jnp.concatenate(sums_q, axis=1)
            total_v = total_v + jnp.concatenate(sums_v, axis=1)
            part = dot_nt(gqkv[i], w_ref[0, :, : 3 * hc])

            @pl.when(step == 0)
            def _(i=i, part=part):
                out[i] = part

            @pl.when(step > 0)
            def _(i=i, part=part):
                out[i] += part

            for n in range(n_t - 2):
                if i == min(2 * n + 1, ni - 1):

                    @pl.when(step == n + 1)
                    def _(n=n):
                        tick(n)

        dq[pl.ds(step, 1), :] = total_q
        dv[pl.ds(step, 1), :] = total_v

        @pl.when(step == n_t - 1)
        def _():
            in_copy().start()

        left = dot_tn(in_ref[...].reshape(m, D), gqkv[...].reshape(m, 3 * hc)).astype(BF16)
        right = dot_tn(gh_ref[...].reshape(m, D), att_ref[0].reshape(m, hc)).astype(BF16)

        @pl.when(step > 0)
        def _():
            stage_copy(0).wait()

        ahead = [slice(None)] * (len(plane) + 1)
        stage[(*ahead, slice(0, 3 * hc))] = left.reshape((*plane, 2 * pd, 3 * hc))
        stage[(*ahead, slice(3 * hc, f2))] = right.reshape((*plane, 2 * pd, hc))
        for k in range(n_t):

            @pl.when(step == k)
            def _(k=k):
                stage_copy(k).start()

        @pl.when(step == n_t - 2)
        def _():
            take_rows(0, mixed_ref)

        @pl.when(step == n_t - 1)
        def _():
            stage_copy(0).wait()
            tick(n_t - 2)
            first_norm_back()
            send_rows(1)
            part_hop(0)
            tick(n_t - 1)
            part_hop(1)
            for n in range(n_t, n_jobs - 1):
                tick(n)
            part_hop(2)
            take_rows(1, dtok_ref)
            tick(n_jobs - 1)
            part_hop(3)
            finish()

    dma = pltpu.SemaphoreType.DMA
    chunk = (2 * pd, f2)
    vmem = pltpu.VMEM

    def chunk_block(last):
        return pl.BlockSpec((1, ni, PT, last), lambda k: (k, 0, 0, 0))

    anywhere = pl.BlockSpec(memory_space=pl.ANY)
    shape = jax.ShapeDtypeStruct
    n_v = n_p - 1 + n_t
    outs = pl.pallas_call(
        kernel,
        grid=(n_t,),
        in_specs=[
            pl.BlockSpec(memory_space=pltpu.SMEM),
            fixed((ni, PT, D)),
            fixed((ni, PT, D)),
            chunk_block(3 * hc),
            chunk_block(hc),
            chunk_block(hh),
            pl.BlockSpec((1, D, f2), lambda k: (k, 0, 0)),
            anywhere,
            anywhere,
            anywhere,
            anywhere,
            fixed((8, D)),
            fixed((4, D)),
            fixed((n_t, 1, f2)),
        ],
        out_specs=[anywhere] * 3 + [fixed((16, 128))] + [anywhere] * 4,
        out_shape=[
            shape((2, 3, pd, f2), F32),
            shape((cfg.block, D), BF16),
            shape((cfg.block, D), BF16),
            shape((16, 128), F32),
            shape((n_t, *plane, *chunk), BF16),
            shape((2, len(caps), widest, D), BF16),
            shape((imgs, PT, D), F32),
            shape((len(to_z), *chunk), BF16),
        ],
        scratch_shapes=[
            vmem((ni, PT, 3 * hc), BF16),
            vmem((*plane, *chunk), BF16),
            vmem((2, 2, 2 if square else 1, *chunk), BF16),
            vmem((n_jobs, 2, n_got, *chunk), BF16),
            vmem((n_jobs, 2, *(chunk if square else (16, 128))), BF16),
            vmem((3, *chunk), F32),
            vmem((ni, PT, D), F32),
            vmem((n_t, hc), F32),
            vmem((n_t, hc), F32),
            vmem((imgs, PT, D), BF16),
            vmem((len(caps), widest, D), BF16),
            vmem((max(widest, PT), D), BF16),
            vmem((cfg.block, D), BF16),
            vmem((PT, D), F32),
            vmem((PT, D), F32),
            vmem((n_dev, 16, 128), F32),
            vmem((n_p - 1, 2 * n_t, 16, 128), F32),
            vmem((n_t, 16, 128), F32),
            vmem((n_t, 16, 128), F32),
            dma,
            dma((2, 2)),
            dma((n_jobs, 2, 1 if square else n_p - 1)),
            dma((n_jobs, 2, 1 if square else n_p - 1)),
            dma((n_jobs, 2)),
            dma((n_jobs, 2)),
            dma((len(to_z),)),
            dma((len(to_z),)),
            dma((2, len(caps))),
            dma((2, len(caps))),
            dma((2,)),
            dma((2,)),
            dma((n_v,)),
            dma((n_v,)),
            dma((3,)),
            dma,
        ],
        compiler_params=params(collective_id=1, has_side_effects=True),
        cost_estimate=pl.CostEstimate(
            flops=4 * m * D * f2 * n_t + 10 * m * PT * HD * n_t * hh,
            bytes_accessed=4 * n_t * D * f2 + 20 * m * D,
            transcendentals=m * PT * n_t * hh,
        ),
        name="reduce_and_attend_back",
    )(
        counts,
        grad_hidden,
        attn_in,
        qkv,
        attended,
        lse,
        weights,
        mlp_grads.reshape((*plane, n_t, 2, *chunk)),
        residual,
        x,
        mixed,
        vectors,
        sums,
        fc1_sums,
    )
    return outs[:4]


def mlp_pass(x, attn_out, vectors, cot, fc1, weights, cfg):
    n_p, n_t, m, pd, w, ni, imgs = cfg.n_p, cfg.n_t, cfg.m, cfg.pd, cfg.f2, cfg.ni, cfg.imgs

    def kernel(
        x_ref, outs_ref, vec_ref, cot_ref, fc1_ref, w1_ref, w2_ref,
        sum_ref, grad_ref, res_ref, gh_ref, sums_ref, mixed_ref,
        other, other_y, mlp_in, act_all, gpre_all, back, y, gh, c_send, c_recv, own_sem,
    ):
        step = pl.program_id(0)
        pair = {"c": 1 - lax.axis_index("c")}
        mine, theirs = pl.ds(0, imgs), pl.ds(imgs, imgs)

        def pair_copy(index, source, target):
            return remote(source, target, (c_send, c_recv), index, pair)

        def back_copy():
            return pair_copy(2, back.at[theirs], other)

        def y_copy():
            return pair_copy(3, y.at[theirs], other_y)

        @pl.when(step == 0)
        def _():
            own_part = pltpu.make_async_copy(outs_ref.at[mine], res_ref, own_sem)
            own_part.start()
            greet_pair()
            out_copy = pair_copy(0, outs_ref.at[theirs], other)
            out_copy.start()
            own_part.wait()
            out_copy.wait()
            for i in range(imgs):
                value = x_ref[i].astype(F32) + (res_ref[i] + other[i]) + vec_ref[6:7, :]
                res_ref[i] = value
                normed, _ = norm(value)
                mlp_in[i] = (normed * vec_ref[1:2, :] + vec_ref[3:4, :]).astype(BF16)
            in_copy = pair_copy(1, mlp_in.at[mine], mlp_in.at[theirs])
            in_copy.start()
            in_copy.wait()

        w1, w2 = w1_ref[0, 0], w2_ref[0, 0]
        total = jnp.zeros((1, w), F32)
        for i in range(ni):
            rows = slice(i * PT, (i + 1) * PT)
            pre = dot(mlp_in[i], w1) + fc1_ref[0]
            phi = 0.5 * (1.0 + lax.erf(pre * (1.0 / math.sqrt(2.0))))
            act_all[rows, :] = (pre * phi).astype(BF16)
            slope = phi + pre * jnp.exp(-0.5 * pre * pre) * (1.0 / math.sqrt(2.0 * math.pi))
            gpre = dot(cot_ref[i], w2) * slope
            total = total + jnp.sum(gpre, axis=0, keepdims=True)
            gpre_all[rows, :] = gpre.astype(BF16)
        sum_ref[0] = total

        def add(target, left, right):
            value = dot_nt(left, right).reshape(ni, PT, D)

            @pl.when(step == 0)
            def _():
                target[...] = value

            @pl.when(step > 0)
            def _():
                target[...] += value

        add(back, gpre_all[...], w1)

        @pl.when(step == n_t - 1)
        def _():
            back_copy().start()

        add(y, act_all[...], w2)

        @pl.when(step == n_t - 1)
        def _():
            y_copy().start()

        grad_1 = dot_tn(mlp_in[...].reshape(m, D), gpre_all[...]).astype(BF16)
        grad_ref[:, 0, 0] = grad_1.reshape(n_p, 2 * pd, w)
        grad_2 = dot_tn(cot_ref[...].reshape(m, D), act_all[...]).astype(BF16)
        grad_ref[:, 0, 1] = grad_2.reshape(n_p, 2 * pd, w)

        @pl.when(step == n_t - 1)
        def _():
            back_copy().wait()
            sums = [jnp.zeros((1, D), F32)] * 4
            for i in range(imgs):
                up = back[i] + other[i]
                hidden = res_ref[i]
                other[i] = hidden
                normed, inverse = norm(hidden)
                cot_f = cot_ref[i].astype(F32)
                grad = cot_f + norm_back(up, normed, inverse, vec_ref[1:2, :])
                res_ref[i] = grad
                gh[i] = grad.astype(BF16)
                terms = (up * normed, up, grad, cot_f)
                sums = [s + jnp.sum(t, axis=0, keepdims=True) for s, t in zip(sums, terms)]
            grad_copy = pair_copy(4, gh.at[mine], gh.at[theirs])
            grad_copy.start()
            for r in range(4):
                sums_ref[r : r + 1, :] = sums[r]
            y_copy().wait()
            for i in range(imgs):
                mixed_ref[i] = (other[i] + (y[i] + other_y[i]) + vec_ref[7:8, :]).astype(BF16)
            grad_copy.wait()
            store = pltpu.make_async_copy(gh, gh_ref, own_sem)
            store.start()
            store.wait()

    def half_spec(unit):
        return pl.BlockSpec((1, 1, D, w), lambda i: (unit, i, 0, 0))

    full = fixed((ni, PT, D))
    own = fixed((imgs, PT, D))
    shape, vmem, dma = jax.ShapeDtypeStruct, pltpu.VMEM, pltpu.SemaphoreType.DMA
    return pl.pallas_call(
        kernel,
        grid=(n_t,),
        in_specs=[
            own,
            pl.BlockSpec(memory_space=pl.ANY),
            fixed((8, D)),
            full,
            pl.BlockSpec((1, 1, w), lambda i: (i, 0, 0)),
            half_spec(0),
            half_spec(1),
        ],
        out_specs=[
            pl.BlockSpec((1, 1, w), lambda i: (i, 0, 0)),
            pl.BlockSpec((n_p, 1, 2, 2 * pd, w), lambda i: (0, i, 0, 0, 0)),
            own,
            pl.BlockSpec(memory_space=pl.ANY),
            fixed((4, D)),
            own,
        ],
        out_shape=[
            shape((n_t, 1, w), F32),
            shape((n_p, n_t, 2, 2 * pd, w), BF16),
            shape((imgs, PT, D), F32),
            shape((ni, PT, D), BF16),
            shape((4, D), F32),
            shape((imgs, PT, D), BF16),
        ],
        scratch_shapes=[
            vmem((imgs, PT, D), F32),
            vmem((imgs, PT, D), F32),
            vmem((ni, PT, D), BF16),
            vmem((m, w), BF16),
            vmem((m, w), BF16),
            vmem((ni, PT, D), F32),
            vmem((ni, PT, D), F32),
            vmem((ni, PT, D), BF16),
            dma((5,)),
            dma((5,)),
            dma,
        ],
        compiler_params=params(collective_id=2, has_side_effects=True),
        cost_estimate=pl.CostEstimate(
            flops=12 * m * D * w * n_t,
            bytes_accessed=12 * m * D + 8 * D * w * n_t,
            transcendentals=2 * m * w * n_t,
        ),
        name="mlp_pass",
    )(x, attn_out, vectors, cot, fc1.reshape(n_t, 1, w), weights, weights)


def body(cfg, tokens, counts, gains, biases, fc1_bias, w_qkv, w_o, w_1, w_2, cotangent):
    pd, f2, hc = cfg.pd, cfg.f2, cfg.hc
    halves = jnp.stack(
        [
            jnp.concatenate(
                [
                    w_qkv.reshape(pd, 3, 2, hc).transpose(2, 0, 1, 3).reshape(2, pd, 3 * hc),
                    w_o.T.reshape(pd, 2, hc).transpose(1, 0, 2),
                ],
                axis=2,
            ),
            w_1.reshape(pd, 2, f2).transpose(1, 0, 2),
            w_2.T.reshape(pd, 2, f2).transpose(1, 0, 2),
        ],
        axis=1,
    )
    small = jnp.concatenate([gains, biases, fc1_bias.reshape(4, -1)])
    small = jnp.pad(small, ((0, 4), (0, 128 - small.shape[1])))

    x, cot, attn_in, qkv, attended, lse, attn_out, vectors, fc1, attn_w, mlp_w = gather_and_attend(
        counts, tokens, cotangent, small, halves, cfg
    )
    fc1_sums, mlp_grads, residual, grad_hidden, sums, mixed = mlp_pass(
        x, attn_out, vectors, cot, fc1, mlp_w, cfg
    )
    both, mixed, d_tokens, small = reduce_and_attend_back(
        counts, grad_hidden, attn_in, qkv, attended, lse, attn_w, mlp_grads, residual, x, mixed, vectors, sums,
        fc1_sums, cfg,
    )
    d_qkv = both[:, 0, :, : 3 * hc].reshape(2, pd, 3, hc).transpose(1, 2, 0, 3).reshape(pd, 3, 2 * hc)
    d_o = both[:, 0, :, 3 * hc :].transpose(0, 2, 1).reshape(2 * hc, pd)
    d_1 = both[:, 1].transpose(1, 0, 2).reshape(pd, 2 * f2)
    d_2 = both[:, 2].transpose(0, 2, 1).reshape(2 * f2, pd)
    piece = D // (cfg.n_dp * cfg.n_t)
    small = small[:, :piece]
    return (
        mixed,
        d_tokens,
        d_qkv,
        d_o,
        d_1,
        d_2,
        small[:2],
        small[2:8],
        small[8:12].reshape(-1),
    )


def solution(mesh):
    n_dp, n_t = mesh.shape["dp"], mesh.shape["tensor"]
    split = Mesh(mesh.devices.reshape(n_dp // 2, 2, n_t), ALL)

    def program(tokens, *rest):
        cfg = Cfg(n_dp, n_t, tokens.shape[0])
        return body(cfg, tokens, *rest)

    dp = ("p", "c")
    return jax.shard_map(
        program,
        mesh=split,
        in_specs=(
            P(ALL, None),
            P(dp, None),
            P(None, ALL),
            P(None, ALL),
            P(ALL),
            P(dp, None, "t"),
            P("t", dp),
            P(dp, "t"),
            P("t", dp),
            P(ALL, None),
        ),
        out_specs=(
            P(ALL, None),
            P(ALL, None),
            P(dp, None, "t"),
            P("t", dp),
            P(dp, "t"),
            P("t", dp),
            P(None, ALL),
            P(None, ALL),
            P(ALL),
        ),
        check_vma=False,
    )
```

time: 1850 us -> 610 us (0.33)
  waiting for transfers between devices: 1060 us -> 0 us
  Pallas kernels: 0 us -> 575 us
  blocking collectives: 234 us -> 0 us
  matrix products: 221 us -> 0 us
  local copies, waits for them, and re-layouts: 237 us -> 23.6 us
  other arithmetic: 74.7 us -> 2.61 us
    reduce_scatter x8 -> x0, waiting for transfers between devices: 650 us -> none  [the longest x1 218 us: body(): lax.psum_scatter(jnp.dot(expand(attended, block_rows * lax.axis_size('ten...]
    pallas_call x0 -> x3, Pallas kernels: none -> 575 us  [the longest x1 247 us: reduce_and_attend_back(): pl.pallas_call(kernel, grid=(n_t,), in_specs=[pl.BlockSpec(memory_space=p...]
    all_gather x7 -> x0, waiting for transfers between devices: 410 us -> none  [the longest x1 106 us: body(): lax.all_gather(attn_norm.astype(jnp.bfloat16), 'tensor', axis=0, tiled=True)]
    dot_general x40 -> x0, matrix products: 221 us -> none  [the longest x1 32.8 us: body(): jnp.dot(mlp_in, first_all, preferred_element_type=jnp.float32) + fc1_cols]
    all_gather x3 -> x0, blocking collectives: 146 us -> none  [the longest x1 71 us: body(): lax.all_gather(biases, ('dp', 'tensor'), axis=1, tiled=True)]
    gather x8 -> x0, local copies, waits for them, and re-layouts: 129 us -> none  [the longest x4 62.6 us: expand(): picked = jnp.take(compact, places, axis=0)]
    unnamed x2 -> x0, blocking collectives: 88.8 us -> none
    another operation x20 -> x1, local copies, waits for them, and re-layouts: 35.2 us -> 0.07 us  [body(): jnp.stack([jnp.concatenate([w_qkv.reshape(pd, 3, 2, hc).transpose(2, 0, 1...]
  transfers between devices with their start and end apart: 15 -> 0, of which waited for: 12 -> 0; matrix products, arithmetic and copies ran while one was open for 19% -> 0% of each run, Pallas kernels for 0% -> 0%
where the time goes in v3:
time: 610 us; the launch traced here: 602 us
  Pallas kernels  575 us (94%)
  local copies, waits for them, and re-layouts  23.6 us (4%)
    pallas_call x1, Pallas kernels, reduce_and_attend_back(): pl.pallas_call(kernel, grid=(n_t,), in_specs=[pl.BlockSpec(memory_space=p...  247 us
    pallas_call x1, Pallas kernels, gather_and_attend(): pl.pallas_call(kernel, in_specs=[smem, vmem, vmem, vmem, anywhere], out_s...  240 us
    pallas_call x1, Pallas kernels, mlp_pass(): pl.pallas_call(kernel, grid=(n_t,), in_specs=[own, pl.BlockSpec(memory_sp...  88.3 us

profile of v3, /device:TPU:0, one launch (start us, length us, event | category | flops | bytes accessed | tf_op | source)
XLA Modules:
  0.0 602.5 jit_solution(11746013364068555341)
XLA Ops:
  0.6 0.0 copy-start.2
  0.7 0.0 copy-start.3
  0.7 0.8 reshape.57
  1.5 1.3 select_maximum_fusion.small_ref
  2.8 1.0 reshape.60
  3.8 1.2 reshape.58
  5.0 0.9 copy.30
  5.9 0.2 copy.32
  6.1 0.1 maximum_bitcast_fusion
  6.2 0.0 copy-done.2
  6.2 0.0 copy-done.3
  6.2 0.1 bitcast_bitcast_fusion
  6.3 1.2 pad_maximum_fusion.half_ref
  7.5 239.9 %gather_and_attend.1 = (bf16[4,272,1280]{2,1,0:T(8,128)(2,1)}, bf16[4,272,1280]{2,1,0:T(8,128)(2,1)}, bf16[4,272,1280]{2,1,0:T(8,128)(2,1)}, bf16[4,4,272,480]{3...) custom-call(s32[1,4]{1,0:T(1,128)} %counts_ref.3, ...), custom_call_target="tpu_custom_call" | custom-call | flops 7130316800 | bytes 23265280 | tf_op jit(solution)/shard_map/gather_and_attend/pallas_call | solution.py:428
  247.4 1.3 reshape.63.fc1_ref
  248.7 88.3 %mlp_pass.1 = (f32[4,1,640]{2,1,0:T(1,128)}, bf16[4,4,2,320,640]{4,3,2,1,0:T(8,128)(2,1)}, f32[2,272,1280]{2,1,0:T(8,128)}, bf16[4,272,1280]{2,1,0:T(8,128)(2,1)...) custom-call(bf16[4,272,1280]{2,1,0:T(8,128)(2,1)} %get-tuple-element.30.x_ref, ...), custom_call_target="tpu_custom_call" | custom-call | flops 42781900800 | bytes 42926080 | tf_op jit(solution)/shard_map/mlp_pass/pallas_call | solution.py:1098
  337.0 246.9 %reduce_and_attend_back.1 = (f32[2,3,160,640]{3,2,1,0:T(8,128)}, bf16[648,1280]{1,0:T(8,128)(2,1)}, bf16[648,1280]{1,0:T(8,128)(2,1)}, f32[16,128]{1,0:T(8,128)}...) custom-call(s32[1,4]{1,0:T(1,128)} %counts_ref.3, ...), custom_call_target="tpu_custom_call" | custom-call | flops 16154624000 | bytes 40960000 | tf_op jit(solution)/shard_map/reduce_and_attend_back/pallas_call | solution.py:892
  583.9 0.0 copy-start
  583.9 1.4 slice.29
  585.3 0.7 slice.31
  586.0 1.3 slice.30
  587.2 0.6 reshape.69
  587.9 1.1 slice_bitcast_fusion.2
  589.0 0.3 copy.37
  589.3 1.0 reshape.66
  590.2 2.0 slice.25
  592.2 0.0 copy-done
  592.2 0.1 slice_bitcast_fusion
  592.3 0.9 copy.43
  593.3 1.4 copy.35
  594.7 0.9 copy.36
  595.6 1.7 reshape.65
  597.3 0.0 copy-start.1
  597.3 0.9 copy.42
  598.2 2.7 copy.50
  600.9 0.0 copy-done.1
  600.9 1.2 copy.51
  (1 shorter events, 0.0 us)
Async XLA Ops:
  0.6 5.6 copy-start.2
  0.7 5.6 copy-start.3
  583.9 8.3 %copy-start = (f32[2,3,160,640]{3,2,1,0:T(8,128)S(1)}, f32[2,3,160,640]{3,2,1,0:T(8,128)}, u32[]{:S(2)}) copy-start(f32[2,3,160,640]{3,2,1,0:T(8,128)} %get-tuple-element.49) | copy-start | bytes 7372804
  597.3 3.7 copy-start.1

commit v4 on v3

--- a/solution.py
+++ b/solution.py
@@ -36,6 +36,7 @@
         self.hc = self.hh * HD
         self.f2 = FF // n_t // 2
         assert 4 * self.hc == self.f2
+        self.early = n_t // 2
         self.caps = self._caps()
 
     def _caps(self):
@@ -108,13 +109,6 @@
     pl.semaphore_wait(barrier, len(found))
 
 
-def greet_pair():
-    barrier = pltpu.get_barrier_semaphore()
-    other = {"c": 1 - lax.axis_index("c")}
-    pl.semaphore_signal(barrier, inc=1, device_id=other, device_id_type=MESH)
-    pl.semaphore_wait(barrier, 1)
-
-
 def remote(source, target, sems, index, device):
     return pltpu.make_async_remote_copy(
         src_ref=source,
@@ -170,9 +164,9 @@
 
     def kernel(
         counts_ref, tok_ref, ct_ref, small_ref, half_ref,
-        x_ref, cot_ref, in_ref, qkv_ref, att_ref, lse_ref, out_ref, vec_ref, fc1_ref, g0_ref, g_ref,
-        w, sent, got, parts, q_bias, v_bias,
-        z_send, z_recv, p_send, p_recv, r_send, r_recv, c_send, c_recv, v_send, v_recv, own_sem, out_sem,
+        x_out, cot_out, in_out, qkv_out, att_out, lse_out, hidden_out, mlp_out, vec_ref, fc1_ref, g0_ref, g_ref,
+        x_ref, cot_ref, in_ref, qkv_ref, att_ref, lse_ref, out_ref, other, mlp_in, w, sent, got, parts, q_bias, v_bias,
+        z_send, z_recv, p_send, p_recv, r_send, r_recv, c_send, c_recv, v_send, v_recv, own_sem, out_sem, image_sem,
     ):
         p, core, z = (lax.axis_index(axis) for axis in ALL)
         layout = Layout(counts_ref, cfg)
@@ -230,12 +224,13 @@
             trade(group).wait()
 
         def send_p(group, k):
-            if k > 0:
-                z_copy(group, k).wait_recv()
-            if k + 1 < n_t:
-                z_copy(group, k + 1).start()
             for mask in direct:
                 p_copy(group, k, mask).start()
+
+        def send_z(group, k):
+            if k > 1:
+                z_copy(group, k - 1).wait_recv()
+            z_copy(group, k).start()
 
         def send_d(group, k):
             for mask in direct:
@@ -243,15 +238,15 @@
             for copy in d_copies(group, k):
                 copy.start()
 
-        def finish(group):
-            for k in range(n_t):
+        def finish(group, chunks):
+            for k in chunks:
                 for copy in d_copies(group, k):
                     copy.wait_recv()
                     copy.wait_send()
                 for mask in direct:
                     p_copy(group, k, mask).wait_send()
-                if k > 0:
-                    z_copy(group, k).wait_send()
+            for k in range(1, n_t if group == 0 else cfg.early + 1):
+                z_copy(group, k).wait_send()
 
         def row_copy(which, s):
             shift, size = caps[s]
@@ -350,36 +345,68 @@
         send_rows(0, tok_ref)
         have_own(0)
         send_p(0, 0)
+        send_z(0, 1)
+        have_own(1)
+        send_p(1, 0)
         part_stage(1)
-        send_rows(1, ct_ref)
+        send_d(0, 0)
         part_stage(2)
-        send_p(0, 1)
-        send_d(0, 0)
         take_rows(0, tok_ref, x_ref)
         pair_rows(0, x_ref).start()
-        have_own(1)
-        part_stage(3)
-        spread()
-        for k in range(2, n_t):
+        z_last = n_t - 1
+        for k in range(1, n_t):
+            if k < z_last:
+                send_z(0, k + 1)
+            else:
+                z_copy(0, k).wait_recv()
+            if k == z_last - 1:
+                send_z(1, 1)
             send_p(0, k)
-            send_d(0, k - 1)
-        send_p(1, 0)
-        take_rows(1, ct_ref, cot_ref)
-        pair_rows(1, cot_ref).start()
-        send_d(0, n_t - 1)
+            if k == 1:
+                send_d(1, 0)
+                part_stage(3)
+                spread()
+            else:
+                send_d(0, k - 1)
+        send_d(0, z_last)
+        steps = []
+        for k in range(1, cfg.early + 1):
+            if k < cfg.early:
+                steps.append(lambda k=k: send_z(1, k + 1))
+                steps.append(lambda k=k: send_p(1, k))
+            else:
+                steps.append(lambda k=k: z_copy(1, k).wait_recv())
+            if k > 1:
+                steps.append(lambda k=k: send_d(1, k - 1))
+        for step in steps[:2]:
+            step()
+        steps = steps[2:]
+        send_rows(1, ct_ref)
         pair_rows(0, x_ref).wait()
-        finish(0)
-        kept = pltpu.make_async_copy(w, g0_ref, out_sem)
+        finish(0, range(n_t))
+        kept = pltpu.make_async_copy(w, g0_ref, out_sem.at[0])
         kept.start()
-
-        steps = []
-        for k in range(1, n_t):
-            steps += [lambda k=k: send_p(1, k), lambda k=k: send_d(1, k - 1)]
-        steps.append(lambda: send_d(1, n_t - 1))
-        early = 2 * len(steps) // 5
+        x_copy = pltpu.make_async_copy(x_ref, x_out, out_sem.at[1])
+        x_copy.start()
+        early = len(steps)
+
+        def image_copies(i):
+            return [
+                pltpu.make_async_copy(in_ref.at[i], in_out.at[i], image_sem.at[0, i]),
+                pltpu.make_async_copy(qkv_ref.at[:, i], qkv_out.at[:, i], image_sem.at[1, i]),
+                pltpu.make_async_copy(att_ref.at[:, i], att_out.at[:, i], image_sem.at[2, i]),
+                pltpu.make_async_copy(lse_ref.at[:, i], lse_out.at[:, i], image_sem.at[3, i]),
+            ]
+
         keyed = lax.broadcasted_iota(jnp.int32, (PT, PT), 1) < TOK_IMG
 
-        def image(i, carry):
+        mine, theirs = pl.ds(0, imgs), pl.ds(imgs, imgs)
+
+        def out_copy():
+            return remote(out_ref.at[theirs], other, (c_send, c_recv), 4, pair)
+
+        def image(turn, carry):
+            i = lax.rem(turn + imgs, ni)
             normed, _ = norm(x_ref[i].astype(F32))
             attn_in = (normed * vec_ref[0:1, :] + vec_ref[2:3, :]).astype(BF16)
             in_ref[i] = attn_in
@@ -406,20 +433,49 @@
                     out_ref[i] = part
                 else:
                     out_ref[i] += part
+            for copy in image_copies(i):
+                copy.start()
+
+            @pl.when(turn == imgs - 1)
+            def _():
+                out_copy().start()
+
             for j in range(early):
 
-                @pl.when(i == (j + 1) * ni // early - 1)
+                @pl.when(turn == min(j, ni - 1))
                 def _(j=j):
                     steps[j]()
 
             return carry
 
         lax.fori_loop(0, ni, image, 0)
+        out_copy().wait()
+        for i in range(imgs):
+            hidden = x_ref[i].astype(F32) + (out_ref[i] + other[i]) + vec_ref[6:7, :]
+            out_ref[i] = hidden
+            normed, _ = norm(hidden)
+            mlp_in[i] = (normed * vec_ref[1:2, :] + vec_ref[3:4, :]).astype(BF16)
+        in_copy = remote(mlp_in.at[mine], mlp_in.at[theirs], (c_send, c_recv), 5, pair)
+        in_copy.start()
+        hidden_copy = pltpu.make_async_copy(out_ref.at[mine], hidden_out, out_sem.at[3])
+        hidden_copy.start()
+        take_rows(1, ct_ref, cot_ref)
+        pair_rows(1, cot_ref).start()
+        in_copy.wait()
+        mlp_copy = pltpu.make_async_copy(mlp_in, mlp_out, out_sem.at[4])
+        mlp_copy.start()
+        finish(1, range(cfg.early))
         pair_rows(1, cot_ref).wait()
-        for step in steps[early:]:
-            step()
-        finish(1)
+        cot_copy = pltpu.make_async_copy(cot_ref, cot_out, out_sem.at[2])
+        cot_copy.start()
         kept.wait()
+        x_copy.wait()
+        hidden_copy.wait()
+        mlp_copy.wait()
+        for i in range(ni):
+            for copy in image_copies(i):
+                copy.wait()
+        cot_copy.wait()
 
     vmem = pl.BlockSpec(memory_space=pltpu.VMEM)
     smem = pl.BlockSpec(memory_space=pltpu.SMEM)
@@ -428,7 +484,7 @@
     return pl.pallas_call(
         kernel,
         in_specs=[smem, vmem, vmem, vmem, anywhere],
-        out_specs=[vmem] * 9 + [anywhere] * 2,
+        out_specs=[anywhere] * 8 + [vmem] * 2 + [anywhere] * 2,
         out_shape=[
             jax.ShapeDtypeStruct((ni, PT, D), BF16),
             jax.ShapeDtypeStruct((ni, PT, D), BF16),
@@ -436,13 +492,23 @@
             jax.ShapeDtypeStruct((n_t, ni, PT, 3 * hc), BF16),
             jax.ShapeDtypeStruct((n_t, ni, PT, hc), BF16),
             jax.ShapeDtypeStruct((n_t, ni, PT, hh), F32),
-            jax.ShapeDtypeStruct((ni, PT, D), F32),
+            jax.ShapeDtypeStruct((imgs, PT, D), F32),
+            jax.ShapeDtypeStruct((ni, PT, D), BF16),
             jax.ShapeDtypeStruct((8, D), F32),
             jax.ShapeDtypeStruct((n_t, f2), F32),
             jax.ShapeDtypeStruct((n_t, D, f2), BF16),
             jax.ShapeDtypeStruct((2, n_t, D, f2), BF16),
         ],
         scratch_shapes=[
+            pltpu.VMEM((ni, PT, D), BF16),
+            pltpu.VMEM((ni, PT, D), BF16),
+            pltpu.VMEM((ni, PT, D), BF16),
+            pltpu.VMEM((n_t, ni, PT, 3 * hc), BF16),
+            pltpu.VMEM((n_t, ni, PT, hc), BF16),
+            pltpu.VMEM((n_t, ni, PT, hh), F32),
+            pltpu.VMEM((ni, PT, D), F32),
+            pltpu.VMEM((imgs, PT, D), F32),
+            pltpu.VMEM((ni, PT, D), BF16),
             pltpu.VMEM((n_t, D, f2), BF16),
             pltpu.VMEM((2, len(caps), widest, D), BF16),
             pltpu.VMEM((2, len(caps), widest, D), BF16),
@@ -455,12 +521,13 @@
             dma((2, n_t, n_p)),
             dma((2, len(caps))),
             dma((2, len(caps))),
-            dma((4,)),
-            dma((4,)),
+            dma((6,)),
+            dma((6,)),
             dma((n_t + n_p,)),
             dma((n_t + n_p,)),
             dma((2,)),
-            dma,
+            dma((5,)),
+            dma((4, ni)),
         ],
         compiler_params=params(collective_id=0, has_side_effects=True),
         cost_estimate=pl.CostEstimate(
@@ -481,7 +548,9 @@
     scale = HD**-0.5
     square = n_p == 4
     plane = (2, 2) if square else (n_p,)
-    jobs = [((k, k), k) for k in range(n_t)] + [((k, k + 1), None) for k in range(0, n_t, 2)]
+    order = list(range(n_t))[::-1]
+    jobs = [((k, k), k) for k in order[:-1]]
+    jobs += [((k, k - 1), None) for k in order[::2]] + [((0, 0), 0)]
     n_jobs = len(jobs)
     n_got = 2 if square else n_p - 1
     n_dev = 2 * n_p * n_t
@@ -498,7 +567,7 @@
         counts_ref, gh_ref, in_ref, qkv_ref, att_ref, lse_ref, w_ref, g_ref, res_ref, x_ref, mix_ref, vec_ref,
         sums_ref, fsum_ref,
         half_ref, mixed_ref, dtok_ref, small_ref, own_grads, rows_got, in_other, got_z,
-        gqkv, stage, held, got, got_2, total, out, dq, dv,
+        gqkv, stage, held, got, got_2, got_step, total, out, dq, dv,
         images, sent, taken, block, res_in, other_in, parts, parts_p, parts_c, parts_t,
         stage_sem, held_sem, s_send, s_recv, t_send, t_recv, z_send, z_recv, r_send, r_recv, c_send, c_recv,
         v_send, v_recv, in_sem, out_sem,
@@ -540,6 +609,9 @@
             source = got.at[n, part, (py, px)[part] if square else 0]
             target = {"t": lax.rem(z - k + n_t, n_t)}
             index = to_z[n, part]
+            if jobs[n][1] is not None:
+                target = {"t": lax.rem(z - 1 + n_t, n_t)}
+                return remote(source, got_step.at[index], (z_send, z_recv), index, target)
             return remote(source, got_z.at[index], (z_send, z_recv), index, target)
 
         def loads(n):
@@ -587,6 +659,10 @@
                     whole = held[n % 2, part, 0].astype(F32)
                     for q in range(n_p - 1):
                         whole = whole + got[n, part, q].astype(F32)
+                if k is not None and k < n_t - 1:
+                    before = n - 1 if k > 0 else n_t - 2
+                    z_copy(before, part).wait_recv()
+                    whole = whole + got_step[to_z[before, part]].astype(F32)
                 if chunks[part] == 0:
                     total[0 if k is None else 1 + part] = whole
                 else:
@@ -602,9 +678,6 @@
             if n + 2 < n_jobs:
                 begin(n + 2)
 
-        def stage_copy(k):
-            return pltpu.make_async_copy(stage, own_grads.at[k], stage_sem)
-
         def finish():
             last(n_jobs - 1)
             for n in range(n_jobs):
@@ -612,21 +685,22 @@
                     copy.wait_send()
                 for part in range(2):
                     if (n, part) in to_z:
-                        z_copy(n, part).wait()
+                        z_copy(n, part).wait_send()
+                        if jobs[n][1] is None:
+                            z_copy(n, part).wait_recv()
+            direct = [(n, part) for n, part in to_z if jobs[n][1] is None]
             reads = [
-                pltpu.make_async_copy(got_z.at[index], got.at[n, part, 0], z_recv.at[index])
-                for (n, part), index in to_z.items()
+                pltpu.make_async_copy(got_z.at[to_z[spot]], got.at[(*spot, 0)], z_recv.at[to_z[spot]])
+                for spot in direct
             ]
             for read in reads:
                 read.start()
             for read in reads:
                 read.wait()
-            for unit in range(3):
-                whole = total[unit]
-                for n, part in to_z:
-                    if unit == (0 if jobs[n][1] is None else 1 + part):
-                        whole = whole + got[n, part, 0].astype(F32)
-                total[unit] = whole
+            whole = total[0]
+            for spot in direct:
+                whole = whole + got[(*spot, 0)].astype(F32)
+            total[0] = whole
 
             def rows(member):
                 return total.at[:, pl.ds(pl.multiple_of(member * pd, 16), pd), :]
@@ -835,28 +909,28 @@
                     def _(n=n):
                         tick(n)
 
-        dq[pl.ds(step, 1), :] = total_q
-        dv[pl.ds(step, 1), :] = total_v
+        dq[pl.ds(n_t - 1 - step, 1), :] = total_q
+        dv[pl.ds(n_t - 1 - step, 1), :] = total_v
 
         @pl.when(step == n_t - 1)
         def _():
             in_copy().start()
 
-        left = dot_tn(in_ref[...].reshape(m, D), gqkv[...].reshape(m, 3 * hc)).astype(BF16)
-        right = dot_tn(gh_ref[...].reshape(m, D), att_ref[0].reshape(m, hc)).astype(BF16)
-
-        @pl.when(step > 0)
-        def _():
-            stage_copy(0).wait()
-
-        ahead = [slice(None)] * (len(plane) + 1)
-        stage[(*ahead, slice(0, 3 * hc))] = left.reshape((*plane, 2 * pd, 3 * hc))
-        stage[(*ahead, slice(3 * hc, f2))] = right.reshape((*plane, 2 * pd, hc))
-        for k in range(n_t):
-
-            @pl.when(step == k)
-            def _(k=k):
-                stage_copy(k).start()
+        for side in range(2):
+            cols = slice(side * D // 2, (side + 1) * D // 2)
+            ahead = (side,) if square else (slice(side * n_p // 2, (side + 1) * n_p // 2),)
+            ahead = ahead + (slice(None),) * len(plane)
+            for lhs, rhs, lanes in (
+                (in_ref, gqkv[...].reshape(m, 3 * hc), slice(0, 3 * hc)),
+                (gh_ref, att_ref[0].reshape(m, hc), slice(3 * hc, f2)),
+            ):
+                value = dot_tn(lhs[:, :, cols].reshape(m, D // 2), rhs).astype(BF16)
+                stage[(*ahead, lanes)] = value.reshape(
+                    (n_p // 2, 2 * pd, lanes.stop - lanes.start)
+                )
+        store = pltpu.make_async_copy(stage, own_grads.at[n_t - 1 - step], stage_sem)
+        store.start()
+        store.wait()
 
         @pl.when(step == n_t - 2)
         def _():
@@ -864,7 +938,6 @@
 
         @pl.when(step == n_t - 1)
         def _():
-            stage_copy(0).wait()
             tick(n_t - 2)
             first_norm_back()
             send_rows(1)
@@ -874,8 +947,8 @@
             for n in range(n_t, n_jobs - 1):
                 tick(n)
             part_hop(2)
+            tick(n_jobs - 1)
             take_rows(1, dtok_ref)
-            tick(n_jobs - 1)
             part_hop(3)
             finish()
 
@@ -884,7 +957,7 @@
     vmem = pltpu.VMEM
 
     def chunk_block(last):
-        return pl.BlockSpec((1, ni, PT, last), lambda k: (k, 0, 0, 0))
+        return pl.BlockSpec((1, ni, PT, last), lambda k: (n_t - 1 - k, 0, 0, 0))
 
     anywhere = pl.BlockSpec(memory_space=pl.ANY)
     shape = jax.ShapeDtypeStruct
@@ -899,7 +972,7 @@
             chunk_block(3 * hc),
             chunk_block(hc),
             chunk_block(hh),
-            pl.BlockSpec((1, D, f2), lambda k: (k, 0, 0)),
+            pl.BlockSpec((1, D, f2), lambda k: (n_t - 1 - k, 0, 0)),
             anywhere,
             anywhere,
             anywhere,
@@ -925,6 +998,7 @@
             vmem((2, 2, 2 if square else 1, *chunk), BF16),
             vmem((n_jobs, 2, n_got, *chunk), BF16),
             vmem((n_jobs, 2, *(chunk if square else (16, 128))), BF16),
+            vmem((2 * (n_t - 1), *chunk), BF16),
             vmem((3, *chunk), F32),
             vmem((ni, PT, D), F32),
             vmem((n_t, hc), F32),
@@ -982,57 +1056,125 @@
     return outs[:4]
 
 
-def mlp_pass(x, attn_out, vectors, cot, fc1, weights, cfg):
+def mlp_pass(hidden, mlp_in, vectors, cot, fc1, weights, cfg):
     n_p, n_t, m, pd, w, ni, imgs = cfg.n_p, cfg.n_t, cfg.m, cfg.pd, cfg.f2, cfg.ni, cfg.imgs
+    early = cfg.early
 
     def kernel(
-        x_ref, outs_ref, vec_ref, cot_ref, fc1_ref, w1_ref, w2_ref,
-        sum_ref, grad_ref, res_ref, gh_ref, sums_ref, mixed_ref,
-        other, other_y, mlp_in, act_all, gpre_all, back, y, gh, c_send, c_recv, own_sem,
+        hidden_ref, mlp_in, vec_ref, cot_ref, fc1_ref, g_ref,
+        sum_ref, grad_ref, res_ref, gh_ref, sums_ref, mixed_ref, late_ref,
+        other, other_y, act_all, gpre_all, back, y, gh, w_all,
+        c_send, c_recv, own_sem, load_sem, keep_sem, z_send, z_recv, p_send, p_recv,
     ):
         step = pl.program_id(0)
+        p, z = lax.axis_index("p"), lax.axis_index("t")
         pair = {"c": 1 - lax.axis_index("c")}
+
+        def rows(mask):
+            return pl.ds(pl.multiple_of((p ^ mask) * 2 * pd, 16), 2 * pd)
+
+        def own_rows(j):
+            return g_ref.at[:, early, rows(0), :] if j == 0 else late_ref.at[:, j, rows(0), :]
+
+        def keep():
+            return pltpu.make_async_copy(own_rows(0), late_ref.at[:, 0, rows(0), :], keep_sem)
+
+        def z_copy(j):
+            target = {"t": lax.rem(z + 1, n_t)}
+            return remote(own_rows(j - 1), own_rows(j), (z_send, z_recv), j, target)
+
+        def p_copy(j, mask):
+            target = late_ref.at[:, j, rows(0), :]
+            return remote(own_rows(j), target, (p_send, p_recv), (j, mask), {"p": p ^ mask})
+
+        def d_copies(j):
+            if n_p != 4:
+                return []
+            ref_1, ref_2 = late_ref.at[0, j, rows(1), :], late_ref.at[1, j, rows(2), :]
+            return [
+                remote(ref_1, ref_1, (p_send, p_recv), (j, 3), {"p": p ^ 2}),
+                remote(ref_2, ref_2, (p_send, p_recv), (j, 0), {"p": p ^ 1}),
+            ]
+
+        direct = (1, 2) if n_p == 4 else tuple(range(1, n_p))
+
+        def send_p(j):
+            if j > 0:
+                z_copy(j).wait_recv()
+            if early + j + 1 < n_t:
+                z_copy(j + 1).start()
+            for mask in direct:
+                p_copy(j, mask).start()
+
+        def send_d(j):
+            for mask in direct:
+                p_copy(j, mask).wait_recv()
+            for copy in d_copies(j):
+                copy.start()
+            if early + j + 1 < n_t:
+                send_p(j + 1)
+
+        def complete(j):
+            if j == 0:
+                keep().wait()
+            for copy in d_copies(j):
+                copy.wait_recv()
+
+        def load(k):
+            source = g_ref.at[:, k] if k < early else late_ref.at[:, k - early]
+            return pltpu.make_async_copy(source, w_all.at[k % 2], load_sem.at[k % 2])
         mine, theirs = pl.ds(0, imgs), pl.ds(imgs, imgs)
 
         def pair_copy(index, source, target):
             return remote(source, target, (c_send, c_recv), index, pair)
 
         def back_copy():
-            return pair_copy(2, back.at[theirs], other)
+            return pair_copy(0, back.at[theirs], other)
 
         def y_copy():
-            return pair_copy(3, y.at[theirs], other_y)
+            return pair_copy(1, y.at[theirs], other_y)
 
         @pl.when(step == 0)
         def _():
-            own_part = pltpu.make_async_copy(outs_ref.at[mine], res_ref, own_sem)
-            own_part.start()
-            greet_pair()
-            out_copy = pair_copy(0, outs_ref.at[theirs], other)
-            out_copy.start()
-            own_part.wait()
-            out_copy.wait()
-            for i in range(imgs):
-                value = x_ref[i].astype(F32) + (res_ref[i] + other[i]) + vec_ref[6:7, :]
-                res_ref[i] = value
-                normed, _ = norm(value)
-                mlp_in[i] = (normed * vec_ref[1:2, :] + vec_ref[3:4, :]).astype(BF16)
-            in_copy = pair_copy(1, mlp_in.at[mine], mlp_in.at[theirs])
-            in_copy.start()
-            in_copy.wait()
-
-        w1, w2 = w1_ref[0, 0], w2_ref[0, 0]
+            pltpu.make_async_copy(hidden_ref, res_ref, own_sem).start()
+            keep().start()
+            for k in range(min(2, early)):
+                load(k).start()
+            enter(cfg)
+            send_p(0)
+        slot = lax.rem(step, 2)
+        for k in range(n_t):
+
+            @pl.when(step == k)
+            def _(k=k):
+                load(k).wait()
+
+        w1, w2 = w_all[slot, 0], w_all[slot, 1]
         total = jnp.zeros((1, w), F32)
         for i in range(ni):
-            rows = slice(i * PT, (i + 1) * PT)
+            rows_i = slice(i * PT, (i + 1) * PT)
             pre = dot(mlp_in[i], w1) + fc1_ref[0]
             phi = 0.5 * (1.0 + lax.erf(pre * (1.0 / math.sqrt(2.0))))
-            act_all[rows, :] = (pre * phi).astype(BF16)
+            act_all[rows_i, :] = (pre * phi).astype(BF16)
             slope = phi + pre * jnp.exp(-0.5 * pre * pre) * (1.0 / math.sqrt(2.0 * math.pi))
             gpre = dot(cot_ref[i], w2) * slope
             total = total + jnp.sum(gpre, axis=0, keepdims=True)
-            gpre_all[rows, :] = gpre.astype(BF16)
+            gpre_all[rows_i, :] = gpre.astype(BF16)
+            if i == min(1, ni - 1):
+                for j in range(n_t - early):
+
+                    @pl.when(step == j)
+                    def _(j=j):
+                        send_d(j)
+
         sum_ref[0] = total
+        for k in range(2, n_t):
+
+            @pl.when(step == k - 1)
+            def _(k=k):
+                if k >= early:
+                    complete(k - early)
+                load(k).start()
 
         def add(target, left, right):
             value = dot_nt(left, right).reshape(ni, PT, D)
@@ -1064,6 +1206,7 @@
 
         @pl.when(step == n_t - 1)
         def _():
+            pltpu.make_async_copy(hidden_ref, res_ref, own_sem).wait()
             back_copy().wait()
             sums = [jnp.zeros((1, D), F32)] * 4
             for i in range(imgs):
@@ -1077,7 +1220,7 @@
                 gh[i] = grad.astype(BF16)
                 terms = (up * normed, up, grad, cot_f)
                 sums = [s + jnp.sum(t, axis=0, keepdims=True) for s, t in zip(sums, terms)]
-            grad_copy = pair_copy(4, gh.at[mine], gh.at[theirs])
+            grad_copy = pair_copy(2, gh.at[mine], gh.at[theirs])
             grad_copy.start()
             for r in range(4):
                 sums_ref[r : r + 1, :] = sums[r]
@@ -1087,10 +1230,14 @@
             grad_copy.wait()
             store = pltpu.make_async_copy(gh, gh_ref, own_sem)
             store.start()
+            for j in range(n_t - early):
+                for copy in d_copies(j):
+                    copy.wait_send()
+                for mask in direct:
+                    p_copy(j, mask).wait_send()
+                if j > 0:
+                    z_copy(j).wait_send()
             store.wait()
-
-    def half_spec(unit):
-        return pl.BlockSpec((1, 1, D, w), lambda i: (unit, i, 0, 0))
 
     full = fixed((ni, PT, D))
     own = fixed((imgs, PT, D))
@@ -1099,13 +1246,12 @@
         kernel,
         grid=(n_t,),
         in_specs=[
-            own,
             pl.BlockSpec(memory_space=pl.ANY),
+            full,
             fixed((8, D)),
             full,
             pl.BlockSpec((1, 1, w), lambda i: (i, 0, 0)),
-            half_spec(0),
-            half_spec(1),
+            pl.BlockSpec(memory_space=pl.ANY),
         ],
         out_specs=[
             pl.BlockSpec((1, 1, w), lambda i: (i, 0, 0)),
@@ -1114,6 +1260,7 @@
             pl.BlockSpec(memory_space=pl.ANY),
             fixed((4, D)),
             own,
+            pl.BlockSpec(memory_space=pl.ANY),
         ],
         out_shape=[
             shape((n_t, 1, w), F32),
@@ -1122,19 +1269,26 @@
             shape((ni, PT, D), BF16),
             shape((4, D), F32),
             shape((imgs, PT, D), BF16),
+            shape((2, n_t - early, D, w), BF16),
         ],
         scratch_shapes=[
             vmem((imgs, PT, D), F32),
             vmem((imgs, PT, D), F32),
-            vmem((ni, PT, D), BF16),
             vmem((m, w), BF16),
             vmem((m, w), BF16),
             vmem((ni, PT, D), F32),
             vmem((ni, PT, D), F32),
             vmem((ni, PT, D), BF16),
-            dma((5,)),
-            dma((5,)),
+            vmem((2, 2, D, w), BF16),
+            dma((3,)),
+            dma((3,)),
             dma,
+            dma((2,)),
+            dma,
+            dma((n_t - early,)),
+            dma((n_t - early,)),
+            dma((n_t - early, n_p)),
+            dma((n_t - early, n_p)),
         ],
         compiler_params=params(collective_id=2, has_side_effects=True),
         cost_estimate=pl.CostEstimate(
@@ -1143,7 +1297,7 @@
             transcendentals=2 * m * w * n_t,
         ),
         name="mlp_pass",
-    )(x, attn_out, vectors, cot, fc1.reshape(n_t, 1, w), weights, weights)
+    )(hidden, mlp_in, vectors, cot, fc1.reshape(n_t, 1, w), weights)[:-1]
 
 
 def body(cfg, tokens, counts, gains, biases, fc1_bias, w_qkv, w_o, w_1, w_2, cotangent):
@@ -1165,11 +1319,11 @@
     small = jnp.concatenate([gains, biases, fc1_bias.reshape(4, -1)])
     small = jnp.pad(small, ((0, 4), (0, 128 - small.shape[1])))
 
-    x, cot, attn_in, qkv, attended, lse, attn_out, vectors, fc1, attn_w, mlp_w = gather_and_attend(
+    x, cot, attn_in, qkv, attended, lse, hidden, mlp_in, vectors, fc1, attn_w, mlp_w = gather_and_attend(
         counts, tokens, cotangent, small, halves, cfg
     )
     fc1_sums, mlp_grads, residual, grad_hidden, sums, mixed = mlp_pass(
-        x, attn_out, vectors, cot, fc1, mlp_w, cfg
+        hidden, mlp_in, vectors, cot, fc1, mlp_w, cfg
     )
     both, mixed, d_tokens, small = reduce_and_attend_back(
         counts, grad_hidden, attn_in, qkv, attended, lse, attn_w, mlp_grads, residual, x, mixed, vectors, sums,

time: 610 us -> 485 us (0.80)
  Pallas kernels: 575 us -> 452 us
    pallas_call x1, Pallas kernels: 240 us -> 139 us  [gather_and_attend(): pl.pallas_call(kernel, in_specs=[smem, vmem, vmem, vmem, anywhere], out_s...]
    pallas_call x1, Pallas kernels: 247 us -> 202 us  [reduce_and_attend_back(): pl.pallas_call(kernel, grid=(n_t,), in_specs=[pl.BlockSpec(memory_space=p...]
    pallas_call x1, Pallas kernels: 88.3 us -> 111 us  [mlp_pass(): pl.pallas_call(kernel, grid=(n_t,), in_specs=[pl.BlockSpec(memory_space=p...]
where the time goes in v4:
time: 485 us; the launch traced here: 479 us
  Pallas kernels  452 us (93%)
  local copies, waits for them, and re-layouts  23.7 us (5%)
    pallas_call x1, Pallas kernels, reduce_and_attend_back(): pl.pallas_call(kernel, grid=(n_t,), in_specs=[pl.BlockSpec(memory_space=p...  202 us
    pallas_call x1, Pallas kernels, gather_and_attend(): pl.pallas_call(kernel, in_specs=[smem, vmem, vmem, vmem, anywhere], out_s...  139 us
    pallas_call x1, Pallas kernels, mlp_pass(): pl.pallas_call(kernel, grid=(n_t,), in_specs=[pl.BlockSpec(memory_space=p...  111 us

profile of v4, /device:TPU:0, one launch (start us, length us, event | category | flops | bytes accessed | tf_op | source)
XLA Modules:
  0.0 479.0 jit_solution(2190532494709590330)
XLA Ops:
  0.6 0.0 copy-start.2
  0.7 0.0 copy-start.3
  0.7 0.8 reshape.57
  1.5 1.3 select_maximum_fusion.small_ref
  2.8 1.0 reshape.60
  3.8 1.2 reshape.58
  5.0 0.9 copy.30
  5.9 0.2 copy.32
  6.1 0.1 maximum_bitcast_fusion
  6.2 0.0 copy-done.2
  6.2 0.0 copy-done.3
  6.2 0.1 bitcast_bitcast_fusion
  6.3 1.2 pad_maximum_fusion.half_ref
  7.5 139.2 %gather_and_attend.1 = (bf16[4,272,1280]{2,1,0:T(8,128)(2,1)}, bf16[4,272,1280]{2,1,0:T(8,128)(2,1)}, bf16[4,272,1280]{2,1,0:T(8,128)(2,1)}, bf16[4,4,272,480]{3...) custom-call(s32[1,4]{1,0:T(1,128)} %counts_ref.3, ...), custom_call_target="tpu_custom_call" | custom-call | flops 7130316800 | bytes 23265280 | tf_op jit(solution)/shard_map/gather_and_attend/pallas_call | solution.py:484
  146.8 1.3 reshape.63.fc1_ref
  148.1 110.8 %mlp_pass.1 = (f32[4,1,640]{2,1,0:T(1,128)}, bf16[4,4,2,320,640]{4,3,2,1,0:T(8,128)(2,1)}, f32[2,272,1280]{2,1,0:T(8,128)}, bf16[4,272,1280]{2,1,0:T(8,128)(2,1)...) custom-call(f32[2,272,1280]{2,1,0:T(8,128)} %get-tuple-element.31.hidden_ref, ...), custom_call_target="tpu_custom_call" | custom-call | flops 42781900800 | bytes 42926080 | tf_op jit(solution)/shard_map/mlp_pass/pallas_call | solution.py:1245
  258.8 201.6 %reduce_and_attend_back.1 = (f32[2,3,160,640]{3,2,1,0:T(8,128)}, bf16[648,1280]{1,0:T(8,128)(2,1)}, bf16[648,1280]{1,0:T(8,128)(2,1)}, f32[16,128]{1,0:T(8,128)}...) custom-call(s32[1,4]{1,0:T(1,128)} %counts_ref.3, ...), custom_call_target="tpu_custom_call" | custom-call | flops 16154624000 | bytes 40960000 | tf_op jit(solution)/shard_map/reduce_and_attend_back/pallas_call | solution.py:965
  460.4 0.0 copy-start
  460.4 1.4 slice.29
  461.8 0.7 slice.31
  462.5 1.3 slice.30
  463.7 0.6 reshape.69
  464.4 1.1 slice_bitcast_fusion.2
  465.5 0.3 copy.37
  465.8 1.0 reshape.66
  466.7 2.0 slice.25
  468.7 0.0 copy-done
  468.7 0.1 slice_bitcast_fusion
  468.8 0.9 copy.43
  469.8 1.4 copy.35
  471.2 0.9 copy.36
  472.1 1.7 reshape.65
  473.8 0.0 copy-start.1
  473.8 0.9 copy.42
  474.7 2.7 copy.50
  477.4 0.0 copy-done.1
  477.4 1.2 copy.51
  (1 shorter events, 0.0 us)
Async XLA Ops:
  0.6 5.6 %copy-start.2 = (bf16[1280,160]{0,1:T(8,128)(2,1)S(1)}, bf16[1280,160]{0,1:T(8,128)(2,1)}, u32[]{:S(2)}) copy-start(bf16[1280,160]{0,1:T(8,128)(2,1)} %param.18) | copy-start | bytes 1228804
  0.7 5.6 %copy-start.3 = (bf16[160,1280]{1,0:T(8,128)(2,1)S(1)}, bf16[160,1280]{1,0:T(8,128)(2,1)}, u32[]{:S(2)}) copy-start(bf16[160,1280]{1,0:T(8,128)(2,1)} %param.17) | copy-start | bytes 1228804
  460.4 8.3 %copy-start = (f32[2,3,160,640]{3,2,1,0:T(8,128)S(1)}, f32[2,3,160,640]{3,2,1,0:T(8,128)}, u32[]{:S(2)}) copy-start(f32[2,3,160,640]{3,2,1,0:T(8,128)} %get-tuple-element.51) | copy-start | bytes 7372804
  473.8 3.7 copy-start.1

commit v5 on v4

--- a/solution.py
+++ b/solution.py
@@ -342,17 +342,15 @@
         for group in range(2):
             trade(group).start()
         part_stage(0)
-        send_rows(0, tok_ref)
         have_own(0)
         send_p(0, 0)
         send_z(0, 1)
         have_own(1)
         send_p(1, 0)
+        send_rows(0, tok_ref)
         part_stage(1)
         send_d(0, 0)
         part_stage(2)
-        take_rows(0, tok_ref, x_ref)
-        pair_rows(0, x_ref).start()
         z_last = n_t - 1
         for k in range(1, n_t):
             if k < z_last:
@@ -368,6 +366,9 @@
                 spread()
             else:
                 send_d(0, k - 1)
+            if k == z_last - 1:
+                take_rows(0, tok_ref, x_ref)
+                pair_rows(0, x_ref).start()
         send_d(0, z_last)
         steps = []
         for k in range(1, cfg.early + 1):
@@ -540,7 +541,7 @@
 
 
 def reduce_and_attend_back(
-    counts, grad_hidden, attn_in, qkv, attended, lse, weights, mlp_grads, residual, x, mixed, vectors, sums, fc1_sums, cfg
+    counts, grad_hidden, attn_in, qkv, attended, lse, weights, mlp_grads, mlp_sums, residual, x, mixed, vectors, sums, fc1_sums, cfg
 ):
     n_t, n_p, ni, hc, hh, f2, pd, m, imgs = (
         cfg.n_t, cfg.n_p, cfg.ni, cfg.hc, cfg.hh, cfg.f2, cfg.pd, cfg.m, cfg.imgs,
@@ -549,8 +550,7 @@
     square = n_p == 4
     plane = (2, 2) if square else (n_p,)
     order = list(range(n_t))[::-1]
-    jobs = [((k, k), k) for k in order[:-1]]
-    jobs += [((k, k - 1), None) for k in order[::2]] + [((0, 0), 0)]
+    jobs = [((k, k), k) for k in order[:-1]] + [((k, k - 1), None) for k in order[::2]]
     n_jobs = len(jobs)
     n_got = 2 if square else n_p - 1
     n_dev = 2 * n_p * n_t
@@ -564,13 +564,13 @@
                 to_z[n, part] = len(to_z)
 
     def kernel(
-        counts_ref, gh_ref, in_ref, qkv_ref, att_ref, lse_ref, w_ref, g_ref, res_ref, x_ref, mix_ref, vec_ref,
+        counts_ref, gh_ref, in_ref, qkv_ref, att_ref, lse_ref, w_ref, g_ref, msum_ref, res_ref, x_ref, mix_ref, vec_ref,
         sums_ref, fsum_ref,
-        half_ref, mixed_ref, dtok_ref, small_ref, own_grads, rows_got, in_other, got_z,
+        half_ref, mixed_ref, dtok_ref, small_ref, own_grads, in_other, got_z,
         gqkv, stage, held, got, got_2, got_step, total, out, dq, dv,
-        images, sent, taken, block, res_in, other_in, parts, parts_p, parts_c, parts_t,
+        images, sent, rows_got, x_in, block, res_in, other_in, parts, parts_p, parts_c, parts_t,
         stage_sem, held_sem, s_send, s_recv, t_send, t_recv, z_send, z_recv, r_send, r_recv, c_send, c_recv,
-        v_send, v_recv, in_sem, out_sem,
+        v_send, v_recv, in_sem, out_sem, block_sem,
     ):
         p, core, z = (lax.axis_index(axis) for axis in ALL)
         py, px = p >> 1, p & 1
@@ -660,11 +660,10 @@
                     for q in range(n_p - 1):
                         whole = whole + got[n, part, q].astype(F32)
                 if k is not None and k < n_t - 1:
-                    before = n - 1 if k > 0 else n_t - 2
-                    z_copy(before, part).wait_recv()
-                    whole = whole + got_step[to_z[before, part]].astype(F32)
+                    z_copy(n - 1, part).wait_recv()
+                    whole = whole + got_step[to_z[n - 1, part]].astype(F32)
                 if chunks[part] == 0:
-                    total[0 if k is None else 1 + part] = whole
+                    total[0] = whole
                 else:
                     got[n, part, here if square else 0] = whole.astype(BF16)
                     z_copy(n, part).start()
@@ -678,8 +677,16 @@
             if n + 2 < n_jobs:
                 begin(n + 2)
 
+        def sums_copy():
+            return pltpu.make_async_copy(msum_ref, total.at[pl.ds(1, 2)], stage_sem.at[1])
+
         def finish():
-            last(n_jobs - 1)
+            for s, (shift, _) in enumerate(caps):
+
+                @pl.when(layout.has(z - shift))
+                def _(s=s):
+                    row_copy(1, s).wait_send()
+
             for n in range(n_jobs):
                 for copy in first_copies(n) + second_copies(n):
                     copy.wait_send()
@@ -701,6 +708,10 @@
             for spot in direct:
                 whole = whole + got[(*spot, 0)].astype(F32)
             total[0] = whole
+            sums_copy().wait()
+            for part in range(2):
+                z_copy(n_t - 2, part).wait_recv()
+                total[1 + part] += got_step[to_z[n_t - 2, part]].astype(F32)
 
             def rows(member):
                 return total.at[:, pl.ds(pl.multiple_of(member * pd, 16), pd), :]
@@ -711,6 +722,7 @@
             traded.start()
             kept.wait()
             traded.wait()
+            block_store(1).wait()
 
         def row_copy(which, s):
             shift, size = caps[s]
@@ -733,38 +745,34 @@
 
                 @pl.when(layout.has(z - shift))
                 def _(s=s, shift=shift, size=size):
+                    if which == 1:
+                        row_copy(0, s).wait_send()
                     want = layout.window_back(z, z - shift, size) + row_ids(size)
                     sent[s, :size] = of_images(want, want >= 0)
                     row_copy(which, s).start()
 
-        def take_rows(which, target):
-            row = row_ids(cfg.block)
+        def block_store(which):
+            return pltpu.make_async_copy(block, (mixed_ref, dtok_ref)[which], block_sem)
+
+        def take_rows(which):
+            if which == 1:
+                block_store(0).wait()
+            row = row_ids(-(-cfg.block // 16) * 16)
             position = layout.start(z) + row
             valid = position < layout.end(z)
-            block[...] = of_images(position - cfg.rows * z, valid)
+            block[...] = of_images(position - cfg.rows * z, valid)[: cfg.block]
             for s, (shift, size) in enumerate(caps):
                 source = z + shift
 
                 @pl.when(layout.has(source))
                 def _(s=s, size=size, source=source):
                     row_copy(which, s).wait_recv()
-                    load = pltpu.make_async_copy(
-                        rows_got.at[which, s, pl.ds(0, size)], taken.at[pl.ds(0, size)], in_sem.at[0]
-                    )
-                    load.start()
-                    load.wait()
                     local = position - cfg.rows * source
                     mine = valid & (local >= 0) & (local < cfg.rows)
                     spots = jnp.where(mine, local - layout.window_back(source, z, size), -1)
-                    block[...] += dot(one_hot(spots, size), taken[:size]).astype(BF16)
-
-                @pl.when(layout.has(z - shift))
-                def _(s=s):
-                    row_copy(which, s).wait_send()
-
-            store = pltpu.make_async_copy(block, target, in_sem.at[0])
-            store.start()
-            store.wait()
+                    block[...] += dot(one_hot(spots, size), rows_got[which, s, :size]).astype(BF16)[: cfg.block]
+
+            block_store(which).start()
 
         device = (2 * p + core) * n_t + z
 
@@ -833,26 +841,30 @@
         def first_norm_back():
             in_copy().wait()
             gain, shift = jnp.zeros((1, D), F32), jnp.zeros((1, D), F32)
+            half = PT // 2
             for i in range(imgs):
-                reads = [
-                    pltpu.make_async_copy(res_ref.at[i], res_in, in_sem.at[0]),
-                    pltpu.make_async_copy(in_other.at[i], other_in, in_sem.at[1]),
-                    pltpu.make_async_copy(x_ref.at[i], taken.at[pl.ds(0, PT)], in_sem.at[2]),
-                ]
-                for read in reads:
-                    read.start()
-                for read in reads:
-                    read.wait()
-                up = out[i] + other_in[...]
-                normed, inverse = norm(taken[:PT].astype(F32))
-                grad = res_in[...] + norm_back(up, normed, inverse, vec_ref[0:1, :])
-                images[i] = grad.astype(BF16)
-                gain = gain + jnp.sum(up * normed, axis=0, keepdims=True)
-                shift = shift + jnp.sum(up, axis=0, keepdims=True)
+                for begin_at in (0, half):
+                    some = pl.ds(begin_at, half)
+                    reads = [
+                        pltpu.make_async_copy(res_ref.at[i, some], res_in, in_sem.at[0]),
+                        pltpu.make_async_copy(in_other.at[i, some], other_in, in_sem.at[1]),
+                        pltpu.make_async_copy(x_ref.at[i, some], x_in, in_sem.at[2]),
+                    ]
+                    for read in reads:
+                        read.start()
+                    for read in reads:
+                        read.wait()
+                    up = out[i, begin_at : begin_at + half] + other_in[...]
+                    normed, inverse = norm(x_in[...].astype(F32))
+                    grad = res_in[...] + norm_back(up, normed, inverse, vec_ref[0:1, :])
+                    images[i, begin_at : begin_at + half] = grad.astype(BF16)
+                    gain = gain + jnp.sum(up * normed, axis=0, keepdims=True)
+                    shift = shift + jnp.sum(up, axis=0, keepdims=True)
             gather_parts(gain, shift)
 
         @pl.when(step == 0)
         def _():
+            sums_copy().start()
             fetch(0)
             fetch(1)
             read = pltpu.make_async_copy(mix_ref, images, in_sem.at[0])
@@ -928,13 +940,13 @@
                 stage[(*ahead, lanes)] = value.reshape(
                     (n_p // 2, 2 * pd, lanes.stop - lanes.start)
                 )
-        store = pltpu.make_async_copy(stage, own_grads.at[n_t - 1 - step], stage_sem)
+        store = pltpu.make_async_copy(stage, own_grads.at[n_t - 1 - step], stage_sem.at[0])
         store.start()
         store.wait()
 
         @pl.when(step == n_t - 2)
         def _():
-            take_rows(0, mixed_ref)
+            take_rows(0)
 
         @pl.when(step == n_t - 1)
         def _():
@@ -948,7 +960,8 @@
                 tick(n)
             part_hop(2)
             tick(n_jobs - 1)
-            take_rows(1, dtok_ref)
+            last(n_jobs - 1)
+            take_rows(1)
             part_hop(3)
             finish()
 
@@ -977,18 +990,18 @@
             anywhere,
             anywhere,
             anywhere,
+            anywhere,
             fixed((8, D)),
             fixed((4, D)),
             fixed((n_t, 1, f2)),
         ],
-        out_specs=[anywhere] * 3 + [fixed((16, 128))] + [anywhere] * 4,
+        out_specs=[anywhere] * 3 + [fixed((16, 128))] + [anywhere] * 3,
         out_shape=[
             shape((2, 3, pd, f2), F32),
             shape((cfg.block, D), BF16),
             shape((cfg.block, D), BF16),
             shape((16, 128), F32),
             shape((n_t, *plane, *chunk), BF16),
-            shape((2, len(caps), widest, D), BF16),
             shape((imgs, PT, D), F32),
             shape((len(to_z), *chunk), BF16),
         ],
@@ -1005,15 +1018,16 @@
             vmem((n_t, hc), F32),
             vmem((imgs, PT, D), BF16),
             vmem((len(caps), widest, D), BF16),
-            vmem((max(widest, PT), D), BF16),
+            vmem((2, len(caps), widest, D), BF16),
+            vmem((PT // 2, D), BF16),
             vmem((cfg.block, D), BF16),
-            vmem((PT, D), F32),
-            vmem((PT, D), F32),
+            vmem((PT // 2, D), F32),
+            vmem((PT // 2, D), F32),
             vmem((n_dev, 16, 128), F32),
             vmem((n_p - 1, 2 * n_t, 16, 128), F32),
             vmem((n_t, 16, 128), F32),
             vmem((n_t, 16, 128), F32),
-            dma,
+            dma((2,)),
             dma((2, 2)),
             dma((n_jobs, 2, 1 if square else n_p - 1)),
             dma((n_jobs, 2, 1 if square else n_p - 1)),
@@ -1028,6 +1042,7 @@
             dma((n_v,)),
             dma((n_v,)),
             dma((3,)),
+            dma,
             dma,
         ],
         compiler_params=params(collective_id=1, has_side_effects=True),
@@ -1045,7 +1060,8 @@
         attended,
         lse,
         weights,
-        mlp_grads.reshape((*plane, n_t, 2, *chunk)),
+        mlp_grads,
+        mlp_sums,
         residual,
         x,
         mixed,
@@ -1059,12 +1075,16 @@
 def mlp_pass(hidden, mlp_in, vectors, cot, fc1, weights, cfg):
     n_p, n_t, m, pd, w, ni, imgs = cfg.n_p, cfg.n_t, cfg.m, cfg.pd, cfg.f2, cfg.ni, cfg.imgs
     early = cfg.early
+    square = n_p == 4
+    plane = (2, 2) if square else (n_p,)
+    piece = (2 * pd, w)
 
     def kernel(
         hidden_ref, mlp_in, vec_ref, cot_ref, fc1_ref, g_ref,
-        sum_ref, grad_ref, res_ref, gh_ref, sums_ref, mixed_ref, late_ref,
-        other, other_y, act_all, gpre_all, back, y, gh, w_all,
+        sum_ref, grad_ref, plane_ref, res_ref, gh_ref, sums_ref, mixed_ref, late_ref,
+        other, other_y, act_all, gpre_all, back, y, gh, w_all, stage, held, got, got_2,
         c_send, c_recv, own_sem, load_sem, keep_sem, z_send, z_recv, p_send, p_recv,
+        stage_sem, s_send, s_recv, t_send, t_recv,
     ):
         step = pl.program_id(0)
         p, z = lax.axis_index("p"), lax.axis_index("t")
@@ -1133,6 +1153,57 @@
 
         def y_copy():
             return pair_copy(1, y.at[theirs], other_y)
+
+        py, px = p >> 1, p & 1
+
+        def first_copies():
+            if square:
+                return [
+                    remote(grad_ref.at[:, px ^ 1, 0, 0], got.at[0], (s_send, s_recv), (0, 0), {"p": p ^ 1}),
+                    remote(grad_ref.at[py ^ 1, :, 0, 1], got.at[1], (s_send, s_recv), (1, 0), {"p": p ^ 2}),
+                ]
+            return [
+                remote(grad_ref.at[p ^ q, 0, part], got.at[part, q - 1], (s_send, s_recv), (part, q - 1), {"p": p ^ q})
+                for part in range(2)
+                for q in range(1, n_p)
+            ]
+
+        def second_copies():
+            if not square:
+                return []
+            return [
+                remote(got.at[0, py ^ 1], got_2.at[0], (t_send, t_recv), 0, {"p": p ^ 2}),
+                remote(got.at[1, px ^ 1], got_2.at[1], (t_send, t_recv), 1, {"p": p ^ 1}),
+            ]
+
+        def middle():
+            for copy in first_copies():
+                copy.wait_recv()
+            if square:
+                for part, here in enumerate((py, px)):
+                    both = held[part, here ^ 1].astype(F32) + got[part, here ^ 1].astype(F32)
+                    got[part, here ^ 1] = both.astype(BF16)
+                for copy in second_copies():
+                    copy.start()
+
+        def last():
+            for copy in second_copies():
+                copy.wait_recv()
+            for part, here in enumerate((py, px)):
+                if square:
+                    whole = held[part, here].astype(F32) + got[part, here].astype(F32)
+                    whole = whole + got_2[part].astype(F32)
+                else:
+                    whole = held[part, 0].astype(F32)
+                    for q in range(n_p - 1):
+                        whole = whole + got[part, q].astype(F32)
+                plane_ref[part] = whole
+            for copy in first_copies() + second_copies():
+                copy.wait_send()
+
+        def stage_copy(k):
+            ahead = (slice(None),) * len(plane)
+            return pltpu.make_async_copy(stage, grad_ref.at[(*ahead, k)], stage_sem)
 
         @pl.when(step == 0)
         def _():
@@ -1160,14 +1231,70 @@
             gpre = dot(cot_ref[i], w2) * slope
             total = total + jnp.sum(gpre, axis=0, keepdims=True)
             gpre_all[rows_i, :] = gpre.astype(BF16)
-            if i == min(1, ni - 1):
-                for j in range(n_t - early):
-
-                    @pl.when(step == j)
-                    def _(j=j):
-                        send_d(j)
-
         sum_ref[0] = total
+
+        def add(target, left, right):
+            value = dot_nt(left, right).reshape(ni, PT, D)
+
+            @pl.when(step == 0)
+            def _():
+                target[...] = value
+
+            @pl.when(step > 0)
+            def _():
+                target[...] += value
+
+        add(back, gpre_all[...], w1)
+
+        for j in range(1, n_t - early):
+
+            @pl.when(step == early - 1 + j)
+            def _(j=j):
+                send_d(j)
+
+        @pl.when(step == n_t - 2)
+        def _():
+            for copy in first_copies():
+                copy.start()
+
+        @pl.when(step == n_t - 1)
+        def _():
+            back_copy().start()
+
+        add(y, act_all[...], w2)
+
+        @pl.when(step == n_t - 1)
+        def _():
+            y_copy().start()
+
+        @pl.when(step > 0)
+        def _():
+            stage_copy(0).wait()
+
+        ahead = (slice(None),) * len(plane)
+        grad_1 = dot_tn(mlp_in[...].reshape(m, D), gpre_all[...]).astype(BF16)
+        stage[(*ahead, 0)] = grad_1.reshape((*plane, *piece))
+        grad_2 = dot_tn(cot_ref[...].reshape(m, D), act_all[...]).astype(BF16)
+        stage[(*ahead, 1)] = grad_2.reshape((*plane, *piece))
+        stage_copy(step).start()
+
+        @pl.when(step == 0)
+        def _():
+            if square:
+                held[0] = stage[:, px, 0]
+                held[1] = stage[py, :, 1]
+            else:
+                held[0, 0] = stage[p, 0]
+                held[1, 0] = stage[p, 1]
+
+        @pl.when(step == n_t - 1)
+        def _():
+            middle()
+
+        @pl.when(step == early - 2)
+        def _():
+            send_d(0)
+
         for k in range(2, n_t):
 
             @pl.when(step == k - 1)
@@ -1175,34 +1302,6 @@
                 if k >= early:
                     complete(k - early)
                 load(k).start()
-
-        def add(target, left, right):
-            value = dot_nt(left, right).reshape(ni, PT, D)
-
-            @pl.when(step == 0)
-            def _():
-                target[...] = value
-
-            @pl.when(step > 0)
-            def _():
-                target[...] += value
-
-        add(back, gpre_all[...], w1)
-
-        @pl.when(step == n_t - 1)
-        def _():
-            back_copy().start()
-
-        add(y, act_all[...], w2)
-
-        @pl.when(step == n_t - 1)
-        def _():
-            y_copy().start()
-
-        grad_1 = dot_tn(mlp_in[...].reshape(m, D), gpre_all[...]).astype(BF16)
-        grad_ref[:, 0, 0] = grad_1.reshape(n_p, 2 * pd, w)
-        grad_2 = dot_tn(cot_ref[...].reshape(m, D), act_all[...]).astype(BF16)
-        grad_ref[:, 0, 1] = grad_2.reshape(n_p, 2 * pd, w)
 
         @pl.when(step == n_t - 1)
         def _():
@@ -1230,6 +1329,8 @@
             grad_copy.wait()
             store = pltpu.make_async_copy(gh, gh_ref, own_sem)
             store.start()
+            last()
+            stage_copy(0).wait()
             for j in range(n_t - early):
                 for copy in d_copies(j):
                     copy.wait_send()
@@ -1255,7 +1356,8 @@
         ],
         out_specs=[
             pl.BlockSpec((1, 1, w), lambda i: (i, 0, 0)),
-            pl.BlockSpec((n_p, 1, 2, 2 * pd, w), lambda i: (0, i, 0, 0, 0)),
+            pl.BlockSpec(memory_space=pl.ANY),
+            fixed((2, *piece)),
             own,
             pl.BlockSpec(memory_space=pl.ANY),
             fixed((4, D)),
@@ -1264,7 +1366,8 @@
         ],
         out_shape=[
             shape((n_t, 1, w), F32),
-            shape((n_p, n_t, 2, 2 * pd, w), BF16),
+            shape((*plane, n_t, 2, *piece), BF16),
+            shape((2, *piece), F32),
             shape((imgs, PT, D), F32),
             shape((ni, PT, D), BF16),
             shape((4, D), F32),
@@ -1280,6 +1383,10 @@
             vmem((ni, PT, D), F32),
             vmem((ni, PT, D), BF16),
             vmem((2, 2, D, w), BF16),
+            vmem((*plane, 2, *piece), BF16),
+            vmem((2, 2 if square else 1, *piece), BF16),
+            vmem((2, 2 if square else n_p - 1, *piece), BF16),
+            vmem((2, *(piece if square else (16, 128))), BF16),
             dma((3,)),
             dma((3,)),
             dma,
@@ -1289,6 +1396,11 @@
             dma((n_t - early,)),
             dma((n_t - early, n_p)),
             dma((n_t - early, n_p)),
+            dma,
+            dma((2, 1 if square else n_p - 1)),
+            dma((2, 1 if square else n_p - 1)),
+            dma((2,)),
+            dma((2,)),
         ],
         compiler_params=params(collective_id=2, has_side_effects=True),
         cost_estimate=pl.CostEstimate(
@@ -1322,12 +1434,12 @@
     x, cot, attn_in, qkv, attended, lse, hidden, mlp_in, vectors, fc1, attn_w, mlp_w = gather_and_attend(
         counts, tokens, cotangent, small, halves, cfg
     )
-    fc1_sums, mlp_grads, residual, grad_hidden, sums, mixed = mlp_pass(
+    fc1_sums, mlp_grads, mlp_sums, residual, grad_hidden, sums, mixed = mlp_pass(
         hidden, mlp_in, vectors, cot, fc1, mlp_w, cfg
     )
     both, mixed, d_tokens, small = reduce_and_attend_back(
-        counts, grad_hidden, attn_in, qkv, attended, lse, attn_w, mlp_grads, residual, x, mixed, vectors, sums,
-        fc1_sums, cfg,
+        counts, grad_hidden, attn_in, qkv, attended, lse, attn_w, mlp_grads, mlp_sums, residual, x, mixed,
+        vectors, sums, fc1_sums, cfg,
     )
     d_qkv = both[:, 0, :, : 3 * hc].reshape(2, pd, 3, hc).transpose(1, 2, 0, 3).reshape(pd, 3, 2 * hc)
     d_o = both[:, 0, :, 3 * hc :].transpose(0, 2, 1).reshape(2 * hc, pd)

time: 485 us -> 463 us (0.955)
  the two profiles are of different devices: /device:TPU:0 before, /device:TPU:27 now
where the time goes in v5:
time: 463 us; the launch traced here: 457 us
  Pallas kernels  430 us (93%)
  local copies, waits for them, and re-layouts  23.6 us (5%)
    pallas_call x1, Pallas kernels, reduce_and_attend_back(): pl.pallas_call(kernel, grid=(n_t,), in_specs=[pl.BlockSpec(memory_space=p...  201 us
    pallas_call x1, Pallas kernels, gather_and_attend(): pl.pallas_call(kernel, in_specs=[smem, vmem, vmem, vmem, anywhere], out_s...  135 us
    pallas_call x1, Pallas kernels, mlp_pass(): pl.pallas_call(kernel, grid=(n_t,), in_specs=[pl.BlockSpec(memory_space=p...  94.3 us

profile of v5, /device:TPU:27, one launch (start us, length us, event | category | flops | bytes accessed | tf_op | source)
XLA Modules:
  0.0 457.0 jit_solution(11301651683123698979)
XLA Ops:
  0.6 0.0 copy-start.2
  0.7 0.0 copy-start.3
  0.7 0.8 reshape.54
  1.5 1.3 select_maximum_fusion.small_ref
  2.8 1.0 reshape.57
  3.8 1.2 reshape.55
  5.0 0.9 copy.30
  5.9 0.2 copy.32
  6.1 0.1 maximum_bitcast_fusion
  6.2 0.0 copy-done.2
  6.2 0.0 copy-done.3
  6.2 0.1 bitcast_bitcast_fusion
  6.3 1.2 pad_maximum_fusion.half_ref
  7.5 134.6 %gather_and_attend.1 = (bf16[4,272,1280]{2,1,0:T(8,128)(2,1)}, bf16[4,272,1280]{2,1,0:T(8,128)(2,1)}, bf16[4,272,1280]{2,1,0:T(8,128)(2,1)}, bf16[4,4,272,480]{3...) custom-call(s32[1,4]{1,0:T(1,128)} %counts_ref.3, ...), custom_call_target="tpu_custom_call" | custom-call | flops 7130316800 | bytes 23265280 | tf_op jit(solution)/shard_map/gather_and_attend/pallas_call | solution.py:485
  142.1 1.3 reshape.60.fc1_ref
  143.4 94.3 %mlp_pass.1 = (f32[4,1,640]{2,1,0:T(1,128)}, bf16[2,2,4,2,320,640]{5,4,3,2,1,0:T(8,128)(2,1)}, f32[2,320,640]{2,1,0:T(8,128)}, f32[2,272,1280]{2,1,0:T(8,128)}, ...) custom-call(f32[2,272,1280]{2,1,0:T(8,128)} %get-tuple-element.32.hi, ...), custom_call_target="tpu_custom_call" | custom-call | flops 42781900800 | bytes 42926080 | tf_op jit(solution)/shard_map/mlp_pass/pallas_call | solution.py:1346
  237.7 200.7 %reduce_and_attend_back.1 = (f32[2,3,160,640]{3,2,1,0:T(8,128)}, bf16[648,1280]{1,0:T(8,128)(2,1)}, bf16[648,1280]{1,0:T(8,128)(2,1)}, f32[16,128]{1,0:T(8,128)}...) custom-call(s32[1,4]{1,0:T(1,128)} %counts_ref.3, ...), custom_call_target="tpu_custom_call" | custom-call | flops 16154624000 | bytes 40960000 | tf_op jit(solution)/shard_map/reduce_and_attend_back/pallas_call | solution.py:978
  438.4 0.0 copy-start
  438.4 1.4 slice.29
  439.8 0.7 slice.31
  440.5 1.3 slice.30
  441.8 0.6 reshape.65
  442.4 1.1 slice_bitcast_fusion.2
  443.5 0.3 copy.37
  443.8 1.0 reshape.62
  444.7 2.0 slice.25
  446.7 0.0 copy-done
  446.7 0.1 slice_bitcast_fusion
  446.8 0.9 copy.43
  447.8 1.4 copy.35
  449.2 0.9 copy.36
  450.1 1.7 reshape.61
  451.8 0.0 copy-start.1
  451.8 0.9 copy.42
  452.7 2.7 copy.50
  455.5 0.0 copy-done.1
  455.5 1.2 copy.51
  (1 shorter events, 0.0 us)
Async XLA Ops:
  0.6 5.6 %copy-start.2 = (bf16[1280,160]{0,1:T(8,128)(2,1)S(1)}, bf16[1280,160]{0,1:T(8,128)(2,1)}, u32[]{:S(2)}) copy-start(bf16[1280,160]{0,1:T(8,128)(2,1)} %param.18) | copy-start | bytes 1228804
  0.7 5.6 %copy-start.3 = (bf16[160,1280]{1,0:T(8,128)(2,1)S(1)}, bf16[160,1280]{1,0:T(8,128)(2,1)}, u32[]{:S(2)}) copy-start(bf16[160,1280]{1,0:T(8,128)(2,1)} %param.17) | copy-start | bytes 1228804
  438.4 8.3 %copy-start = (f32[2,3,160,640]{3,2,1,0:T(8,128)S(1)}, f32[2,3,160,640]{3,2,1,0:T(8,128)}, u32[]{:S(2)}) copy-start(f32[2,3,160,640]{3,2,1,0:T(8,128)} %get-tuple-element.53) | copy-start | bytes 7372804
  451.8 3.7 copy-start.1

commit v6 on v5

--- a/solution.py
+++ b/solution.py
@@ -566,7 +566,7 @@
     def kernel(
         counts_ref, gh_ref, in_ref, qkv_ref, att_ref, lse_ref, w_ref, g_ref, msum_ref, res_ref, x_ref, mix_ref, vec_ref,
         sums_ref, fsum_ref,
-        half_ref, mixed_ref, dtok_ref, small_ref, own_grads, in_other, got_z,
+        half_0, half_1, half_2, mixed_ref, dtok_ref, small_ref, own_grads, in_other, got_z,
         gqkv, stage, held, got, got_2, got_step, total, out, dq, dv,
         images, sent, rows_got, x_in, block, res_in, other_in, parts, parts_p, parts_c, parts_t,
         stage_sem, held_sem, s_send, s_recv, t_send, t_recv, z_send, z_recv, r_send, r_recv, c_send, c_recv,
@@ -713,15 +713,18 @@
                 z_copy(n_t - 2, part).wait_recv()
                 total[1 + part] += got_step[to_z[n_t - 2, part]].astype(F32)
 
-            def rows(member):
-                return total.at[:, pl.ds(pl.multiple_of(member * pd, 16), pd), :]
-
-            kept = pltpu.make_async_copy(rows(core), half_ref.at[core], out_sem)
-            traded = remote(rows(1 - core), half_ref.at[core], (c_send, c_recv), 1, pair)
-            kept.start()
-            traded.start()
-            kept.wait()
-            traded.wait()
+            def rows(unit, member):
+                return total.at[unit, pl.ds(pl.multiple_of(member * pd, 16), pd), :]
+
+            moves = []
+            for unit, half_ref in enumerate((half_0, half_1, half_2)):
+                moves.append(pltpu.make_async_copy(rows(unit, core), half_ref.at[core], out_sem.at[unit]))
+                target = half_ref.at[core]
+                moves.append(remote(rows(unit, 1 - core), target, (c_send, c_recv), 1 + unit, pair))
+            for move in moves:
+                move.start()
+            for move in moves:
+                move.wait()
             block_store(1).wait()
 
         def row_copy(which, s):
@@ -876,8 +879,9 @@
             send_rows(0)
 
         keyed = lax.broadcasted_iota(jnp.int32, (PT, PT), 1) < TOK_IMG
-        total_q, total_v = jnp.zeros((1, hc), F32), jnp.zeros((1, hc), F32)
-        for i in range(ni):
+
+        def image(i, carry):
+            total_q, total_v = carry
             grad_att = dot(gh_ref[i], w_ref[0, :, 3 * hc :]).astype(BF16)
             sums_q, sums_v = [], []
             for h in range(hh):
@@ -907,20 +911,23 @@
             part = dot_nt(gqkv[i], w_ref[0, :, : 3 * hc])
 
             @pl.when(step == 0)
-            def _(i=i, part=part):
+            def _():
                 out[i] = part
 
             @pl.when(step > 0)
-            def _(i=i, part=part):
+            def _():
                 out[i] += part
 
             for n in range(n_t - 2):
-                if i == min(2 * n + 1, ni - 1):
-
-                    @pl.when(step == n + 1)
-                    def _(n=n):
-                        tick(n)
-
+
+                @pl.when((step == n + 1) & (i == min(2 * n + 1, ni - 1)))
+                def _(n=n):
+                    tick(n)
+
+            return total_q, total_v
+
+        nothing = jnp.zeros((1, hc), F32)
+        total_q, total_v = lax.fori_loop(0, ni, image, (nothing, nothing))
         dq[pl.ds(n_t - 1 - step, 1), :] = total_q
         dv[pl.ds(n_t - 1 - step, 1), :] = total_v
 
@@ -995,9 +1002,11 @@
             fixed((4, D)),
             fixed((n_t, 1, f2)),
         ],
-        out_specs=[anywhere] * 3 + [fixed((16, 128))] + [anywhere] * 3,
+        out_specs=[anywhere] * 5 + [fixed((16, 128))] + [anywhere] * 3,
         out_shape=[
-            shape((2, 3, pd, f2), F32),
+            shape((2, pd, f2), F32),
+            shape((2, pd, f2), F32),
+            shape((2, pd, f2), F32),
             shape((cfg.block, D), BF16),
             shape((cfg.block, D), BF16),
             shape((16, 128), F32),
@@ -1037,12 +1046,12 @@
             dma((len(to_z),)),
             dma((2, len(caps))),
             dma((2, len(caps))),
-            dma((2,)),
-            dma((2,)),
+            dma((4,)),
+            dma((4,)),
             dma((n_v,)),
             dma((n_v,)),
             dma((3,)),
-            dma,
+            dma((3,)),
             dma,
         ],
         compiler_params=params(collective_id=1, has_side_effects=True),
@@ -1069,7 +1078,7 @@
         sums,
         fc1_sums,
     )
-    return outs[:4]
+    return outs[:6]
 
 
 def mlp_pass(hidden, mlp_in, vectors, cot, fc1, weights, cfg):
@@ -1437,14 +1446,14 @@
     fc1_sums, mlp_grads, mlp_sums, residual, grad_hidden, sums, mixed = mlp_pass(
         hidden, mlp_in, vectors, cot, fc1, mlp_w, cfg
     )
-    both, mixed, d_tokens, small = reduce_and_attend_back(
+    attn, first, second, mixed, d_tokens, small = reduce_and_attend_back(
         counts, grad_hidden, attn_in, qkv, attended, lse, attn_w, mlp_grads, mlp_sums, residual, x, mixed,
         vectors, sums, fc1_sums, cfg,
     )
-    d_qkv = both[:, 0, :, : 3 * hc].reshape(2, pd, 3, hc).transpose(1, 2, 0, 3).reshape(pd, 3, 2 * hc)
-    d_o = both[:, 0, :, 3 * hc :].transpose(0, 2, 1).reshape(2 * hc, pd)
-    d_1 = both[:, 1].transpose(1, 0, 2).reshape(pd, 2 * f2)
-    d_2 = both[:, 2].transpose(0, 2, 1).reshape(2 * f2, pd)
+    d_qkv = attn[:, :, : 3 * hc].reshape(2, pd, 3, hc).transpose(1, 2, 0, 3).reshape(pd, 3, 2 * hc)
+    d_o = attn[:, :, 3 * hc :].transpose(0, 2, 1).reshape(2 * hc, pd)
+    d_1 = first.transpose(1, 0, 2).reshape(pd, 2 * f2)
+    d_2 = second.transpose(0, 2, 1).reshape(2 * f2, pd)
     piece = D // (cfg.n_dp * cfg.n_t)
     small = small[:, :piece]
     return (

time: 463 us -> 455 us (0.983)
  no operation moved by 1% of the time
where the time goes in v6:
time: 455 us; the launch traced here: 449 us
  Pallas kernels  426 us (94%)
  local copies, waits for them, and re-layouts  19.9 us (4%)
    pallas_call x1, Pallas kernels, reduce_and_attend_back(): pl.pallas_call(kernel, grid=(n_t,), in_specs=[pl.BlockSpec(memory_space=p...  197 us
    pallas_call x1, Pallas kernels, gather_and_attend(): pl.pallas_call(kernel, in_specs=[smem, vmem, vmem, vmem, anywhere], out_s...  135 us
    pallas_call x1, Pallas kernels, mlp_pass(): pl.pallas_call(kernel, grid=(n_t,), in_specs=[pl.BlockSpec(memory_space=p...  94.2 us

profile of v6, /device:TPU:27, one launch (start us, length us, event | category | flops | bytes accessed | tf_op | source)
XLA Modules:
  0.0 449.2 jit_solution(3870467579037529040)
XLA Ops:
  0.6 0.0 copy-start.4
  0.7 0.0 copy-start.5
  0.7 0.8 reshape.57
  1.5 1.3 select_maximum_fusion.small_ref
  2.8 1.0 reshape.60
  3.8 1.2 reshape.58
  5.0 0.9 copy.30
  5.9 0.2 copy.32
  6.1 0.1 maximum_bitcast_fusion
  6.2 0.0 copy-done.4
  6.2 0.0 copy-done.5
  6.2 0.1 bitcast_bitcast_fusion
  6.3 1.2 pad_maximum_fusion.half_ref
  7.5 134.6 %gather_and_attend.1 = (bf16[4,272,1280]{2,1,0:T(8,128)(2,1)}, bf16[4,272,1280]{2,1,0:T(8,128)(2,1)}, bf16[4,272,1280]{2,1,0:T(8,128)(2,1)}, bf16[4,4,272,480]{3...) custom-call(s32[1,4]{1,0:T(1,128)} %counts_ref.3, ...), custom_call_target="tpu_custom_call" | custom-call | flops 7130316800 | bytes 23265280 | tf_op jit(solution)/shard_map/gather_and_attend/pallas_call | solution.py:485
  142.1 1.3 reshape.63.fc1_ref
  143.4 94.2 %mlp_pass.1 = (f32[4,1,640]{2,1,0:T(1,128)}, bf16[2,2,4,2,320,640]{5,4,3,2,1,0:T(8,128)(2,1)}, f32[2,320,640]{2,1,0:T(8,128)}, f32[2,272,1280]{2,1,0:T(8,128)}, ...) custom-call(f32[2,272,1280]{2,1,0:T(8,128)} %get-tuple-element.34.hi, ...), custom_call_target="tpu_custom_call" | custom-call | flops 42781900800 | bytes 42926080 | tf_op jit(solution)/shard_map/mlp_pass/pallas_call | solution.py:1355
  237.6 196.8 %reduce_and_attend_back.1 = (f32[2,160,640]{2,1,0:T(8,128)}, f32[2,160,640]{2,1,0:T(8,128)}, f32[2,160,640]{2,1,0:T(8,128)}, bf16[648,1280]{1,0:T(8,128)(2,1)}, ...) custom-call(s32[1,4]{1,0:T(1,128)} %counts_ref.3, ...), custom_call_target="tpu_custom_call" | custom-call | flops 16154624000 | bytes 40960000 | tf_op jit(solution)/shard_map/reduce_and_attend_back/pallas_call | solution.py:985
  434.4 1.2 slice.21
  435.6 0.7 slice.23
  436.3 1.3 slice.22
  437.6 0.6 reshape.69
  438.2 1.1 slice_bitcast_fusion
  439.4 1.1 slice.19
  440.5 0.3 copy.37
  440.8 1.0 reshape.66
  441.7 0.3 copy.35
  442.0 0.0 copy-start.2
  442.1 0.9 copy.36
  442.9 0.0 copy-start.3
  443.0 1.7 reshape.65
  444.7 0.0 copy-done.3
  444.7 0.0 copy-start.1
  444.7 0.9 copy.42
  445.6 0.0 copy-done.2
  445.6 0.0 copy-start
  445.6 0.9 copy.43
  446.6 0.0 copy-done.1
  446.6 1.2 copy.50
  447.8 0.0 copy-done
  447.8 1.2 copy.51
  (1 shorter events, 0.0 us)
Async XLA Ops:
  0.6 5.6 %copy-start.4 = (bf16[1280,160]{0,1:T(8,128)(2,1)S(1)}, bf16[1280,160]{0,1:T(8,128)(2,1)}, u32[]{:S(2)}) copy-start(bf16[1280,160]{0,1:T(8,128)(2,1)} %param.18) | copy-start | bytes 1228804
  0.7 5.6 %copy-start.5 = (bf16[160,1280]{1,0:T(8,128)(2,1)S(1)}, bf16[160,1280]{1,0:T(8,128)(2,1)}, u32[]{:S(2)}) copy-start(bf16[160,1280]{1,0:T(8,128)(2,1)} %param.17) | copy-start | bytes 1228804
  442.0 3.6 copy-start.2
  442.9 1.7 copy-start.3
  444.7 1.9 copy-start.1
  445.6 2.1 copy-start
